TPU v7x, 32 devices: a whole 2x2x4 slice. The times are simulated.
32 devices in a mesh: narrow: 4 (over x, core), wide: 8 (over z, y).
Axes of the slice: x: 2, y: 2, z: 4, core: 2. Of those that a mesh axis runs over, the one named last changes fastest.
Arguments:
- targets: bfloat16 [64, 288, 768], P(('narrow', 'wide')), may hold values from -6 to 6
- memory: bfloat16 [64, 1024, 768], P('narrow', 'wide'), may hold values from -6 to 6
- cotangent: bfloat16 [64, 288, 768], P(('narrow', 'wide')), may hold values from -6 to 6
- target_len: int32 [64], P(('narrow', 'wide')), may hold values from 1 to 288, 13824 in all
- memory_len: int32 [64], P(('narrow', 'wide')), may hold values from 1 to 1024, 49152 in all
- self_query: bfloat16 [768, 768], P(('narrow', 'wide')), may hold values from -0.109375 to 0.109375
- self_key: bfloat16 [768, 768], P(('narrow', 'wide')), may hold values from -0.109375 to 0.109375
- self_value: bfloat16 [768, 768], P(('narrow', 'wide')), may hold values from -0.21875 to 0.21875
- self_out: bfloat16 [768, 768], P(('narrow', 'wide')), may hold values from -0.625 to 0.625
- cross_query: bfloat16 [768, 768], P(('narrow', 'wide')), may hold values from -0.109375 to 0.109375
- cross_key: bfloat16 [768, 768], P(('narrow', 'wide')), may hold values from -0.109375 to 0.109375
- cross_value: bfloat16 [768, 768], P(('narrow', 'wide')), may hold values from -0.21875 to 0.21875
- cross_out: bfloat16 [768, 768], P(('narrow', 'wide')), may hold values from -0.875 to 0.875
- ff_gate: bfloat16 [768, 2048], P(('narrow', 'wide')), may hold values from -0.21875 to 0.21875
- ff_up: bfloat16 [768, 2048], P(('narrow', 'wide')), may hold values from -0.21875 to 0.21875
- ff_down: bfloat16 [2048, 768], P(('narrow', 'wide')), may hold values from -0.1875 to 0.1875
- self_gain: bfloat16 [768], P(('narrow', 'wide')), may hold values from 0.5 to 1.5
- cross_gain: bfloat16 [768], P(('narrow', 'wide')), may hold values from 0.5 to 1.5
- ff_gain: bfloat16 [768], P(('narrow', 'wide')), may hold values from 0.5 to 1.5
- position_bias: bfloat16 [32, 12], replicated, may hold values from -4 to 4
Outputs:
- layer_out: bfloat16 [64, 288, 768], P(('narrow', 'wide'))
- grad_targets: float32 [64, 288, 768], P(('narrow', 'wide'))
- grad_memory: float32 [64, 1024, 768], P('narrow', 'wide')
- grad_self_query: float32 [768, 768], P(('narrow', 'wide'))
- grad_self_key: float32 [768, 768], P(('narrow', 'wide'))
- grad_self_value: float32 [768, 768], P(('narrow', 'wide'))
- grad_self_out: float32 [768, 768], P(('narrow', 'wide'))
- grad_cross_query: float32 [768, 768], P(('narrow', 'wide'))
- grad_cross_key: float32 [768, 768], P(('narrow', 'wide'))
- grad_cross_value: float32 [768, 768], P(('narrow', 'wide'))
- grad_cross_out: float32 [768, 768], P(('narrow', 'wide'))
- grad_ff_gate: float32 [768, 2048], P(('narrow', 'wide'))
- grad_ff_up: float32 [768, 2048], P(('narrow', 'wide'))
- grad_ff_down: float32 [2048, 768], P(('narrow', 'wide'))
- grad_self_gain: float32 [768], P(('narrow', 'wide'))
- grad_cross_gain: float32 [768], P(('narrow', 'wide'))
- grad_ff_gain: float32 [768], P(('narrow', 'wide'))
- grad_position_bias: float32 [32, 12], replicated
Inputs may be any that keep to these rules, and one draw needn't show every extreme that they name: `target_len`: at least one pair has 288 live target slots. `memory_len`: at least one pair has 1024 live memory rows.
All inputs are finite; a program needn't handle non-finite values. No bound on the sum of `target_len` or of `memory_len` on one device may be relied on, other than what follows from the above.
Results may differ from a plain program's by a relative error of at most 0.025.
The roundings to bfloat16 on the way count: a program that leaves them out, or rounds other values in their place, can miss the bound.
Values may be sent and summed in bfloat16 or wider, within the bound.
No kernel may reach another device: no remote copies, remote signals or barrier semaphores. Data moves between devices by JAX's collectives and lax.ppermute only.
A program may use at most 256 MiB of HBM per device.

v0:
```python
import jax
import jax.numpy as jnp
import numpy as np
from jax import lax
from jax.sharding import PartitionSpec as P

HEADS = 12
HEAD_DIM = 64
BUCKETS = 32
REACH = 128
MEM = 1024


negative = -1e30
epsilon = 1e-06


def bucket_matrix(length, buckets, reach):
    rows = np.arange(length)[:, None]
    cols = np.arange(length)[None, :]
    apart = np.maximum(rows - cols, 0)
    exact = buckets // 2
    safe = np.maximum(apart, 1)
    far = exact + (np.log(safe / exact) / np.log(reach / exact) * (buckets - exact)).astype(
        np.int64
    )
    far = np.minimum(far, buckets - 1)
    return np.where(apart < exact, apart, far).astype(np.int32)


def project(left, weight):
    return jnp.einsum("pld,de->ple", left, weight, preferred_element_type=jnp.float32)


def project_back(grad, weight):
    return jnp.einsum("ple,de->pld", grad, weight, preferred_element_type=jnp.float32)


def weight_grad(left, grad):
    return jnp.einsum("pld,ple->de", left, grad, preferred_element_type=jnp.float32)


def rms_norm(value, gain):
    return value * lax.rsqrt(jnp.mean(value * value, axis=-1, keepdims=True) + epsilon) * gain


def gelu_tanh(value):
    return jax.nn.gelu(value, approximate=True)


def heads_of(value):
    return value.reshape(value.shape[0], value.shape[1], HEADS, HEAD_DIM)


def scores_of(query, keys, bias, mask):
    scores = (
        jnp.einsum(
            "pqhd,pkhd->phqk", heads_of(query), heads_of(keys), preferred_element_type=jnp.float32
        )
        + bias
    )
    return jnp.where(mask, scores, negative)


def attend_forward(query, keys, values, bias, mask):
    scores = scores_of(query, keys, bias, mask)
    top = jnp.max(scores, axis=-1, keepdims=True)
    total = jnp.log(jnp.sum(jnp.exp(scores - top), axis=-1, keepdims=True)) + top
    probs = jnp.exp(scores - total)
    mixed = jnp.einsum(
        "phqk,pkhd->pqhd",
        probs.astype(jnp.bfloat16),
        heads_of(values),
        preferred_element_type=jnp.float32,
    )
    return (mixed.reshape(query.shape).astype(jnp.bfloat16), total)


def attend_backward(query, keys, values, bias, mask, total, grad_mixed):
    probs = jnp.exp(scores_of(query, keys, bias, mask) - total)
    grad_heads = heads_of(grad_mixed)
    grad_probs = jnp.einsum(
        "pqhd,pkhd->phqk", grad_heads, heads_of(values), preferred_element_type=jnp.float32
    )
    inner = jnp.sum(probs * grad_probs, axis=-1, keepdims=True)
    grad_scores = (probs * (grad_probs - inner)).astype(jnp.bfloat16)
    grad_query = jnp.einsum(
        "phqk,pkhd->pqhd", grad_scores, heads_of(keys), preferred_element_type=jnp.float32
    )
    grad_keys = jnp.einsum(
        "phqk,pqhd->pkhd", grad_scores, heads_of(query), preferred_element_type=jnp.float32
    )
    grad_values = jnp.einsum(
        "phqk,pqhd->pkhd",
        probs.astype(jnp.bfloat16),
        grad_heads,
        preferred_element_type=jnp.float32,
    )
    return (
        grad_query.reshape(query.shape).astype(jnp.bfloat16),
        grad_keys.reshape(keys.shape).astype(jnp.bfloat16),
        grad_values.reshape(values.shape).astype(jnp.bfloat16),
        grad_scores,
    )


def on_device(
    targets,
    memory,
    cotangent,
    target_len,
    memory_len,
    self_query,
    self_key,
    self_value,
    self_out,
    cross_query,
    cross_key,
    cross_value,
    cross_out,
    ff_gate,
    ff_up,
    ff_down,
    self_gain,
    cross_gain,
    ff_gain,
    position_bias,
):
    s_query, s_key, s_value, s_out, gain_one = (
        lax.all_gather(self_query, ("narrow", "wide"), axis=0, tiled=True),
        lax.all_gather(self_key, ("narrow", "wide"), axis=0, tiled=True),
        lax.all_gather(self_value, ("narrow", "wide"), axis=0, tiled=True),
        lax.all_gather(self_out, ("narrow", "wide"), axis=0, tiled=True),
        lax.all_gather(self_gain, ("narrow", "wide"), axis=0, tiled=True),
    )
    c_query, c_key, c_value, c_out, gain_two = (
        lax.all_gather(cross_query, ("narrow", "wide"), axis=0, tiled=True),
        lax.all_gather(cross_key, ("narrow", "wide"), axis=0, tiled=True),
        lax.all_gather(cross_value, ("narrow", "wide"), axis=0, tiled=True),
        lax.all_gather(cross_out, ("narrow", "wide"), axis=0, tiled=True),
        lax.all_gather(cross_gain, ("narrow", "wide"), axis=0, tiled=True),
    )
    f_gate, f_up, f_down, gain_three = (
        lax.all_gather(ff_gate, ("narrow", "wide"), axis=0, tiled=True),
        lax.all_gather(ff_up, ("narrow", "wide"), axis=0, tiled=True),
        lax.all_gather(ff_down, ("narrow", "wide"), axis=0, tiled=True),
        lax.all_gather(ff_gain, ("narrow", "wide"), axis=0, tiled=True),
    )
    gain_one = gain_one.astype(jnp.float32)
    gain_two = gain_two.astype(jnp.float32)
    gain_three = gain_three.astype(jnp.float32)
    length = targets.shape[1]
    places = jnp.arange(length)
    causal = (places[:, None] >= places[None, :])[None, None]
    live = (places[None, :] < target_len[:, None]).astype(jnp.float32)[:, :, None]
    table = jnp.asarray(bucket_matrix(length, BUCKETS, REACH))
    bias = jnp.transpose(position_bias.astype(jnp.float32)[table], (2, 0, 1))[None]
    mem_mask = (jnp.arange(MEM)[None, :] < memory_len[:, None])[:, None, None, :]
    inputs = targets.astype(jnp.float32)
    normed_one = rms_norm(inputs, gain_one).astype(jnp.bfloat16)
    query_one = project(normed_one, s_query).astype(jnp.bfloat16)
    key_one = project(normed_one, s_key).astype(jnp.bfloat16)
    value_one = project(normed_one, s_value).astype(jnp.bfloat16)
    mixed_one, total_one = attend_forward(query_one, key_one, value_one, bias, causal)
    first = inputs + project(mixed_one, s_out)
    normed_two = rms_norm(first, gain_two).astype(jnp.bfloat16)
    query_two = project(normed_two, c_query).astype(jnp.bfloat16)
    memory_rows = lax.all_to_all(memory, "wide", split_axis=0, concat_axis=1, tiled=True)
    key_two = project(memory_rows, c_key).astype(jnp.bfloat16)
    value_two = project(memory_rows, c_value).astype(jnp.bfloat16)
    mixed_two, total_two = attend_forward(query_two, key_two, value_two, 0.0, mem_mask)
    second = first + project(mixed_two, c_out)
    third_normalized_rows = rms_norm(second, gain_three).astype(jnp.bfloat16)
    gate = project(third_normalized_rows, f_gate)
    upward = project(third_normalized_rows, f_up)
    activated, gelu_pull = jax.vjp(gelu_tanh, gate)
    hidden = (activated * upward).astype(jnp.bfloat16)
    third = second + project(hidden, f_down)
    layer_out = (third * live).astype(jnp.bfloat16)
    grad_third = cotangent.astype(jnp.float32) * live
    branch_ff = grad_third.astype(jnp.bfloat16)
    d_down = weight_grad(hidden, branch_ff)
    grad_hidden = project_back(branch_ff, f_down)
    grad_gate = gelu_pull(grad_hidden * upward)[0].astype(jnp.bfloat16)
    grad_up = (grad_hidden * activated).astype(jnp.bfloat16)
    d_gate = weight_grad(third_normalized_rows, grad_gate)
    d_up = weight_grad(third_normalized_rows, grad_up)
    grad_normed_three = project_back(grad_gate, f_gate) + project_back(grad_up, f_up)
    _, norm_three = jax.vjp(rms_norm, second, gain_three)
    back_three, d_gain_three = norm_three(grad_normed_three)
    grad_second = grad_third + back_three
    ff_shards = (
        lax.psum_scatter(d_gate, ("narrow", "wide"), scatter_dimension=0, tiled=True),
        lax.psum_scatter(d_up, ("narrow", "wide"), scatter_dimension=0, tiled=True),
        lax.psum_scatter(d_down, ("narrow", "wide"), scatter_dimension=0, tiled=True),
        lax.psum_scatter(d_gain_three, ("narrow", "wide"), scatter_dimension=0, tiled=True),
    )
    branch_cross = grad_second.astype(jnp.bfloat16)
    d_cross_out = weight_grad(mixed_two, branch_cross)
    grad_mixed_two = project_back(branch_cross, c_out).astype(jnp.bfloat16)
    grad_query_two, grad_key_two, grad_value_two, _ = attend_backward(
        query_two, key_two, value_two, 0.0, mem_mask, total_two, grad_mixed_two
    )
    d_cross_query = weight_grad(normed_two, grad_query_two)
    cross_key_gradient = weight_grad(memory_rows, grad_key_two)
    d_cross_value = weight_grad(memory_rows, grad_value_two)
    rows_grad = project_back(grad_key_two, c_key) + project_back(grad_value_two, c_value)
    grad_memory = lax.all_to_all(
        rows_grad.astype(jnp.bfloat16), "wide", split_axis=1, concat_axis=0, tiled=True
    ).astype(rows_grad.dtype)
    _, norm_two = jax.vjp(rms_norm, first, gain_two)
    back_two, d_gain_two = norm_two(project_back(grad_query_two, c_query))
    grad_first = grad_second + back_two
    cross_shards = (
        lax.psum_scatter(d_cross_query, ("narrow", "wide"), scatter_dimension=0, tiled=True),
        lax.psum_scatter(cross_key_gradient, ("narrow", "wide"), scatter_dimension=0, tiled=True),
        lax.psum_scatter(d_cross_value, ("narrow", "wide"), scatter_dimension=0, tiled=True),
        lax.psum_scatter(d_cross_out, ("narrow", "wide"), scatter_dimension=0, tiled=True),
        lax.psum_scatter(d_gain_two, ("narrow", "wide"), scatter_dimension=0, tiled=True),
    )
    branch_self = grad_first.astype(jnp.bfloat16)
    d_self_out = weight_grad(mixed_one, branch_self)
    grad_mixed_one = project_back(branch_self, s_out).astype(jnp.bfloat16)
    grad_query_one, grad_key_one, grad_value_one, grad_scores_one = attend_backward(
        query_one, key_one, value_one, bias, causal, total_one, grad_mixed_one
    )
    grad_bias = jnp.sum(grad_scores_one.astype(jnp.float32), axis=0)
    onehot = (table[:, :, None] == jnp.arange(BUCKETS)[None, None, :]).astype(jnp.float32)
    d_position = jnp.einsum("hij,ijb->bh", grad_bias, onehot, precision=lax.Precision.HIGHEST)
    d_self_query = weight_grad(normed_one, grad_query_one)
    d_self_key = weight_grad(normed_one, grad_key_one)
    d_self_value = weight_grad(normed_one, grad_value_one)
    grad_normed_one = (
        project_back(grad_query_one, s_query)
        + project_back(grad_key_one, s_key)
        + project_back(grad_value_one, s_value)
    )
    _, norm_one = jax.vjp(rms_norm, inputs, gain_one)
    back_one, d_gain_one = norm_one(grad_normed_one)
    grad_targets = grad_first + back_one
    grad_position = lax.psum(d_position, ("narrow", "wide"))
    self_attention_pieces = (
        lax.psum_scatter(d_self_query, ("narrow", "wide"), scatter_dimension=0, tiled=True),
        lax.psum_scatter(d_self_key, ("narrow", "wide"), scatter_dimension=0, tiled=True),
        lax.psum_scatter(d_self_value, ("narrow", "wide"), scatter_dimension=0, tiled=True),
        lax.psum_scatter(d_self_out, ("narrow", "wide"), scatter_dimension=0, tiled=True),
        lax.psum_scatter(d_gain_one, ("narrow", "wide"), scatter_dimension=0, tiled=True),
    )
    g_gate, g_up, g_down, g_gain_three = ff_shards
    g_cquery, g_ckey, g_cvalue, g_cout, g_gain_two = cross_shards
    (
        self_query_gradient,
        self_key_gradient,
        self_value_gradient,
        self_output_gradient,
        first_gain_gradient,
    ) = self_attention_pieces
    return (
        layer_out,
        grad_targets,
        grad_memory,
        self_query_gradient,
        self_key_gradient,
        self_value_gradient,
        self_output_gradient,
        g_cquery,
        g_ckey,
        g_cvalue,
        g_cout,
        g_gate,
        g_up,
        g_down,
        first_gain_gradient,
        g_gain_two,
        g_gain_three,
        grad_position,
    )


def solution(mesh):
    in_specs = (
        P(("narrow", "wide"), None, None),
        P("narrow", "wide", None),
        P(("narrow", "wide"), None, None),
        P(("narrow", "wide")),
        P(("narrow", "wide")),
        P(("narrow", "wide"), None),
        P(("narrow", "wide"), None),
        P(("narrow", "wide"), None),
        P(("narrow", "wide"), None),
        P(("narrow", "wide"), None),
        P(("narrow", "wide"), None),
        P(("narrow", "wide"), None),
        P(("narrow", "wide"), None),
        P(("narrow", "wide"), None),
        P(("narrow", "wide"), None),
        P(("narrow", "wide"), None),
        P(("narrow", "wide")),
        P(("narrow", "wide")),
        P(("narrow", "wide")),
        P(),
    )
    out_specs = (
        P(("narrow", "wide"), None, None),
        P(("narrow", "wide"), None, None),
        P("narrow", "wide", None),
        P(("narrow", "wide"), None),
        P(("narrow", "wide"), None),
        P(("narrow", "wide"), None),
        P(("narrow", "wide"), None),
        P(("narrow", "wide"), None),
        P(("narrow", "wide"), None),
        P(("narrow", "wide"), None),
        P(("narrow", "wide"), None),
        P(("narrow", "wide"), None),
        P(("narrow", "wide"), None),
        P(("narrow", "wide"), None),
        P(("narrow", "wide")),
        P(("narrow", "wide")),
        P(("narrow", "wide")),
        P(),
    )
    return jax.shard_map(
        on_device, mesh=mesh, in_specs=in_specs, out_specs=out_specs, check_vma=False
    )
```

profile of v0, /device:TPU:0, one launch (start us, length us, event | category | flops | bytes accessed | tf_op | source)
XLA Modules:
  0.0 1924.6 jit_solution(14316600707207476563)
XLA Ops:
  14.0 7.4 all-to-all-start
  24.0 90.8 %all-reduce.7 = (bf16[768]{0:T(1024)(128)(2,1)S(1)}, bf16[768]{0:T(1024)(128)(2,1)S(1)}, bf16[768]{0:T(1024)(128)(2,1)S(1)}) all-reduce(bf16[768]{0:T(1024)(128)(2,1)S(1)} %dynamic-update-slice, bf16[768]{0:T(1024)(128)(2,1)S(1)} %dynamic-update-slice.1, ...), channel_id=1, replica_groups=mesh['narrow'=4,'wide'=8] {'narrow','wide'}, use_global_device_ids=true, to_apply=%add | all-reduce | flops 2304 | bytes 9216
  115.5 273.2 %gather_fusion = f32[82944,12]{1,0:T(8,128)} fusion(f32[32,12]{1,0:T(8,128)S(1)} %copy.140, s32[82944]{0:T(1024)S(1)} %broadcast_clamp_fusion), kind=kCustom, calls=%fused_computation | custom fusion | bytes 8294400 | tf_op jit(solution)/shard_map/gather | solution.py:157
  388.7 29.8 %copy.141 = f32[288,288,12]{0,1,2:T(8,128)} copy(f32[288,288,12]{2,1,0:T(8,128)} %bitcast.204) | data formatting | bytes 7962624 | tf_op jit(solution)/shard_map/gather | solution.py:157
  434.6 9.4 fusion.2
  450.6 10.0 fusion.4
  482.1 11.5 select_reduce_fusion
  493.6 10.2 exponential_reduce_fusion
  510.4 12.9 fusion.37
  528.1 37.8 %all-gather.30.cloned.1.call-done = bf16[768,2048]{1,0:T(8,128)(2,1)} async-done(((bf16[24,2048]{1,0:T(8,128)(2,1)}), bf16[768,2048]{1,0:T(8,128)(2,1)}) %all-gather.30.cloned.1.call-update) | async-done | bytes 3145744 | tf_op jit(solution)/shard_map/all_gather | solution.py:145
  572.2 54.3 %all-gather.32.cloned.1.call-done = bf16[2048,768]{1,0:T(8,128)(2,1)} async-done(((bf16[64,768]{1,0:T(8,128)(2,1)}), bf16[2048,768]{1,0:T(8,128)(2,1)}) %all-gather.32.cloned.1.call-update) | async-done | bytes 3145744 | tf_op jit(solution)/shard_map/all_gather | solution.py:146
  632.9 54.5 %all-gather.28.cloned.1.call-done = bf16[768,2048]{1,0:T(8,128)(2,1)} async-done(((bf16[24,2048]{1,0:T(8,128)(2,1)}), bf16[768,2048]{1,0:T(8,128)(2,1)}) %all-gather.28.cloned.1.call-update) | async-done | bytes 3145744 | tf_op jit(solution)/shard_map/all_gather | solution.py:144
  687.4 10.8 fusion.11
  714.0 12.8 convolution_convert_fusion
  735.6 23.8 %multiply_reduce_fusion = (f32[2,12,288]{2,1,0:T(8,128)S(1)}, f32[2,12,288,1024]{3,2,1,0:T(8,128)}) fusion(f32[2,12,288,1024]{3,2,1,0:T(8,128)} %get-tuple-element.113, f32[2,12,288]{2,1,0:T(8,128)S(1)} %log_add_fusion, pred[2,1024]{1,0:T(4,128)(4,1)S(1)} %iota_compare_fusion.5, bf16[2,288,12,64]{1,3,2,0:T(8,128)(2,1)S(1)} %bitcast.219, ...), kind=kOutput, calls=%fused_computation.2 | convolution fusion | flops 934274304 | bytes 60710912 | tf_op jit(solution)/shard_map/pqhd,pkhd->phqk/dot_general | solution.py:82
  759.5 24.0 %multiply_convert_fusion = bf16[2,12,288,1024]{3,2,1,0:T(8,128)(2,1)} fusion(f32[2,12,288,1024]{3,2,1,0:T(8,128)} %get-tuple-element.118, f32[2,12,288,1024]{3,2,1,0:T(8,128)} %get-tuple-element.113, f32[2,12,288]{2,1,0:T(8,128)S(1)} %get-tuple-element.117, f32[2,12,288]{2,1,0:T(8,128)S(1)} %log_add_fusion, pred[2,1024]{1,0:T(4,128)(4,1)S(1)} %iota_compare_fusion.5), kind=kLoop, calls=%fused_computation.1 | loop fusion | flops 35389440 | bytes 70836224 | tf_op jit(solution)/shard_map/convert_element_type | solution.py:86
  783.6 8.4 convolution_convert_fusion.1
  800.9 10.7 convolution_convert_fusion.7
  837.0 7.6 multiply_reduce_fusion.1
  844.7 11.2 convert_reduce_fusion
  910.7 8.5 copy.166
  925.2 7.5 fusion.65
  935.7 67.0 %all-reduce.6 = (f32[768]{0:T(1024)S(1)}, f32[768]{0:T(1024)S(1)}, f32[768]{0:T(1024)S(1)}, f32[32,12]{0,1:T(8,128)}) all-reduce(f32[768]{0:T(1024)S(1)} %get-tuple-element.94, f32[768]{0:T(1024)S(1)} %get-tuple-element.92, f32[768]{0:T(1024)S(1)} %copy-done.55, ...), channel_id=13, replica_groups=mesh['narrow'=4,'wide'=8] {'narrow','wide'}, use_global_device_ids=true, to_apply=%region_24.25.clone | all-reduce | flops 2688 | bytes 21504
  1018.9 17.3 reduce-scatter.34.cloned.1.call-done
  1036.2 104.6 %reduce-scatter.24.cloned.1.call-done = f32[24,768]{1,0:T(8,128)} async-done(((f32[768,768]{1,0:T(8,128)}), f32[24,768]{1,0:T(8,128)}) %reduce-scatter.24.cloned.1.call-update) | async-done | bytes 73744 | tf_op jit(solution)/shard_map/reduce_scatter | solution.py:215
  1140.8 103.7 %reduce-scatter.22.cloned.1.call-done = f32[24,768]{1,0:T(8,128)} async-done(((f32[768,768]{1,0:T(8,128)}), f32[24,768]{1,0:T(8,128)}) %reduce-scatter.22.cloned.1.call-update) | async-done | bytes 73744 | tf_op jit(solution)/shard_map/reduce_scatter | solution.py:246
  1244.6 104.6 %reduce-scatter.20.cloned.1.call-done = f32[24,768]{1,0:T(8,128)} async-done(((f32[768,768]{1,0:T(8,128)}), f32[24,768]{1,0:T(8,128)}) %reduce-scatter.20.cloned.1.call-update) | async-done | bytes 73744 | tf_op jit(solution)/shard_map/reduce_scatter | solution.py:245
  1349.1 103.9 %reduce-scatter.16.cloned.1.call-done = f32[24,768]{1,0:T(8,128)} async-done(((f32[768,768]{1,0:T(8,128)}), f32[24,768]{1,0:T(8,128)}) %reduce-scatter.16.cloned.1.call-update) | async-done | bytes 73744 | tf_op jit(solution)/shard_map/reduce_scatter | solution.py:243
  1453.0 104.7 %reduce-scatter.18.cloned.1.call-done = f32[24,768]{1,0:T(8,128)} async-done(((f32[768,768]{1,0:T(8,128)}), f32[24,768]{1,0:T(8,128)}) %reduce-scatter.18.cloned.1.call-update) | async-done | bytes 73744 | tf_op jit(solution)/shard_map/reduce_scatter | solution.py:244
  1557.7 119.3 %reduce-scatter.32.cloned.1.call-done = f32[64,768]{1,0:T(8,128)} async-done(((f32[2048,768]{1,0:T(8,128)}), f32[64,768]{1,0:T(8,128)}) %reduce-scatter.32.cloned.1.call-update) | async-done | bytes 196624 | tf_op jit(solution)/shard_map/reduce_scatter | solution.py:195
  1677.1 120.7 %reduce-scatter.28.cloned.1.call-done = f32[24,2048]{1,0:T(8,128)} async-done(((f32[768,2048]{1,0:T(8,128)}), f32[24,2048]{1,0:T(8,128)}) %reduce-scatter.28.cloned.1.call-update) | async-done | bytes 196624 | tf_op jit(solution)/shard_map/reduce_scatter | solution.py:193
  1797.7 119.8 %reduce-scatter.30.cloned.1.call-done = f32[24,2048]{1,0:T(8,128)} async-done(((f32[768,2048]{1,0:T(8,128)}), f32[24,2048]{1,0:T(8,128)}) %reduce-scatter.30.cloned.1.call-update) | async-done | bytes 196624 | tf_op jit(solution)/shard_map/reduce_scatter | solution.py:194
  (279 shorter events, 216.2 us)
Async XLA Ops:
  7.2 411.4 %all-gather.14.cloned.1.call-start = ((), (), s32[]{:S(2)}) async-start(), calls=%async_computation.14 | async-start | bytes 1216512 | tf_op jit(solution)/shard_map/all_gather | solution.py:130
  7.9 415.5 %all-gather.16.cloned.1.call-start = ((), (), s32[]{:S(2)}) async-start(), calls=%async_computation.15 | async-start | bytes 1216512 | tf_op jit(solution)/shard_map/all_gather | solution.py:131
  8.7 420.6 %all-gather.12.cloned.1.call-start = ((), (), s32[]{:S(2)}) async-start(), calls=%async_computation.13 | async-start | bytes 1216512 | tf_op jit(solution)/shard_map/all_gather | solution.py:132
  9.4 456.0 %all-gather.18.cloned.1.call-start = ((), (), s32[]{:S(2)}) async-start(), calls=%async_computation.16 | async-start | bytes 1216512 | tf_op jit(solution)/shard_map/all_gather | solution.py:133
  10.0 459.2 %all-gather.22.cloned.1.call-start = ((), (), s32[]{:S(2)}) async-start(), calls=%async_computation.18 | async-start | bytes 1216512 | tf_op jit(solution)/shard_map/all_gather | solution.py:137
  10.6 466.6 %all-gather.24.cloned.1.call-start = ((), (), s32[]{:S(2)}) async-start(), calls=%async_computation.19 | async-start | bytes 1216512 | tf_op jit(solution)/shard_map/all_gather | solution.py:138
  11.2 492.7 %all-gather.20.cloned.1.call-start = ((), (), s32[]{:S(2)}) async-start(), calls=%async_computation.17 | async-start | bytes 1216512 | tf_op jit(solution)/shard_map/all_gather | solution.py:139
  11.9 511.5 %all-gather.26.cloned.1.call-start = ((), (), s32[]{:S(2)}) async-start(), calls=%async_computation.20 | async-start | bytes 1216512 | tf_op jit(solution)/shard_map/all_gather | solution.py:140
  12.6 553.2 %all-gather.30.cloned.1.call-start = ((), (), s32[]{:S(2)}) async-start(), calls=%async_computation.22 | async-start | bytes 3244032 | tf_op jit(solution)/shard_map/all_gather | solution.py:145
  13.4 613.2 %all-gather.32.cloned.1.call-start = ((), (), s32[]{:S(2)}) async-start(), calls=%async_computation.23 | async-start | bytes 3244032 | tf_op jit(solution)/shard_map/all_gather | solution.py:146
  14.0 101.4 %copy-start.54 = (bf16[32,12]{0,1:T(8,128)(2,1)S(1)}, bf16[32,12]{0,1:T(8,128)(2,1)}, u32[]{:S(2)}) copy-start(bf16[32,12]{0,1:T(8,128)(2,1)} %param.40) | copy-start | bytes 2308
  14.0 459.3 %all-to-all-start = ((bf16[16,128,768]{2,1,0:T(8,128)(2,1)}), bf16[16,128,768]{2,1,0:T(8,128)(2,1)}, u32[]{:S(2)}, u32[]{:S(2)}) async-start(bf16[16,128,768]{2,1,0:T(8,128)(2,1)} %param.22), calls=%async_computation | async-start | bytes 6291456 | tf_op jit(solution)/shard_map/all_to_all | solution.py:168
  21.5 665.9 %all-gather.28.cloned.1.call-start = ((), (), s32[]{:S(2)}) async-start(), calls=%async_computation.21 | async-start | bytes 3244032 | tf_op jit(solution)/shard_map/all_gather | solution.py:144
  22.2 996.7 %reduce-scatter.26.cloned.1.call-start = ((), (), s32[]{:S(2)}) async-start(), calls=%async_computation.29 | async-start | bytes 2433024 | tf_op jit(solution)/shard_map/reduce_scatter | solution.py:218
  23.2 395.3 %copy-start.49 = (f32[2,288]{1,0:T(2,128)}, f32[2,288]{1,0:T(2,128)S(1)}, u32[]{:S(2)}) copy-start(f32[2,288]{1,0:T(2,128)S(1)} %fusion.34) | copy-start | bytes 6916
  114.8 314.5 %copy-start.44 = (f32[768]{0:T(1024)}, f32[768]{0:T(1024)S(1)}, u32[]{:S(2)}) copy-start(f32[768]{0:T(1024)S(1)} %convert_element_type.185) | copy-start | bytes 9220
  388.7 29.8 %copy-start.57 = (s32[2]{0:T(128)S(1)}, s32[2]{0:T(128)}, u32[]{:S(2)}) copy-start(s32[2]{0:T(128)} %param.25) | copy-start | bytes 28
  418.5 32.1 %copy-start.15 = (pred[288,288]{0,1:T(8,128)(4,1)}, pred[288,288]{0,1:T(8,128)(4,1)S(1)}, u32[]{:S(2)}) copy-start(pred[288,288]{0,1:T(8,128)(4,1)S(1)} %iota_compare_fusion.4) | copy-start | bytes 248836
  526.6 178.0 %copy-start.2 = (f32[2,288,768]{2,1,0:T(8,128)}, f32[2,288,768]{2,1,0:T(8,128)S(1)}, u32[]{:S(2)}) copy-start(f32[2,288,768]{2,1,0:T(8,128)S(1)} %get-tuple-element.115) | copy-start | bytes 5308420
  528.1 98.5 %copy-start.51 = (f32[2,288]{1,0:T(2,128)S(1)}, f32[2,288]{1,0:T(2,128)}, u32[]{:S(2)}) copy-start(f32[2,288]{1,0:T(2,128)} %compare_convert_fusion) | copy-start | bytes 6916
  714.0 304.9 %reduce-scatter.36.cloned.1.call-start = ((), (), s32[]{:S(2)}) async-start(), calls=%async_computation.34 | async-start | bytes 2433024
  759.5 276.7 %reduce-scatter.34.cloned.1.call-start = ((), (), s32[]{:S(2)}) async-start(), calls=%async_computation.33 | async-start | bytes 2433024
  800.8 340.0 %reduce-scatter.24.cloned.1.call-start = ((), (), s32[]{:S(2)}) async-start(), calls=%async_computation.28 | async-start | bytes 2433024 | tf_op jit(solution)/shard_map/reduce_scatter | solution.py:215
  816.3 428.3 %reduce-scatter.22.cloned.1.call-start = ((), (), s32[]{:S(2)}) async-start(), calls=%async_computation.27 | async-start | bytes 2433024 | tf_op jit(solution)/shard_map/reduce_scatter | solution.py:246
  824.4 524.8 %reduce-scatter.20.cloned.1.call-start = ((), (), s32[]{:S(2)}) async-start(), calls=%async_computation.26 | async-start | bytes 2433024 | tf_op jit(solution)/shard_map/reduce_scatter | solution.py:245
  835.8 617.2 %reduce-scatter.16.cloned.1.call-start = ((), (), s32[]{:S(2)}) async-start(), calls=%async_computation.24 | async-start | bytes 2433024 | tf_op jit(solution)/shard_map/reduce_scatter | solution.py:243
  862.1 695.6 %reduce-scatter.18.cloned.1.call-start = ((), (), s32[]{:S(2)}) async-start(), calls=%async_computation.25 | async-start | bytes 2433024 | tf_op jit(solution)/shard_map/reduce_scatter | solution.py:244
  870.6 806.5 %reduce-scatter.32.cloned.1.call-start = ((), (), s32[]{:S(2)}) async-start(), calls=%async_computation.32 | async-start | bytes 6488064 | tf_op jit(solution)/shard_map/reduce_scatter | solution.py:195
  878.9 918.9 %reduce-scatter.28.cloned.1.call-start = ((), (), s32[]{:S(2)}) async-start(), calls=%async_computation.30 | async-start | bytes 6488064 | tf_op jit(solution)/shard_map/reduce_scatter | solution.py:193
  885.3 1032.2 %reduce-scatter.30.cloned.1.call-start = ((), (), s32[]{:S(2)}) async-start(), calls=%async_computation.31 | async-start | bytes 6488064 | tf_op jit(solution)/shard_map/reduce_scatter | solution.py:194
  905.6 107.6 %all-to-all-start.1 = ((bf16[2,1024,768]{2,0,1:T(2,128)(2,1)}), bf16[2,1024,768]{2,0,1:T(2,128)(2,1)S(1)}, u32[]{:S(2)}, u32[]{:S(2)}) async-start(bf16[2,1024,768]{2,0,1:T(2,128)(2,1)} %copy.158), calls=%async_computation.1 | async-start | bytes 6291456 | tf_op jit(solution)/shard_map/all_to_all | solution.py:208
  932.7 71.7 %copy-start.50 = (f32[2,288]{1,0:T(2,128)S(1)}, f32[2,288]{1,0:T(2,128)}, u32[]{:S(2)}) copy-start(f32[2,288]{1,0:T(2,128)} %copy-done.49) | copy-start | bytes 6916
  (63 other events, 328.9 us)
Sparse Core Ops, SparseCore 0:
  10.9 102.2 all-gather.13
  116.1 53.1 all-gather.15
  172.2 53.0 all-gather.11
  228.0 53.1 all-gather.17
  283.9 52.9 all-gather.21
  339.7 53.1 all-gather.23
  395.8 52.9 all-gather.19
  451.7 53.1 all-gather.25
  507.8 57.9 all-gather.29
  568.6 57.9 all-gather.31
  629.5 57.9 all-gather.27
  714.1 97.8 reduce-scatter.25
  818.7 98.1 reduce-scatter.35
  922.6 113.5 reduce-scatter.33
  1042.7 98.0 reduce-scatter.23
  1146.5 97.9 reduce-scatter.21
  1251.1 97.9 reduce-scatter.19
  1354.8 98.1 reduce-scatter.15
  1459.7 97.9 reduce-scatter.17
  1563.8 113.2 reduce-scatter.31
  1684.2 113.4 reduce-scatter.27
  1803.9 113.5 reduce-scatter.29
where the time goes:
time: 1930 us; the launch traced here: 1920 us
  waiting for transfers between devices  1050 us (54%)
  local copies, waits for them, and re-layouts  364 us (19%)
  matrix products  248 us (13%)
  blocking collectives  158 us (8%)
  other arithmetic  72.4 us (4%)
    gather x2, local copies, waits for them, and re-layouts, on_device(): position_bias.astype(jnp.float32)[table]  303 us
    unnamed x2, blocking collectives  158 us
    reduce_scatter x1, waiting for transfers between devices, on_device(): lax.psum_scatter(d_gate, ('narrow', 'wide'), scatter_dimension=0, tiled=T...  121 us
    reduce_scatter x1, waiting for transfers between devices, on_device(): lax.psum_scatter(d_up, ('narrow', 'wide'), scatter_dimension=0, tiled=True)  120 us
    reduce_scatter x1, waiting for transfers between devices, on_device(): lax.psum_scatter(d_down, ('narrow', 'wide'), scatter_dimension=0, tiled=T...  119 us
    reduce_scatter x1, waiting for transfers between devices, on_device(): lax.psum_scatter(d_self_key, ('narrow', 'wide'), scatter_dimension=0, til...  105 us
    reduce_scatter x1, waiting for transfers between devices, on_device(): lax.psum_scatter(d_cross_query, ('narrow', 'wide'), scatter_dimension=0,...  105 us
    reduce_scatter x1, waiting for transfers between devices, on_device(): lax.psum_scatter(d_self_value, ('narrow', 'wide'), scatter_dimension=0, t...  105 us
  transfers between devices with their start and end apart: 24, of which 12 were waited for; matrix products, arithmetic and copies ran while one was open for 33% of the time, Pallas kernels for 0%

commit v1 on v0

v1 whole, which is shorter than its diff:
```python
import jax
import jax.numpy as jnp
import numpy as np
from jax import lax
from jax.experimental import pallas as pl
from jax.experimental.pallas import tpu as pltpu
from jax.sharding import PartitionSpec as P

HEADS = 12
HEAD_DIM = 64
BUCKETS = 32
REACH = 128
LANES = 128
BOTH = ("narrow", "wide")

negative = -1e30
epsilon = 1e-06
bf16 = jnp.bfloat16
f32 = jnp.float32

NT = (((1,), (1,)), ((), ()))
NN = (((1,), (0,)), ((), ()))
TN = (((0,), (0,)), ((), ()))


def dot(left, right, dims):
    return lax.dot_general(left, right, dims, preferred_element_type=f32)


def bucket_of_distance(length, buckets, reach):
    apart = np.arange(length)
    exact = buckets // 2
    safe = np.maximum(apart, 1)
    far = exact + (np.log(safe / exact) / np.log(reach / exact) * (buckets - exact)).astype(
        np.int64
    )
    far = np.minimum(far, buckets - 1)
    return np.where(apart < exact, apart, far).astype(np.int32)


def of_head(h, first, value):
    return jnp.where(first if h == 0 else ~first, value, jnp.zeros_like(value))


def self_forward_kernel(q_ref, k_ref, v_ref, bias_ref, mixed_ref, total_ref):
    q, k, v = q_ref[0], k_ref[0], v_ref[0]
    first = lax.broadcasted_iota(jnp.int32, q.shape, 1) < HEAD_DIM
    mixed, totals = [], []
    for h in range(2):
        scores = dot(of_head(h, first, q), k, NT) + bias_ref[h].astype(f32)
        top = jnp.max(scores, axis=1, keepdims=True)
        grown = jnp.exp(scores - top)
        total = jnp.sum(grown, axis=1, keepdims=True)
        mixed.append(dot((grown * (1.0 / total)).astype(bf16), v, NN))
        totals.append(top + jnp.log(total))
    mixed_ref[0] = jnp.where(first, mixed[0], mixed[1]).astype(bf16)
    total_ref[0] = jnp.where(first, totals[0], totals[1])


def self_forward(qkv, bias):
    pairs, length, width = qkv.shape
    width //= 3
    steps = width // LANES
    part = lambda c: pl.BlockSpec((1, length, LANES), lambda p, h: (p, 0, h + c * steps))
    return pl.pallas_call(
        self_forward_kernel,
        out_shape=(
            jax.ShapeDtypeStruct((pairs, length, width), bf16),
            jax.ShapeDtypeStruct((pairs, length, width), f32),
        ),
        grid=(pairs, steps),
        in_specs=[
            part(0),
            part(1),
            part(2),
            pl.BlockSpec((2, length, length), lambda p, h: (h, 0, 0)),
        ],
        out_specs=[part(0), part(0)],
        cost_estimate=pl.CostEstimate(
            flops=pairs * HEADS * length * length * HEAD_DIM * 4,
            transcendentals=pairs * HEADS * length * length,
            bytes_accessed=pairs * length * width * 12,
        ),
        name="self_forward",
    )(qkv, qkv, qkv, bias)


def self_backward_kernel(
    q_ref, k_ref, v_ref, bias_ref, total_ref, grad_ref, grads_ref, diagonal_ref, sum_ref
):
    p, hp = pl.program_id(0), pl.program_id(1)
    steps = pl.num_programs(1)
    q, k, v, grad, total = q_ref[0], k_ref[0], v_ref[0], grad_ref[0], total_ref[0]
    length, padded = q.shape[0], sum_ref.shape[-1]
    first = lax.broadcasted_iota(jnp.int32, q.shape, 1) < HEAD_DIM

    @pl.when(p == 0)
    def _():
        sum_ref[hp] = jnp.zeros(sum_ref.shape[1:], f32)

    found = []
    for h in range(2):
        scores = dot(of_head(h, first, q), k, NT) + bias_ref[h].astype(f32)
        probs = jnp.exp(scores - total[:, HEAD_DIM * h : HEAD_DIM * h + 1])
        grad_probs = dot(of_head(h, first, grad), v, NT)
        inner = jnp.sum(probs * grad_probs, axis=1, keepdims=True)
        grad_scores = (probs * (grad_probs - inner)).astype(bf16)
        sum_ref[hp, h, :, :length] += grad_scores.astype(f32)
        found.append(
            (
                dot(grad_scores, k, NN),
                dot(grad_scores, q, TN),
                dot(probs.astype(bf16), grad, TN),
            )
        )
    for c in range(3):
        grads_ref[0, :, pl.ds(pl.multiple_of((hp + c * steps) * LANES, LANES), LANES)] = (
            jnp.where(first, found[0][c], found[1][c]).astype(bf16)
        )

    @pl.when(p == pl.num_programs(0) - 1)
    def _():
        rows = lax.broadcasted_iota(jnp.int32, (8, padded), 0)
        for h in range(2):
            held = sum_ref[hp, h, 0:8, :]
            for i in range(8, length, 8):
                held = held + pltpu.roll(sum_ref[hp, h, i : i + 8, :], padded - i, 1)
            for bit in (1, 2, 4):
                held = jnp.where(
                    (rows // bit) % 2 == 1, pltpu.roll(held, padded - bit, 1), held
                )
            diagonal_ref[0, h] = held


def self_backward(qkv, bias, total, grad):
    pairs, length, width = qkv.shape
    width //= 3
    steps = width // LANES
    padded = -(-length // LANES) * LANES
    part = lambda c: pl.BlockSpec((1, length, LANES), lambda p, h: (p, 0, h + c * steps))
    return pl.pallas_call(
        self_backward_kernel,
        out_shape=(
            jax.ShapeDtypeStruct(qkv.shape, bf16),
            jax.ShapeDtypeStruct((steps, 2, 8, padded), f32),
        ),
        grid=(pairs, steps),
        in_specs=[
            part(0),
            part(1),
            part(2),
            pl.BlockSpec((2, length, length), lambda p, h: (h, 0, 0)),
            part(0),
            part(0),
        ],
        out_specs=[
            pl.BlockSpec((1, length, 3 * width), lambda p, h: (p, 0, 0)),
            pl.BlockSpec((1, 2, 8, padded), lambda p, h: (h, 0, 0, 0)),
        ],
        scratch_shapes=[pltpu.VMEM((steps, 2, length, padded), f32)],
        cost_estimate=pl.CostEstimate(
            flops=pairs * HEADS * length * length * HEAD_DIM * 10,
            transcendentals=pairs * HEADS * length * length,
            bytes_accessed=pairs * length * width * 18,
        ),
        name="self_backward",
    )(qkv, qkv, qkv, bias, total, grad)


def dead_rows(len_ref, rows):
    places = lax.broadcasted_iota(jnp.int32, (1, rows), 1)
    return jnp.where(places < len_ref[pl.program_id(0)], 0.0, negative)


def cross_forward_kernel(len_ref, q_ref, k_ref, v_ref, mixed_ref, total_ref):
    q, k, v = q_ref[0], k_ref[0], v_ref[0]
    first = lax.broadcasted_iota(jnp.int32, q.shape, 1) < HEAD_DIM
    dead = dead_rows(len_ref, k.shape[0])
    mixed, totals = [], []
    for h in range(2):
        scores = dot(of_head(h, first, q), k, NT) + dead
        top = jnp.max(scores, axis=1, keepdims=True)
        grown = jnp.exp(scores - top)
        total = jnp.sum(grown, axis=1, keepdims=True)
        mixed.append(dot((grown * (1.0 / total)).astype(bf16), v, NN))
        totals.append(top + jnp.log(total))
    mixed_ref[0] = jnp.where(first, mixed[0], mixed[1]).astype(bf16)
    total_ref[0] = jnp.where(first, totals[0], totals[1])


def cross_forward(query, kv, lens):
    pairs, length, width = query.shape
    rows = kv.shape[1]
    steps = width // LANES
    target = pl.BlockSpec((1, length, LANES), lambda p, h, n: (p, 0, h))
    source = lambda c: pl.BlockSpec((1, rows, LANES), lambda p, h, n: (p, 0, h + c * steps))
    return pl.pallas_call(
        cross_forward_kernel,
        out_shape=(
            jax.ShapeDtypeStruct(query.shape, bf16),
            jax.ShapeDtypeStruct(query.shape, f32),
        ),
        grid_spec=pltpu.PrefetchScalarGridSpec(
            num_scalar_prefetch=1,
            grid=(pairs, steps),
            in_specs=[target, source(0), source(1)],
            out_specs=[target, target],
        ),
        cost_estimate=pl.CostEstimate(
            flops=pairs * HEADS * length * rows * HEAD_DIM * 4,
            transcendentals=pairs * HEADS * length * rows,
            bytes_accessed=pairs * (length * width * 8 + rows * width * 4),
        ),
        name="cross_forward",
    )(lens, query, kv, kv)


def cross_backward_kernel(
    len_ref, q_ref, k_ref, v_ref, total_ref, grad_ref, grad_query_ref, grad_kv_ref
):
    hp, steps = pl.program_id(1), pl.num_programs(1)
    q, k, v, grad, total = q_ref[0], k_ref[0], v_ref[0], grad_ref[0], total_ref[0]
    first = lax.broadcasted_iota(jnp.int32, q.shape, 1) < HEAD_DIM
    first_row = lax.broadcasted_iota(jnp.int32, k.shape, 1) < HEAD_DIM
    dead = dead_rows(len_ref, k.shape[0])
    found = []
    for h in range(2):
        scores = dot(of_head(h, first, q), k, NT) + dead
        probs = jnp.exp(scores - total[:, HEAD_DIM * h : HEAD_DIM * h + 1])
        grad_probs = dot(of_head(h, first, grad), v, NT)
        inner = jnp.sum(probs * grad_probs, axis=1, keepdims=True)
        grad_scores = (probs * (grad_probs - inner)).astype(bf16)
        found.append(
            (
                dot(grad_scores, k, NN),
                dot(grad_scores, q, TN),
                dot(probs.astype(bf16), grad, TN),
            )
        )
    grad_query_ref[0] = jnp.where(first, found[0][0], found[1][0]).astype(bf16)
    for c in range(2):
        grad_kv_ref[0, :, pl.ds(pl.multiple_of((hp + c * steps) * LANES, LANES), LANES)] = (
            jnp.where(first_row, found[0][c + 1], found[1][c + 1]).astype(bf16)
        )


def cross_backward(query, kv, lens, total, grad):
    pairs, length, width = query.shape
    rows = kv.shape[1]
    steps = width // LANES
    target = pl.BlockSpec((1, length, LANES), lambda p, h, n: (p, 0, h))
    source = lambda c: pl.BlockSpec((1, rows, LANES), lambda p, h, n: (p, 0, h + c * steps))
    return pl.pallas_call(
        cross_backward_kernel,
        out_shape=(
            jax.ShapeDtypeStruct(query.shape, bf16),
            jax.ShapeDtypeStruct(kv.shape, bf16),
        ),
        grid_spec=pltpu.PrefetchScalarGridSpec(
            num_scalar_prefetch=1,
            grid=(pairs, steps),
            in_specs=[target, source(0), source(1), target, target],
            out_specs=[target, pl.BlockSpec((1, rows, 2 * width), lambda p, h, n: (p, 0, 0))],
        ),
        cost_estimate=pl.CostEstimate(
            flops=pairs * HEADS * length * rows * HEAD_DIM * 10,
            transcendentals=pairs * HEADS * length * rows,
            bytes_accessed=pairs * (length * width * 10 + rows * width * 8),
        ),
        name="cross_backward",
    )(lens, query, kv, kv, total, grad)


class Cube:
    def __init__(self, narrow, wide):
        self.size = narrow * wide
        self.bits = self.size.bit_length() - 1
        self.core = wide.bit_length() - 1
        self.index = lax.axis_index(BOTH)

    def swap(self, value, bit):
        pairs = [(i, i ^ (1 << bit)) for i in range(self.size)]
        return lax.ppermute(value, BOTH, pairs)

    def side(self, bit):
        return (self.index >> bit) & 1

    def total(self, value):
        for bit in range(self.bits):
            value = value + self.swap(value, bit)
        return value

    def scatter(self, value, order):
        rows, width = value.shape
        value = value.reshape((2,) * self.bits + (rows // self.size, width))
        left = list(range(self.bits))[::-1]
        for bit in order:
            axis, side = left.index(bit), self.side(bit)
            send = lax.dynamic_index_in_dim(value, 1 - side, axis, keepdims=False)
            keep = lax.dynamic_index_in_dim(value, side, axis, keepdims=False)
            left.remove(bit)
            value = keep.astype(f32) + self.swap(send, bit).astype(f32)
            if left:
                value = value.astype(bf16)
        return value

    def orders(self):
        rest = [b for b in range(self.bits) if b != self.core]
        one = [self.core, rest[-1], rest[0]] + rest[1:-1][::-1]
        two = [self.core, rest[0], rest[-1]] + rest[1:-1][::-1]
        return one, two

    def scatter_both(self, value):
        half = value.shape[1] // 2 // LANES * LANES
        one, two = self.orders()
        return jnp.concatenate(
            [self.scatter(value[:, :half], one), self.scatter(value[:, half:], two)], axis=1
        )


def rms_norm(value, gain):
    return value * lax.rsqrt(jnp.mean(value * value, axis=-1, keepdims=True) + epsilon) * gain


def gelu_tanh(value):
    return jax.nn.gelu(value, approximate=True)


def on_device(
    targets,
    memory,
    cotangent,
    target_len,
    memory_len,
    self_query,
    self_key,
    self_value,
    self_out,
    cross_query,
    cross_key,
    cross_value,
    cross_out,
    ff_gate,
    ff_up,
    ff_down,
    self_gain,
    cross_gain,
    ff_gain,
    position_bias,
    narrow,
    wide,
):
    cube = Cube(narrow, wide)
    pairs, length, width = targets.shape
    slots = pairs * length
    own, own_ff = self_query.shape[0], ff_down.shape[0]
    inner = ff_gate.shape[1]
    devices = cube.size

    gains = jnp.stack([self_gain, cross_gain, ff_gain], axis=1)
    gains = jnp.pad(gains, ((0, 0), (0, LANES - 3)))
    attention_shard = jnp.concatenate(
        [
            self_query,
            self_key,
            self_value,
            self_out,
            cross_query,
            cross_key,
            cross_value,
            cross_out,
            gains,
        ],
        axis=1,
    )
    attention = lax.all_gather(attention_shard, BOTH, axis=0, tiled=True)
    stack = -(-own_ff // own)
    down_shard = jnp.pad(ff_down, ((0, stack * own - own_ff), (0, 0)))
    down_shard = [down_shard[c * own : (c + 1) * own] for c in range(stack)]
    ff_shard = jnp.concatenate([ff_gate, ff_up] + down_shard, axis=1)
    ff = lax.all_gather(ff_shard, BOTH, axis=0, tiled=True)

    w_qkv = attention[:, : 3 * width]
    s_out = attention[:, 3 * width : 4 * width]
    c_query = attention[:, 4 * width : 5 * width]
    c_kv = attention[:, 5 * width : 7 * width]
    c_out = attention[:, 7 * width : 8 * width]
    gains = attention[:, 8 * width : 8 * width + 3].astype(f32).T
    gain_one, gain_two, gain_three = gains[0], gains[1], gains[2]
    f_gate_up = ff[:, : 2 * inner]
    f_down = jnp.concatenate(
        [
            ff[:, 2 * inner + c * width : 2 * inner + (c + 1) * width].reshape(devices, own, width)
            for c in range(stack)
        ],
        axis=1,
    )[:, :own_ff].reshape(inner, width)

    places = jnp.arange(length)
    apart = places[:, None] - places[None, :]
    bucket = bucket_of_distance(length, BUCKETS, REACH)
    starts = [int(np.argmax(bucket >= b)) for b in range(1, int(bucket[-1]) + 1)]
    bucket_matrix = sum((apart >= start).astype(jnp.int32) for start in starts)
    onehot = (bucket_matrix[:, :, None] == jnp.arange(BUCKETS)[None, None, :]).astype(bf16)
    bias = jnp.einsum("ijb,bh->hij", onehot, position_bias, preferred_element_type=f32)
    bias = jnp.where((apart >= 0)[None], bias, negative).astype(bf16)

    live = (places[None, :] < target_len[:, None]).astype(f32).reshape(slots, 1)
    inputs = targets.astype(f32).reshape(slots, width)

    memory_rows = lax.all_to_all(memory, "wide", split_axis=0, concat_axis=1, tiled=True)
    memory_rows = memory_rows.reshape(-1, width)
    normed_one = rms_norm(inputs, gain_one).astype(bf16)
    qkv_one = dot(normed_one, w_qkv, NN).astype(bf16).reshape(pairs, length, 3 * width)
    mixed_one, total_one = self_forward(qkv_one, bias)
    mixed_one = mixed_one.reshape(slots, width)
    first = inputs + dot(mixed_one, s_out, NN)
    normed_two = rms_norm(first, gain_two).astype(bf16)
    query_two = dot(normed_two, c_query, NN).astype(bf16).reshape(pairs, length, width)
    kv_two = dot(memory_rows, c_kv, NN).astype(bf16).reshape(pairs, -1, 2 * width)
    mixed_two, total_two = cross_forward(query_two, kv_two, memory_len)
    mixed_two = mixed_two.reshape(slots, width)
    second = first + dot(mixed_two, c_out, NN)
    normed_three = rms_norm(second, gain_three).astype(bf16)
    gate = dot(normed_three, f_gate_up[:, :inner], NN)
    upward = dot(normed_three, f_gate_up[:, inner:], NN)
    activated, gelu_pull = jax.vjp(gelu_tanh, gate)
    hidden = (activated * upward).astype(bf16)
    third = second + dot(hidden, f_down, NN)
    layer_out = (third * live).astype(bf16).reshape(pairs, length, width)

    grad_third = cotangent.astype(f32).reshape(slots, width) * live
    branch_ff = grad_third.astype(bf16)
    d_down = dot(hidden, branch_ff, TN).astype(bf16)
    grad_hidden = dot(branch_ff, f_down, NT)
    grad_gate = gelu_pull(grad_hidden * upward)[0].astype(bf16)
    grad_up = (grad_hidden * activated).astype(bf16)
    d_gate = dot(normed_three, grad_gate, TN).astype(bf16)
    d_up = dot(normed_three, grad_up, TN).astype(bf16)
    grad_normed_three = dot(grad_gate, f_gate_up[:, :inner], NT) + dot(
        grad_up, f_gate_up[:, inner:], NT
    )
    d_down = d_down.reshape(devices, own_ff, width)
    d_down = jnp.pad(d_down, ((0, 0), (0, stack * own - own_ff), (0, 0)))
    d_down = [
        d_down[:, c * own : (c + 1) * own].reshape(devices * own, width) for c in range(stack)
    ]
    ff_grads = lax.psum_scatter(
        jnp.concatenate([d_gate, d_up] + d_down, axis=1),
        BOTH,
        scatter_dimension=0,
        tiled=True,
    ).astype(f32)
    _, norm_three = jax.vjp(rms_norm, second, gain_three)
    back_three, d_gain_three = norm_three(grad_normed_three)
    grad_second = grad_third + back_three

    branch_cross = grad_second.astype(bf16)
    d_cross_out = dot(mixed_two, branch_cross, TN).astype(bf16)
    grad_mixed_two = dot(branch_cross, c_out, NT).astype(bf16).reshape(pairs, length, width)
    grad_query_two, grad_kv_two = cross_backward(
        query_two, kv_two, memory_len, total_two, grad_mixed_two
    )
    grad_query_two = grad_query_two.reshape(slots, width)
    grad_kv_two = grad_kv_two.reshape(-1, 2 * width)
    rows_grad = dot(grad_kv_two, c_kv, NT).astype(bf16).reshape(pairs, -1, width)
    grad_memory = lax.all_to_all(
        rows_grad, "wide", split_axis=1, concat_axis=0, tiled=True
    ).astype(f32)
    d_cross_query = dot(normed_two, grad_query_two, TN).astype(bf16)
    d_cross_kv = dot(memory_rows, grad_kv_two, TN).astype(bf16)
    cross_grads = cube.scatter_both(
        jnp.concatenate([d_cross_query, d_cross_kv, d_cross_out], axis=1)
    )
    _, norm_two = jax.vjp(rms_norm, first, gain_two)
    back_two, d_gain_two = norm_two(dot(grad_query_two, c_query, NT))
    grad_first = grad_second + back_two

    branch_self = grad_first.astype(bf16)
    d_self_out = dot(mixed_one, branch_self, TN).astype(bf16)
    grad_mixed_one = dot(branch_self, s_out, NT).astype(bf16).reshape(pairs, length, width)
    grad_qkv_one, diagonals = self_backward(qkv_one, bias, total_one, grad_mixed_one)
    grad_qkv_one = grad_qkv_one.reshape(slots, 3 * width)
    d_qkv = dot(normed_one, grad_qkv_one, TN).astype(bf16)
    self_grads = cube.scatter_both(jnp.concatenate([d_qkv, d_self_out], axis=1))
    grad_normed_one = dot(grad_qkv_one, w_qkv, NT)
    _, norm_one = jax.vjp(rms_norm, inputs, gain_one)
    back_one, d_gain_one = norm_one(grad_normed_one)
    grad_targets = (grad_first + back_one).reshape(pairs, length, width)

    padded = diagonals.shape[-1]
    column = (padded - np.arange(length)) % padded
    to_bucket = np.zeros((padded, BUCKETS), np.float32)
    to_bucket[column, bucket_of_distance(length, BUCKETS, REACH)] = 1.0
    diagonals = jnp.sum(diagonals, axis=2).reshape(HEADS, padded)
    d_position = jnp.einsum(
        "hc,cb->bh", diagonals, jnp.asarray(to_bucket), precision=lax.Precision.HIGHEST
    )
    small = jnp.concatenate(
        [d_gain_one, d_gain_two, d_gain_three, d_position.reshape(-1)]
    ).reshape(-1, LANES)
    small = jnp.pad(small, ((0, -small.shape[0] % 8), (0, 0)))
    small = cube.total(small).reshape(-1)
    gain_grads = small[: 3 * width].reshape(3, devices, width // devices)
    gain_grads = lax.dynamic_index_in_dim(gain_grads, cube.index, 1, keepdims=False)
    grad_position = small[3 * width : 3 * width + BUCKETS * HEADS].reshape(BUCKETS, HEADS)

    g_down = jnp.concatenate(
        [ff_grads[:, 2 * inner + c * width : 2 * inner + (c + 1) * width] for c in range(stack)],
        axis=0,
    )[:own_ff]
    cut = lambda value, c: value[:, c * width : (c + 1) * width]
    return (
        layer_out,
        grad_targets,
        grad_memory,
        cut(self_grads, 0),
        cut(self_grads, 1),
        cut(self_grads, 2),
        cut(self_grads, 3),
        cut(cross_grads, 0),
        cut(cross_grads, 1),
        cut(cross_grads, 2),
        cut(cross_grads, 3),
        ff_grads[:, :inner],
        ff_grads[:, inner : 2 * inner],
        g_down,
        gain_grads[0],
        gain_grads[1],
        gain_grads[2],
        grad_position,
    )


def solution(mesh):
    rows = P(BOTH, None)
    slots = P(BOTH, None, None)
    one = P(BOTH)
    source = P("narrow", "wide", None)
    in_specs = (slots, source, slots, one, one) + (rows,) * 11 + (one,) * 3 + (P(),)
    out_specs = (slots, slots, source) + (rows,) * 11 + (one,) * 3 + (P(),)
    narrow, wide = mesh.shape["narrow"], mesh.shape["wide"]

    def body(*args):
        return on_device(*args, narrow=narrow, wide=wide)

    return jax.shard_map(body, mesh=mesh, in_specs=in_specs, out_specs=out_specs, check_vma=False)
```

time: 1930 us -> 575 us (0.30)
  waiting for transfers between devices: 1050 us -> 230 us
  local copies, waits for them, and re-layouts: 364 us -> 59.8 us
  blocking collectives: 158 us -> 0 us
  matrix products: 248 us -> 102 us
  Pallas kernels: 0 us -> 91.6 us
  other arithmetic: 72.4 us -> 30.4 us
  starting transfers between devices: 14.2 us -> 38.9 us
    reduce_scatter x9 -> x1, waiting for transfers between devices: 881 us -> 4.88 us  [on_device(): lax.psum_scatter(jnp.concatenate([d_gate, d_up] + d_down, axis=1), BOTH,...]
    gather x2 -> x0, local copies, waits for them, and re-layouts: 303 us -> none  [on_device(): position_bias.astype(jnp.float32)[table]]
    unnamed x2 -> x0, blocking collectives: 158 us -> none
    dot_general x46 -> x26, matrix products: 248 us -> 102 us  [the longest x24 99.2 us: dot(): return lax.dot_general(left, right, dims, preferred_element_type=f32)]
    all_gather x11 -> x2, waiting for transfers between devices: 147 us -> 36.9 us  [the longest x1 21.5 us: on_device(): attention = lax.all_gather(attention_shard, BOTH, axis=0, tiled=True)]
    ppermute x0 -> x25, waiting for transfers between devices: none -> 103 us  [swap(): return lax.ppermute(value, BOTH, pairs)]
    pallas_call x0 -> x4, Pallas kernels: none -> 91.6 us  [the longest x1 34.1 us: cross_backward(): pl.pallas_call(cross_backward_kernel, out_shape=(jax.ShapeDtypeStruct(que...]
    all_to_all x1, waiting for transfers between devices: 0.01 us -> 85 us  [on_device(): lax.all_to_all(memory, 'wide', split_axis=0, concat_axis=1, tiled=True)]
  transfers between devices with their start and end apart: 24 -> 30, of which waited for: 12 -> 17; matrix products, arithmetic and copies ran while one was open for 33% -> 22% of each run, Pallas kernels for 0% -> 6%
where the time goes in v1:
time: 575 us; the launch traced here: 568 us
  waiting for transfers between devices  230 us (40%)
  matrix products  102 us (18%)
  Pallas kernels  91.6 us (16%)
  local copies, waits for them, and re-layouts  59.8 us (10%)
  starting transfers between devices  38.9 us (7%)
  other arithmetic  30.4 us (5%)
  between operations  15.2 us (3%)
    ppermute x25, waiting for transfers between devices, swap(): return lax.ppermute(value, BOTH, pairs)  103 us
    dot_general x24, matrix products, dot(): return lax.dot_general(left, right, dims, preferred_element_type=f32)  99.2 us
    all_to_all x1, waiting for transfers between devices, on_device(): lax.all_to_all(memory, 'wide', split_axis=0, concat_axis=1, tiled=True)  85 us
    pallas_call x1, Pallas kernels, cross_backward(): pl.pallas_call(cross_backward_kernel, out_shape=(jax.ShapeDtypeStruct(que...  34.1 us
    ppermute x25, starting transfers between devices, swap(): return lax.ppermute(value, BOTH, pairs)  27.7 us
    pallas_call x1, Pallas kernels, self_backward(): pl.pallas_call(self_backward_kernel, out_shape=(jax.ShapeDtypeStruct(qkv....  22.3 us
    all_gather x1, waiting for transfers between devices, on_device(): attention = lax.all_gather(attention_shard, BOTH, axis=0, tiled=True)  21.5 us
    pallas_call x1, Pallas kernels, cross_forward(): pl.pallas_call(cross_forward_kernel, out_shape=(jax.ShapeDtypeStruct(quer...  20.1 us
  transfers between devices with their start and end apart: 30, of which 17 were waited for; matrix products, arithmetic and copies ran while one was open for 22% of the time, Pallas kernels for 6%

profile of v1, /device:TPU:0, one launch (start us, length us, event | category | flops | bytes accessed | tf_op | source)
XLA Modules:
  0.0 568.4 jit_solution(11255063471672721970)
XLA Ops:
  19.9 7.3 %all-to-all-start = ((bf16[16,128,768]{2,1,0:T(8,128)(2,1)}), bf16[16,128,768]{2,1,0:T(8,128)(2,1)S(1)}, u32[]{:S(2)}, u32[]{:S(2)}) async-start(bf16[16,128,768]{2,1,0:T(8,128)(2,1)} %param.22), calls=%async_computation | async-start | bytes 6291456 | tf_op jit(solution)/shard_map/all_to_all | solution.py:411
  37.2 85.0 %all-to-all-done = bf16[16,128,768]{2,1,0:T(8,128)(2,1)S(1)} async-done(((bf16[16,128,768]{2,1,0:T(8,128)(2,1)}), bf16[16,128,768]{2,1,0:T(8,128)(2,1)S(1)}, u32[]{:S(2)}, u32[]{:S(2)}) %all-to-all-start) | async-done | bytes 3145760 | tf_op jit(solution)/shard_map/all_to_all | solution.py:411
  124.2 21.5 %all-gather.3.cloned.1.call-done = bf16[768,6272]{1,0:T(8,128)(2,1)} async-done(((bf16[24,6272]{1,0:T(8,128)(2,1)}), bf16[768,6272]{1,0:T(8,128)(2,1)}) %all-gather.3.cloned.1.call-update) | async-done | bytes 9633808 | tf_op jit(solution)/shard_map/all_gather | solution.py:376
  145.7 9.4 %fusion.2 = bf16[2048,1536]{0,1:T(8,128)(2,1)} fusion(bf16[2048,768]{1,0:T(8,128)(2,1)} %bitcast.233, bf16[768,6272]{1,0:T(8,128)(2,1)} %all-gather.3.cloned.1.call-done), kind=kOutput, calls=%fused_computation.7 | convolution fusion | flops 4834983936 | bytes 11796480 | tf_op jit(solution)/shard_map/dot_general | solution.py:27
  155.1 8.7 %copy.82 = bf16[2048,1536]{1,0:T(8,128)(2,1)} copy(bf16[2048,1536]{0,1:T(8,128)(2,1)} %fusion.2) | data formatting | bytes 12582912 | tf_op jit(solution)/shard_map/convert_element_type | solution.py:420
  165.4 5.9 %convolution_convert_fusion.1 = bf16[576,2304]{1,0:T(8,128)(2,1)} fusion(bf16[768,6272]{1,0:T(8,128)(2,1)} %all-gather.3.cloned.1.call-done, f32[768]{0:T(1024)S(1)} %get-tuple-element.96, f32[576]{0:T(1024)S(1)} %rsqrt.36, bf16[576,768]{1,0:T(8,128)(2,1)S(1)} %bitcast.230), kind=kOutput, calls=%fused_computation.20 | convolution fusion | flops 2041528320 | bytes 7083264 | tf_op jit(solution)/shard_map/dot_general | solution.py:27
  171.3 15.0 %self_forward.1 = (bf16[2,288,768]{2,1,0:T(8,128)(2,1)}, f32[2,288,768]{2,1,0:T(8,128)}) custom-call(bf16[2,288,2304]{2,1,0:T(8,128)(2,1)} %bitcast.204, bf16[2,288,2304]{2,1,0:T(8,128)(2,1)} %bitcast.205, bf16[2,288,2304]{2,1,0:T(8,128)(2,1)} %bitcast.206, bf16[12,288,288]{2,1,0:T(8,128)(2,1)} %fusion.25.bias_ref), custom_call_target="tpu_custom_call" | custom-call | flops 509607936 | bytes 5308416 | tf_op jit(solution)/shard_map/self_forward/pallas_call | solution.py:65
  188.9 3.8 convolution_convert_fusion.12
  192.7 20.1 %cross_forward.1 = (bf16[2,288,768]{2,1,0:T(8,128)(2,1)}, f32[2,288,768]{2,1,0:T(8,128)}) custom-call(s32[2]{0:T(128)} %len_ref.3, bf16[2,288,768]{2,1,0:T(8,128)(2,1)} %bitcast.245, bf16[2,1024,1536]{2,1,0:T(8,128)(2,1)} %bitcast.210, bf16[2,1024,1536]{2,1,0:T(8,128)(2,1)} %bitcast.211), custom_call_target="tpu_custom_call" | custom-call | flops 1811939328 | bytes 9830400 | tf_op jit(solution)/shard_map/cross_forward/pallas_call | solution.py:197
  215.7 15.4 %all-gather.5.cloned.1.call-done = bf16[768,6400]{1,0:T(8,128)(2,1)} async-done(((bf16[24,6400]{1,0:T(8,128)(2,1)}), bf16[768,6400]{1,0:T(8,128)(2,1)}) %all-gather.5.cloned.1.call-update) | async-done | bytes 9830416 | tf_op jit(solution)/shard_map/all_gather | solution.py:381
  239.4 6.9 %fusion.10 = (bf16[576,2048]{1,0:T(8,128)(2,1)S(1)}, bf16[576,2048]{1,0:T(8,128)(2,1)S(1)}, bf16[576,2048]{1,0:T(8,128)(2,1)}) fusion(f32[576,2048]{1,0:T(8,128)S(1)} %fusion.114, f32[576,2048]{1,0:T(8,128)S(1)} %fusion.19, bf16[576,768]{1,0:T(8,128)(2,1)S(1)} %multiply_convert_fusion.5, bf16[768,6400]{1,0:T(8,128)(2,1)S(1)} %bitcast.240), kind=kOutput, calls=%fused_computation.17 | convolution fusion | flops 1842610176 | bytes 20545536 | tf_op jit(solution)/shard_map/dot_general | solution.py:27
  246.3 4.0 fusion.12
  258.9 3.1 convolution_convert_fusion.11
  262.1 34.1 %cross_backward.1 = (bf16[2,288,768]{2,1,0:T(8,128)(2,1)}, bf16[2,1024,1536]{2,1,0:T(8,128)(2,1)}) custom-call(s32[2]{0:T(128)} %len_ref.3, bf16[2,288,768]{2,1,0:T(8,128)(2,1)} %bitcast.246, bf16[2,1024,1536]{2,1,0:T(8,128)(2,1)} %bitcast.212, bf16[2,1024,1536]{2,1,0:T(8,128)(2,1)} %bitcast.213, f32[2,288,768]{2,1,0:T(8,128)} %get-tuple-element.28.total_ref, ...), custom_call_target="tpu_custom_call" | custom-call | flops 4529848320 | bytes 17006592 | tf_op jit(solution)/shard_map/cross_backward/pallas_call | solution.py:253
  296.2 4.1 convolution_convert_fusion.8
  306.6 3.1 convolution_convert_fusion.10
  309.7 22.3 %self_backward.1 = (bf16[2,288,2304]{2,1,0:T(8,128)(2,1)}, f32[6,2,8,384]{3,2,1,0:T(8,128)}) custom-call(bf16[2,288,2304]{2,1,0:T(8,128)(2,1)} %bitcast.207, bf16[2,288,2304]{2,1,0:T(8,128)(2,1)} %bitcast.208, bf16[2,288,2304]{2,1,0:T(8,128)(2,1)} %bitcast.209, bf16[12,288,288]{2,1,0:T(8,128)(2,1)} %fusion.25.bias_ref, ...), custom_call_target="tpu_custom_call" | custom-call | flops 1274019840 | bytes 7962624 | tf_op jit(solution)/shard_map/self_backward/pallas_call | solution.py:141
  333.6 6.5 %multiply_reduce_fusion.2 = (f32[768]{0:T(1024)S(1)}, f32[576]{0:T(1024)S(1)}, f32[576,768]{1,0:T(8,128)}) fusion(f32[576]{0:T(1024)S(1)} %copy-done.37, bf16[2,288,768]{2,1,0:T(8,128)(2,1)S(1)} %copy-done.12, f32[768]{0:T(1024)S(1)} %copy-done.35, bf16[576,2304]{1,0:T(8,128)(2,1)} %bitcast.251, bf16[768,6272]{1,0:T(8,128)(2,1)} %all-gather.3.cloned.1.call-done, ...), kind=kOutput, calls=%fused_computation.67 | convolution fusion | flops 2041969408 | bytes 9742848 | tf_op jit(solution)/shard_map/dot_general | solution.py:27
  341.8 4.3 fusion.11
  355.7 8.4 %fusion.16 = bf16[768,1536]{0,1:T(8,128)(2,1)S(1)} fusion(bf16[2048,1536]{1,0:T(8,128)(2,1)} %bitcast.254, bf16[2048,768]{1,0:T(8,128)(2,1)} %bitcast.234), kind=kOutput, calls=%fused_computation.35 | convolution fusion | flops 4833017856 | bytes 11796480 | tf_op jit(solution)/shard_map/dot_general | solution.py:27
  375.7 5.4 bitcast_convert_fusion
  388.6 7.2 %convolution_convert_fusion.6 = bf16[2048,768]{1,0:T(8,128)(2,1)S(1)} fusion(bf16[2048,1536]{1,0:T(8,128)(2,1)S(1)} %bitcast.257, bf16[768,6272]{1,0:T(8,128)(2,1)} %all-gather.3.cloned.1.call-done), kind=kOutput, calls=%fused_computation.29 | convolution fusion | flops 4833411072 | bytes 11796480 | tf_op jit(solution)/shard_map/dot_general | solution.py:27
  395.8 4.9 copy.83
  400.7 3.8 all-to-all-start.1
  406.9 3.9 fusion.34
  423.8 29.1 %collective-permute-done.16 = bf16[2,2,2,24,1536]{4,3,2,1,0:T(8,128)(2,1)S(1)} collective-permute-done((bf16[2,2,2,24,1536]{4,3,2,1,0:T(8,128)(2,1)S(1)}, bf16[2,2,2,24,1536]{4,3,2,1,0:T(8,128)(2,1)S(1)}, u32[]{:S(2)}, u32[]{:S(2)}) %collective-permute-start.16) | collective-permute-done | bytes 589856 | tf_op jit(solution)/shard_map/ppermute | solution.py:283
  454.1 3.1 collective-permute-start.12
  457.3 22.4 %collective-permute-done.6 = bf16[2,2,2,24,1536]{4,3,2,1,0:T(8,128)(2,1)S(1)} collective-permute-done((bf16[2,2,2,24,1536]{4,3,2,1,0:T(8,128)(2,1)S(1)}, bf16[2,2,2,24,1536]{4,3,2,1,0:T(8,128)(2,1)S(1)}, u32[]{:S(2)}, u32[]{:S(2)}) %collective-permute-start.6) | collective-permute-done | bytes 589856 | tf_op jit(solution)/shard_map/ppermute | solution.py:283
  482.1 6.1 %collective-permute-start.18 = (bf16[2,24,1536]{2,1,0:T(8,128)(2,1)S(1)}, bf16[2,24,1536]{2,1,0:T(8,128)(2,1)S(1)}, u32[]{:S(2)}, u32[]{:S(2)}) collective-permute-start(bf16[2,24,1536]{2,1,0:T(8,128)(2,1)S(1)} %dynamic-slice_bitcast_fusion.10), channel_id=1, source_target_pairs={{0,4},{1,5},{2,6},{3,7},{4,0},{5,1},{6,2},{7,3},{8,12},{9,13},{10,... | collective-permute-start | bytes 442376 | tf_op jit(solution)/shard_map/ppermute | solution.py:283
  498.5 33.3 %collective-permute-done.18 = bf16[2,24,1536]{2,1,0:T(8,128)(2,1)S(1)} collective-permute-done((bf16[2,24,1536]{2,1,0:T(8,128)(2,1)S(1)}, bf16[2,24,1536]{2,1,0:T(8,128)(2,1)S(1)}, u32[]{:S(2)}, u32[]{:S(2)}) %collective-permute-start.18) | collective-permute-done | bytes 147488 | tf_op jit(solution)/shard_map/ppermute | solution.py:283
  549.9 3.4 copy.84
  553.4 4.9 reduce-scatter.2.cloned.1.call-done
  (282 shorter events, 136.8 us)
Async XLA Ops:
  7.2 138.5 %all-gather.3.cloned.1.call-start = ((), (), s32[]{:S(2)}) async-start(), calls=%async_computation.3 | async-start | bytes 9934848 | tf_op jit(solution)/shard_map/all_gather | solution.py:376
  15.0 216.1 %all-gather.5.cloned.1.call-start = ((), (), s32[]{:S(2)}) async-start(), calls=%async_computation.4 | async-start | bytes 10137600 | tf_op jit(solution)/shard_map/all_gather | solution.py:381
  19.9 102.4 %all-to-all-start = ((bf16[16,128,768]{2,1,0:T(8,128)(2,1)}), bf16[16,128,768]{2,1,0:T(8,128)(2,1)S(1)}, u32[]{:S(2)}, u32[]{:S(2)}) async-start(bf16[16,128,768]{2,1,0:T(8,128)(2,1)} %param.22), calls=%async_computation | async-start | bytes 6291456 | tf_op jit(solution)/shard_map/all_to_all | solution.py:411
  27.2 531.1 %reduce-scatter.2.cloned.1.call-start = ((), (), s32[]{:S(2)}) async-start(), calls=%async_computation.5 | async-start | bytes 10137600 | tf_op jit(solution)/shard_map/reduce_scatter | solution.py:448
  29.3 136.1 %copy-start.36 = (f32[576]{0:T(1024)}, f32[576]{0:T(1024)S(1)}, u32[]{:S(2)}) copy-start(f32[576]{0:T(1024)S(1)} %rsqrt.36) | copy-start | bytes 6916
  262.1 34.1 %copy-start.31 = (f32[576]{0:T(1024)S(1)}, f32[576]{0:T(1024)}, u32[]{:S(2)}) copy-start(f32[576]{0:T(1024)} %copy-done.30) | copy-start | bytes 6916
  340.2 41.3 %collective-permute-start.20 = (f32[24,128]{1,0:T(8,128)S(1)}, f32[24,128]{1,0:T(8,128)S(1)}, u32[]{:S(2)}, u32[]{:S(2)}) collective-permute-start(f32[24,128]{1,0:T(8,128)S(1)} %pad.19), channel_id=1, source_target_pairs={{0,1},{1,0},{2,3},{3,2},{4,5},{5,4},{6,7},{7,6},{8,9},{9,8},{10,11... | collective-permute-start | bytes 36872 | tf_op jit(solution)/shard_map/ppermute | solution.py:283
  370.8 41.4 %collective-permute-start.15 = (bf16[2,2,2,2,24,1536]{5,4,3,2,1,0:T(8,128)(2,1)}, bf16[2,2,2,2,24,1536]{5,4,3,2,1,0:T(8,128)(2,1)}, u32[]{:S(2)}, u32[]{:S(2)}) collective-permute-start(bf16[2,2,2,2,24,1536]{5,4,3,2,1,0:T(8,128)(2,1)} %dynamic-slice_bitcast_fusion), channel_id=1, source_target_pairs={{0,8},{1,9},{2,10},{3,11},{4,12},{5,13},{6,14},{7,15},{8,0},{9,1},... | collective-permute-start | bytes 3538952 | tf_op jit(solution)/shard_map/ppermute | solution.py:283
  375.6 40.8 %collective-permute-start.10 = (bf16[2,2,2,2,24,1536]{5,4,3,2,1,0:T(8,128)(2,1)}, bf16[2,2,2,2,24,1536]{5,4,3,2,1,0:T(8,128)(2,1)}, u32[]{:S(2)}, u32[]{:S(2)}) collective-permute-start(bf16[2,2,2,2,24,1536]{5,4,3,2,1,0:T(8,128)(2,1)} %dynamic-slice_bitcast_fusion.1), channel_id=1, source_target_pairs={{0,8},{1,9},{2,10},{3,11},{4,12},{5,13},{6,14},{7,15},{8,0},{9,1},... | collective-permute-start | bytes 3538952 | tf_op jit(solution)/shard_map/ppermute | solution.py:283
  381.5 6.0 %collective-permute-start.21 = (f32[24,128]{1,0:T(8,128)S(1)}, f32[24,128]{1,0:T(8,128)S(1)}, u32[]{:S(2)}, u32[]{:S(2)}) collective-permute-start(f32[24,128]{1,0:T(8,128)S(1)} %pad_add_fusion), channel_id=1, source_target_pairs={{0,2},{1,3},{2,0},{3,1},{4,6},{5,7},{6,4},{7,5},{8,10},{9,11},{10,... | collective-permute-start | bytes 36872 | tf_op jit(solution)/shard_map/ppermute | solution.py:283
  385.9 33.1 %collective-permute-start.5 = (bf16[2,2,2,2,24,1536]{5,4,2,1,0,3:T(8,128)(2,1)}, bf16[2,2,2,2,24,1536]{5,4,2,1,0,3:T(8,128)(2,1)}, u32[]{:S(2)}, u32[]{:S(2)}) collective-permute-start(bf16[2,2,2,2,24,1536]{5,4,2,1,0,3:T(8,128)(2,1)} %bitcast.201), channel_id=1, source_target_pairs={{0,8},{1,9},{2,10},{3,11},{4,12},{5,13},{6,14},{7,15},{8,0},{9,1},... | collective-permute-start | bytes 3538952 | tf_op jit(solution)/shard_map/ppermute | solution.py:283
  387.1 33.8 %collective-permute-start = (bf16[2,2,2,2,24,1536]{5,4,2,1,3,0:T(8,128)(2,1)}, bf16[2,2,2,2,24,1536]{5,4,2,1,3,0:T(8,128)(2,1)}, u32[]{:S(2)}, u32[]{:S(2)}) collective-permute-start(bf16[2,2,2,2,24,1536]{5,4,2,1,3,0:T(8,128)(2,1)} %bitcast.202), channel_id=1, source_target_pairs={{0,8},{1,9},{2,10},{3,11},{4,12},{5,13},{6,14},{7,15},{8,0},{9,1},... | collective-permute-start | bytes 3538952 | tf_op jit(solution)/shard_map/ppermute | solution.py:283
  387.5 17.0 %collective-permute-start.22 = (f32[24,128]{1,0:T(8,128)S(1)}, f32[24,128]{1,0:T(8,128)S(1)}, u32[]{:S(2)}, u32[]{:S(2)}) collective-permute-start(f32[24,128]{1,0:T(8,128)S(1)} %add.514), channel_id=1, source_target_pairs={{0,4},{1,5},{2,6},{3,7},{4,0},{5,1},{6,2},{7,3},{8,12},{9,13},{10,... | collective-permute-start | bytes 36872 | tf_op jit(solution)/shard_map/ppermute | solution.py:283
  400.7 147.1 %all-to-all-start.1 = ((bf16[2,1024,768]{2,0,1:T(2,128)(2,1)}), bf16[2,1024,768]{2,0,1:T(2,128)(2,1)S(1)}, u32[]{:S(2)}, u32[]{:S(2)}) async-start(bf16[2,1024,768]{2,0,1:T(2,128)(2,1)} %copy.83), calls=%async_computation.1 | async-start | bytes 6291456 | tf_op jit(solution)/shard_map/all_to_all | solution.py:467
  404.5 1.2 collective-permute-start.23
  405.7 5.0 collective-permute-start.24
  414.4 38.6 %collective-permute-start.16 = (bf16[2,2,2,24,1536]{4,3,2,1,0:T(8,128)(2,1)S(1)}, bf16[2,2,2,24,1536]{4,3,2,1,0:T(8,128)(2,1)S(1)}, u32[]{:S(2)}, u32[]{:S(2)}) collective-permute-start(bf16[2,2,2,24,1536]{4,3,2,1,0:T(8,128)(2,1)S(1)} %dynamic-slice_bitcast_fusion.2), channel_id=1, source_target_pairs={{0,1},{1,0},{2,3},{3,2},{4,5},{5,4},{6,7},{7,6},{8,9},{9,8},{10,11... | collective-permute-start | bytes 1769480 | tf_op jit(solution)/shard_map/ppermute | solution.py:283
  418.1 35.9 %collective-permute-start.11 = (bf16[2,2,2,24,1536]{4,3,2,1,0:T(8,128)(2,1)S(1)}, bf16[2,2,2,24,1536]{4,3,2,1,0:T(8,128)(2,1)S(1)}, u32[]{:S(2)}, u32[]{:S(2)}) collective-permute-start(bf16[2,2,2,24,1536]{4,3,2,1,0:T(8,128)(2,1)S(1)} %dynamic-slice_bitcast_fusion.3), channel_id=1, source_target_pairs={{0,16},{1,17},{2,18},{3,19},{4,20},{5,21},{6,22},{7,23},{8,24},{9,... | collective-permute-start | bytes 1769480 | tf_op jit(solution)/shard_map/ppermute | solution.py:283
  420.7 59.0 %collective-permute-start.6 = (bf16[2,2,2,24,1536]{4,3,2,1,0:T(8,128)(2,1)S(1)}, bf16[2,2,2,24,1536]{4,3,2,1,0:T(8,128)(2,1)S(1)}, u32[]{:S(2)}, u32[]{:S(2)}) collective-permute-start(bf16[2,2,2,24,1536]{4,3,2,1,0:T(8,128)(2,1)S(1)} %dynamic-slice_bitcast_fusion.4), channel_id=1, source_target_pairs={{0,1},{1,0},{2,3},{3,2},{4,5},{5,4},{6,7},{7,6},{8,9},{9,8},{10,11... | collective-permute-start | bytes 1769480 | tf_op jit(solution)/shard_map/ppermute | solution.py:283
  422.6 59.1 %collective-permute-start.1 = (bf16[2,2,2,24,1536]{4,3,1,0,2:T(8,128)(2,1)S(1)}, bf16[2,2,2,24,1536]{4,3,1,0,2:T(8,128)(2,1)S(1)}, u32[]{:S(2)}, u32[]{:S(2)}) collective-permute-start(bf16[2,2,2,24,1536]{4,3,1,0,2:T(8,128)(2,1)S(1)} %dynamic-slice_bitcast_fusion.5), channel_id=1, source_target_pairs={{0,16},{1,17},{2,18},{3,19},{4,20},{5,21},{6,22},{7,23},{8,24},{9,... | collective-permute-start | bytes 1769480 | tf_op jit(solution)/shard_map/ppermute | solution.py:283
  453.1 28.8 %collective-permute-start.17 = (bf16[2,2,24,1536]{3,2,1,0:T(8,128)(2,1)S(1)}, bf16[2,2,24,1536]{3,2,1,0:T(8,128)(2,1)S(1)}, u32[]{:S(2)}, u32[]{:S(2)}) collective-permute-start(bf16[2,2,24,1536]{3,2,1,0:T(8,128)(2,1)S(1)} %dynamic-slice_bitcast_fusion.6), channel_id=1, source_target_pairs={{0,16},{1,17},{2,18},{3,19},{4,20},{5,21},{6,22},{7,23},{8,24},{9,... | collective-permute-start | bytes 884744 | tf_op jit(solution)/shard_map/ppermute | solution.py:283
  454.1 36.9 %collective-permute-start.12 = (bf16[2,2,24,1536]{3,2,1,0:T(8,128)(2,1)S(1)}, bf16[2,2,24,1536]{3,2,1,0:T(8,128)(2,1)S(1)}, u32[]{:S(2)}, u32[]{:S(2)}) collective-permute-start(bf16[2,2,24,1536]{3,2,1,0:T(8,128)(2,1)S(1)} %dynamic-slice_bitcast_fusion.7), channel_id=1, source_target_pairs={{0,1},{1,0},{2,3},{3,2},{4,5},{5,4},{6,7},{7,6},{8,9},{9,8},{10,11... | collective-permute-start | bytes 884744 | tf_op jit(solution)/shard_map/ppermute | solution.py:283
  479.9 11.6 %collective-permute-start.7 = (bf16[2,2,24,1536]{3,2,1,0:T(8,128)(2,1)S(1)}, bf16[2,2,24,1536]{3,2,1,0:T(8,128)(2,1)S(1)}, u32[]{:S(2)}, u32[]{:S(2)}) collective-permute-start(bf16[2,2,24,1536]{3,2,1,0:T(8,128)(2,1)S(1)} %dynamic-slice_bitcast_fusion.8), channel_id=1, source_target_pairs={{0,16},{1,17},{2,18},{3,19},{4,20},{5,21},{6,22},{7,23},{8,24},{9,... | collective-permute-start | bytes 884744 | tf_op jit(solution)/shard_map/ppermute | solution.py:283
  481.9 14.4 %collective-permute-start.2 = (bf16[2,2,24,1536]{3,2,1,0:T(8,128)(2,1)S(1)}, bf16[2,2,24,1536]{3,2,1,0:T(8,128)(2,1)S(1)}, u32[]{:S(2)}, u32[]{:S(2)}) collective-permute-start(bf16[2,2,24,1536]{3,2,1,0:T(8,128)(2,1)S(1)} %dynamic-slice_bitcast_fusion.9), channel_id=1, source_target_pairs={{0,1},{1,0},{2,3},{3,2},{4,5},{5,4},{6,7},{7,6},{8,9},{9,8},{10,11... | collective-permute-start | bytes 884744 | tf_op jit(solution)/shard_map/ppermute | solution.py:283
  482.1 49.7 %collective-permute-start.18 = (bf16[2,24,1536]{2,1,0:T(8,128)(2,1)S(1)}, bf16[2,24,1536]{2,1,0:T(8,128)(2,1)S(1)}, u32[]{:S(2)}, u32[]{:S(2)}) collective-permute-start(bf16[2,24,1536]{2,1,0:T(8,128)(2,1)S(1)} %dynamic-slice_bitcast_fusion.10), channel_id=1, source_target_pairs={{0,4},{1,5},{2,6},{3,7},{4,0},{5,1},{6,2},{7,3},{8,12},{9,13},{10,... | collective-permute-start | bytes 442376 | tf_op jit(solution)/shard_map/ppermute | solution.py:283
  491.1 43.9 %collective-permute-start.13 = (bf16[2,24,1536]{2,1,0:T(8,128)(2,1)S(1)}, bf16[2,24,1536]{2,1,0:T(8,128)(2,1)S(1)}, u32[]{:S(2)}, u32[]{:S(2)}) collective-permute-start(bf16[2,24,1536]{2,1,0:T(8,128)(2,1)S(1)} %dynamic-slice_bitcast_fusion.11), channel_id=1, source_target_pairs={{0,4},{1,5},{2,6},{3,7},{4,0},{5,1},{6,2},{7,3},{8,12},{9,13},{10,... | collective-permute-start | bytes 442376 | tf_op jit(solution)/shard_map/ppermute | solution.py:283
  491.6 46.6 %collective-permute-start.8 = (bf16[2,24,1536]{2,1,0:T(8,128)(2,1)S(1)}, bf16[2,24,1536]{2,1,0:T(8,128)(2,1)S(1)}, u32[]{:S(2)}, u32[]{:S(2)}) collective-permute-start(bf16[2,24,1536]{2,1,0:T(8,128)(2,1)S(1)} %dynamic-slice_bitcast_fusion.12), channel_id=1, source_target_pairs={{0,4},{1,5},{2,6},{3,7},{4,0},{5,1},{6,2},{7,3},{8,12},{9,13},{10,... | collective-permute-start | bytes 442376 | tf_op jit(solution)/shard_map/ppermute | solution.py:283
  496.4 44.0 %collective-permute-start.3 = (bf16[2,24,1536]{2,1,0:T(8,128)(2,1)S(1)}, bf16[2,24,1536]{2,1,0:T(8,128)(2,1)S(1)}, u32[]{:S(2)}, u32[]{:S(2)}) collective-permute-start(bf16[2,24,1536]{2,1,0:T(8,128)(2,1)S(1)} %dynamic-slice_bitcast_fusion.13), channel_id=1, source_target_pairs={{0,4},{1,5},{2,6},{3,7},{4,0},{5,1},{6,2},{7,3},{8,12},{9,13},{10,... | collective-permute-start | bytes 442376 | tf_op jit(solution)/shard_map/ppermute | solution.py:283
  531.9 10.0 %collective-permute-start.19 = (bf16[24,1536]{1,0:T(8,128)(2,1)S(1)}, bf16[24,1536]{1,0:T(8,128)(2,1)S(1)}, u32[]{:S(2)}, u32[]{:S(2)}) collective-permute-start(bf16[24,1536]{1,0:T(8,128)(2,1)S(1)} %dynamic-slice_bitcast_fusion.14), channel_id=1, source_target_pairs={{0,2},{1,3},{2,0},{3,1},{4,6},{5,7},{6,4},{7,5},{8,10},{9,11},{10,... | collective-permute-start | bytes 221192 | tf_op jit(solution)/shard_map/ppermute | solution.py:283
  535.1 8.4 %collective-permute-start.14 = (bf16[24,1536]{1,0:T(8,128)(2,1)S(1)}, bf16[24,1536]{1,0:T(8,128)(2,1)S(1)}, u32[]{:S(2)}, u32[]{:S(2)}) collective-permute-start(bf16[24,1536]{1,0:T(8,128)(2,1)S(1)} %dynamic-slice_bitcast_fusion.15), channel_id=1, source_target_pairs={{0,2},{1,3},{2,0},{3,1},{4,6},{5,7},{6,4},{7,5},{8,10},{9,11},{10,... | collective-permute-start | bytes 221192 | tf_op jit(solution)/shard_map/ppermute | solution.py:283
  538.3 6.8 %collective-permute-start.9 = (bf16[24,1536]{1,0:T(8,128)(2,1)S(1)}, bf16[24,1536]{1,0:T(8,128)(2,1)S(1)}, u32[]{:S(2)}, u32[]{:S(2)}) collective-permute-start(bf16[24,1536]{1,0:T(8,128)(2,1)S(1)} %dynamic-slice_bitcast_fusion.16), channel_id=1, source_target_pairs={{0,2},{1,3},{2,0},{3,1},{4,6},{5,7},{6,4},{7,5},{8,10},{9,11},{10,... | collective-permute-start | bytes 221192 | tf_op jit(solution)/shard_map/ppermute | solution.py:283
  540.4 6.7 %collective-permute-start.4 = (bf16[24,1536]{1,0:T(8,128)(2,1)S(1)}, bf16[24,1536]{1,0:T(8,128)(2,1)S(1)}, u32[]{:S(2)}, u32[]{:S(2)}) collective-permute-start(bf16[24,1536]{1,0:T(8,128)(2,1)S(1)} %dynamic-slice_bitcast_fusion.17), channel_id=1, source_target_pairs={{0,2},{1,3},{2,0},{3,1},{4,6},{5,7},{6,4},{7,5},{8,10},{9,11},{10,... | collective-permute-start | bytes 221192 | tf_op jit(solution)/shard_map/ppermute | solution.py:283
  (50 other events, 468.6 us)
Sparse Core Ops, SparseCore 0:
  15.1 130.5 all-gather.2
  148.6 82.3 all-gather.4
  355.8 202.3 reduce-scatter.1

commit v2 on v1

v2 whole, which is shorter than its diff:
```python
import functools

import jax
import jax.numpy as jnp
import numpy as np
from jax import lax
from jax.experimental import pallas as pl
from jax.experimental.pallas import tpu as pltpu
from jax.sharding import PartitionSpec as P

HEADS = 12
HEAD_DIM = 64
BUCKETS = 32
REACH = 128
LANES = 128
BOTH = ("narrow", "wide")
SHARE = 8

negative = -1e30
epsilon = 1e-06
bf16 = jnp.bfloat16
f32 = jnp.float32

NT = (((1,), (1,)), ((), ()))
NN = (((1,), (0,)), ((), ()))
TN = (((0,), (0,)), ((), ()))


def cost(flops=0, transcendentals=0, bytes_accessed=0):
    return pl.CostEstimate(
        flops=flops // SHARE,
        transcendentals=transcendentals // SHARE,
        bytes_accessed=bytes_accessed // SHARE,
    )


def dot(left, right, dims):
    return lax.dot_general(left, right, dims, preferred_element_type=f32)


def bucket_of_distance(length, buckets, reach):
    apart = np.arange(length)
    exact = buckets // 2
    safe = np.maximum(apart, 1)
    far = exact + (np.log(safe / exact) / np.log(reach / exact) * (buckets - exact)).astype(
        np.int64
    )
    far = np.minimum(far, buckets - 1)
    return np.where(apart < exact, apart, far).astype(np.int32)


def of_head(h, first, value):
    return jnp.where(first if h == 0 else ~first, value, jnp.zeros_like(value))


def self_forward_kernel(q_ref, k_ref, v_ref, bias_ref, mixed_ref, total_ref):
    q, k, v = q_ref[0], k_ref[0], v_ref[0]
    first = lax.broadcasted_iota(jnp.int32, q.shape, 1) < HEAD_DIM
    mixed, totals = [], []
    for h in range(2):
        scores = dot(of_head(h, first, q), k, NT) + bias_ref[h].astype(f32)
        top = jnp.max(scores, axis=1, keepdims=True)
        grown = jnp.exp(scores - top)
        total = jnp.sum(grown, axis=1, keepdims=True)
        mixed.append(dot((grown * (1.0 / total)).astype(bf16), v, NN))
        totals.append(top + jnp.log(total))
    mixed_ref[0] = jnp.where(first, mixed[0], mixed[1]).astype(bf16)
    total_ref[0] = jnp.where(first, totals[0], totals[1])


def self_forward(qkv, bias):
    pairs, length, width = qkv.shape
    width //= 3
    steps = width // LANES
    part = lambda c: pl.BlockSpec((1, length, LANES), lambda p, h: (p, 0, h + c * steps))
    return pl.pallas_call(
        self_forward_kernel,
        out_shape=(
            jax.ShapeDtypeStruct((pairs, length, width), bf16),
            jax.ShapeDtypeStruct((pairs, length, width), f32),
        ),
        grid=(pairs, steps),
        in_specs=[
            part(0),
            part(1),
            part(2),
            pl.BlockSpec((2, length, length), lambda p, h: (h, 0, 0)),
        ],
        out_specs=[part(0), part(0)],
        cost_estimate=cost(
            flops=pairs * HEADS * length * length * HEAD_DIM * 4,
            transcendentals=pairs * HEADS * length * length,
            bytes_accessed=pairs * length * width * 12,
        ),
        name="self_forward",
    )(qkv, qkv, qkv, bias)


def self_backward_kernel(
    q_ref, k_ref, v_ref, bias_ref, total_ref, grad_ref, grads_ref, diagonal_ref, sum_ref
):
    p, hp = pl.program_id(0), pl.program_id(1)
    steps = pl.num_programs(1)
    q, k, v, grad, total = q_ref[0], k_ref[0], v_ref[0], grad_ref[0], total_ref[0]
    length, padded = q.shape[0], sum_ref.shape[-1]
    first = lax.broadcasted_iota(jnp.int32, q.shape, 1) < HEAD_DIM

    @pl.when(p == 0)
    def _():
        sum_ref[hp] = jnp.zeros(sum_ref.shape[1:], f32)

    found = []
    for h in range(2):
        scores = dot(of_head(h, first, q), k, NT) + bias_ref[h].astype(f32)
        probs = jnp.exp(scores - total[:, HEAD_DIM * h : HEAD_DIM * h + 1])
        grad_probs = dot(of_head(h, first, grad), v, NT)
        inner = jnp.sum(probs * grad_probs, axis=1, keepdims=True)
        grad_scores = (probs * (grad_probs - inner)).astype(bf16)
        sum_ref[hp, h, :, :length] += grad_scores.astype(f32)
        found.append(
            (
                dot(grad_scores, k, NN),
                dot(grad_scores, q, TN),
                dot(probs.astype(bf16), grad, TN),
            )
        )
    for c in range(3):
        grads_ref[0, :, pl.ds(pl.multiple_of((hp + c * steps) * LANES, LANES), LANES)] = (
            jnp.where(first, found[0][c], found[1][c]).astype(bf16)
        )

    @pl.when(p == pl.num_programs(0) - 1)
    def _():
        rows = lax.broadcasted_iota(jnp.int32, (8, padded), 0)
        for h in range(2):
            held = sum_ref[hp, h, 0:8, :]
            for i in range(8, length, 8):
                held = held + pltpu.roll(sum_ref[hp, h, i : i + 8, :], padded - i, 1)
            for bit in (1, 2, 4):
                held = jnp.where(
                    (rows // bit) % 2 == 1, pltpu.roll(held, padded - bit, 1), held
                )
            diagonal_ref[0, h] = held


def self_backward(qkv, bias, total, grad):
    pairs, length, width = qkv.shape
    width //= 3
    steps = width // LANES
    padded = -(-length // LANES) * LANES
    part = lambda c: pl.BlockSpec((1, length, LANES), lambda p, h: (p, 0, h + c * steps))
    return pl.pallas_call(
        self_backward_kernel,
        out_shape=(
            jax.ShapeDtypeStruct(qkv.shape, bf16),
            jax.ShapeDtypeStruct((steps, 2, 8, padded), f32),
        ),
        grid=(pairs, steps),
        in_specs=[
            part(0),
            part(1),
            part(2),
            pl.BlockSpec((2, length, length), lambda p, h: (h, 0, 0)),
            part(0),
            part(0),
        ],
        out_specs=[
            pl.BlockSpec((1, length, 3 * width), lambda p, h: (p, 0, 0)),
            pl.BlockSpec((1, 2, 8, padded), lambda p, h: (h, 0, 0, 0)),
        ],
        scratch_shapes=[pltpu.VMEM((steps, 2, length, padded), f32)],
        cost_estimate=cost(
            flops=pairs * HEADS * length * length * HEAD_DIM * 10,
            transcendentals=pairs * HEADS * length * length,
            bytes_accessed=pairs * length * width * 18,
        ),
        name="self_backward",
    )(qkv, qkv, qkv, bias, total, grad)


def dead_rows(live_rows, rows):
    places = lax.broadcasted_iota(jnp.int32, (1, rows), 1)
    return jnp.where(places < live_rows, 0.0, negative)


def cross_forward_kernel(pair, len_ref, q_ref, memory_ref, wk_ref, wv_ref, *refs):
    mixed_ref, total_ref, k_ref, v_ref = refs[-4:]
    q = q_ref[0]
    rows = k_ref.shape[1]
    memory = memory_ref[...].reshape(rows, -1)
    kv = dot(memory, jnp.concatenate([wk_ref[...], wv_ref[...]], axis=1), NN).astype(bf16)
    k, v = kv[:, :LANES], kv[:, LANES:]
    k_ref[0], v_ref[0] = k, v
    first = lax.broadcasted_iota(jnp.int32, q.shape, 1) < HEAD_DIM
    dead = dead_rows(len_ref[pair], rows)
    mixed, totals = [], []
    for h in range(2):
        scores = dot(of_head(h, first, q), k, NT) + dead
        top = jnp.max(scores, axis=1, keepdims=True)
        grown = jnp.exp(scores - top)
        total = jnp.sum(grown, axis=1, keepdims=True)
        mixed.append(dot((grown * (1.0 / total)).astype(bf16), v, NN))
        totals.append(top + jnp.log(total))
    mixed_ref[0] = jnp.where(first, mixed[0], mixed[1]).astype(bf16)
    total_ref[0] = jnp.where(first, totals[0], totals[1])


def cross_forward(pair, query, memory, query_key, value_out, lens, before):
    pairs, length, width = query.shape
    sources, _, part, _ = memory.shape
    rows = sources * part
    steps = width // LANES
    target = pl.BlockSpec((1, length, LANES), lambda h, n: (pair, 0, h))
    source = pl.BlockSpec((1, rows, LANES), lambda h, n: (pair, 0, h))
    weight = lambda c: pl.BlockSpec((width, LANES), lambda h, n: (0, h + c * steps))
    return pl.pallas_call(
        functools.partial(cross_forward_kernel, pair),
        out_shape=(
            jax.ShapeDtypeStruct(query.shape, bf16),
            jax.ShapeDtypeStruct(query.shape, f32),
            jax.ShapeDtypeStruct((pairs, rows, width), bf16),
            jax.ShapeDtypeStruct((pairs, rows, width), bf16),
        ),
        grid_spec=pltpu.PrefetchScalarGridSpec(
            num_scalar_prefetch=1,
            grid=(steps,),
            in_specs=[
                target,
                pl.BlockSpec((sources, 1, part, width), lambda h, n: (0, pair, 0, 0)),
                weight(1),
                weight(0),
            ]
            + [pl.BlockSpec(memory_space=pl.ANY)] * len(before),
            out_specs=[target, target, source, source],
        ),
        input_output_aliases={5 + i: i for i in range(len(before))},
        cost_estimate=cost(
            flops=rows * width * (length * 4 + width * 4),
            transcendentals=HEADS * length * rows,
            bytes_accessed=length * width * 8 + rows * width * 6,
        ),
        name="cross_forward",
    )(lens, query, memory, query_key, value_out, *before)


def cross_backward_kernel(
    pair, last, len_ref, q_ref, k_ref, v_ref, total_ref, grad_ref, memory_ref, wk_ref, wv_ref, *refs
):
    turned_ref, rows_ref = refs[-2:]
    hp, steps = pl.program_id(0), pl.num_programs(0)
    q, k, v, grad, total = q_ref[0], k_ref[0], v_ref[0], grad_ref[0], total_ref[0]
    rows = k.shape[0]
    first = lax.broadcasted_iota(jnp.int32, q.shape, 1) < HEAD_DIM
    first_row = lax.broadcasted_iota(jnp.int32, k.shape, 1) < HEAD_DIM
    dead = dead_rows(len_ref[pair], rows)
    if pair:
        before_ref, _, *refs = refs
    if last:
        grad_query_ref, grad_memory_ref, d_key_ref, d_value_ref = refs[:4]
    else:
        grad_query_ref, grad_memory_ref, sum_ref = refs[:3]

    @pl.when(hp == 0)
    def _():
        turned_ref[...] = memory_ref[...].reshape(rows, -1).T

    found = []
    for h in range(2):
        scores = dot(of_head(h, first, q), k, NT) + dead
        probs = jnp.exp(scores - total[:, HEAD_DIM * h : HEAD_DIM * h + 1])
        grad_probs = dot(of_head(h, first, grad), v, NT)
        inner = jnp.sum(probs * grad_probs, axis=1, keepdims=True)
        grad_scores = (probs * (grad_probs - inner)).astype(bf16)
        found.append(
            (
                dot(grad_scores, k, NN),
                dot(grad_scores, q, TN),
                dot(probs.astype(bf16), grad, TN),
            )
        )
    grad_query_ref[0] = jnp.where(first, found[0][0], found[1][0]).astype(bf16)
    grad_kv = jnp.concatenate(
        [jnp.where(first_row, found[0][c], found[1][c]).astype(bf16) for c in (1, 2)], axis=1
    )
    weight = jnp.concatenate([wk_ref[...], wv_ref[...]], axis=1)
    back = dot(grad_kv, weight, NT)

    @pl.when(hp == 0)
    def _():
        rows_ref[...] = back

    @pl.when(hp > 0)
    def _():
        rows_ref[...] += back

    @pl.when(hp == steps - 1)
    def _():
        grad_memory_ref[...] = rows_ref[...].astype(bf16).reshape(grad_memory_ref.shape)

    d_kv = dot(turned_ref[...], grad_kv, NN)
    if pair:
        d_kv = d_kv + before_ref[0]
    if last:
        d_key_ref[...] = d_kv[:, :LANES].astype(bf16)
        d_value_ref[...] = d_kv[:, LANES:].astype(bf16)
    else:
        sum_ref[0] = d_kv


def cross_backward(
    pair, query, key, value, lens, total, grad, memory, query_key, value_out, before
):
    pairs, length, width = query.shape
    sources, _, part, _ = memory.shape
    rows = sources * part
    steps = width // LANES
    last = pair == pairs - 1
    target = pl.BlockSpec((1, length, LANES), lambda h, n: (pair, 0, h))
    source = pl.BlockSpec((1, rows, LANES), lambda h, n: (pair, 0, h))
    weight = lambda c: pl.BlockSpec((width, LANES), lambda h, n: (0, h + c * steps))
    held = pl.BlockSpec((sources, 1, part, width), lambda h, n: (0, pair, 0, 0))
    given = pl.BlockSpec((sources, part, width), lambda h, n: (0, 0, 0))
    sums = pl.BlockSpec((1, width, 2 * LANES), lambda h, n: (h, 0, 0))
    out_shape = [jax.ShapeDtypeStruct(query.shape, bf16), jax.ShapeDtypeStruct((sources, part, width), bf16)]
    if last:
        out_shape += [jax.ShapeDtypeStruct((width, width), bf16)] * 2
    else:
        out_shape += [jax.ShapeDtypeStruct((steps, width, 2 * LANES), f32)]
    return pl.pallas_call(
        functools.partial(cross_backward_kernel, pair, last),
        out_shape=out_shape,
        grid_spec=pltpu.PrefetchScalarGridSpec(
            num_scalar_prefetch=1,
            grid=(steps,),
            in_specs=[target, source, source, target, target, held, weight(1), weight(0)]
            + [sums, pl.BlockSpec(memory_space=pl.ANY)][: len(before)],
            out_specs=[target, given] + ([weight(0)] * 2 if last else [sums]),
            scratch_shapes=[pltpu.VMEM((width, rows), bf16), pltpu.VMEM((rows, width), f32)],
        ),
        input_output_aliases={10: 0} if pair else {},
        cost_estimate=cost(
            flops=rows * width * (length * 10 + width * 8),
            transcendentals=HEADS * length * rows,
            bytes_accessed=length * width * 10 + rows * width * 8,
        ),
        name="cross_backward",
    )(lens, query, key, value, total, grad, memory, query_key, value_out, *before)


class Cube:
    def __init__(self, narrow, wide):
        self.narrow, self.wide = narrow, wide
        self.size = narrow * wide
        self.bits = self.size.bit_length() - 1
        self.index = lax.axis_index(BOTH)

    def swap(self, value, mask):
        pairs = [(i, i ^ mask) for i in range(self.size)]
        return lax.ppermute(value, BOTH, pairs)

    def total(self, value, bits):
        for bit in bits:
            value = value + self.swap(value, 1 << bit)
        return value


def merge_four(cube, pieces, split):
    r, n = pieces[0].shape

    def kernel(place_ref, *refs):
        ins, (left_ref, right_ref) = refs[:4], refs[4:]
        for m, ref in enumerate(ins):
            at = place_ref[0] ^ m
            left_ref[at] = ref[:, :split]
            right_ref[at] = ref[:, split:]

    return pl.pallas_call(
        kernel,
        out_shape=(
            jax.ShapeDtypeStruct((4, r, split), bf16),
            jax.ShapeDtypeStruct((4, r, n - split), bf16),
        ),
        grid_spec=pltpu.PrefetchScalarGridSpec(
            num_scalar_prefetch=1,
            grid=(1,),
            in_specs=[pl.BlockSpec((r, n), lambda i, s: (0, 0))] * 4,
            out_specs=[
                pl.BlockSpec((4, r, split), lambda i, s: (0, 0, 0)),
                pl.BlockSpec((4, r, n - split), lambda i, s: (0, 0, 0)),
            ],
        ),
        cost_estimate=cost(flops=0, transcendentals=0, bytes_accessed=16 * r * n),
        name="merge_four",
    )(((cube.index >> 1) & 3).reshape(1), *pieces)


def merge_two(side, mine, come, chunks):
    a, rows, n = mine.shape
    piece = pl.BlockSpec((1, rows, n // chunks), lambda i, c, s: (i, 0, c))

    def kernel(side_ref, mine_ref, come_ref, out_ref):
        out_ref[0, side_ref[0]] = mine_ref[0]
        out_ref[0, 1 - side_ref[0]] = come_ref[0]

    return pl.pallas_call(
        kernel,
        out_shape=jax.ShapeDtypeStruct((a, 2, rows, n), bf16),
        grid_spec=pltpu.PrefetchScalarGridSpec(
            num_scalar_prefetch=1,
            grid=(a, chunks),
            in_specs=[piece, piece],
            out_specs=pl.BlockSpec((1, 2, rows, n // chunks), lambda i, c, s: (i, 0, 0, c)),
        ),
        cost_estimate=cost(
            flops=0, transcendentals=0, bytes_accessed=8 * a * rows * n
        ),
        name="merge_two",
    )(side.reshape(1), mine, come)


class Gather:
    def __init__(self, cube, shard, split):
        self.cube = cube
        pieces = [shard] + [cube.swap(shard, m << 1) for m in (1, 2, 3)]
        self.start = merge_four(cube, pieces, split)

    def half(self, filler):
        cube = self.cube
        one, two = self.start
        r = one.shape[1]
        come_one, come_two = cube.swap(one, 1), cube.swap(two.reshape(1, 4 * r, -1), 16)
        come_one, come_two, filler = tie(come_one, come_two, filler)
        one = merge_two(self.side(0), one, come_one, 1)
        two = merge_two(self.side(4), two.reshape(1, 4 * r, -1), come_two, 1)
        return one.reshape(1, 8 * r, -1), two.reshape(8, r, -1), filler

    def side(self, bit):
        return (self.cube.index >> bit) & 1

    def most(self, one, two):
        cube = self.cube
        r = two.shape[1]
        one = merge_two(self.side(4), one, cube.swap(one, 16), 2 - one.shape[2] // LANES % 2)
        two = merge_two(self.side(0), two, cube.swap(two, 1), 1)
        return [one.reshape(2, 8 * r, -1), two.reshape(2, 8 * r, -1)]

    def finish(self, values):
        core = self.side(3)
        chunks = lambda value: 2 - value.shape[2] // LANES % 2
        return [
            merge_two(core, value, self.cube.swap(value, 8), chunks(value)).reshape(
                -1, value.shape[2]
            )
            for value in values
        ]


class Scatter:
    def __init__(self, cube, grads):
        self.cube = cube
        self.shapes = [(grad.shape[0] // cube.size, grad.shape[1]) for grad in grads]
        self.own = self.shapes[0][0]
        self.flat = [i for i, (r, _) in enumerate(self.shapes) if r == self.own]
        self.tall = [i for i, (r, _) in enumerate(self.shapes) if r != self.own]
        self.grads = [
            grad.reshape(2, 2, cube.wide * r, n)
            for grad, (r, n) in zip(grads, self.shapes, strict=True)
        ]
        self.sides = jnp.stack([cube.index >> 4, (cube.index >> 3) & 1, cube.index & 1])
        self.groups = [(self.own, sum(self.shapes[i][1] for i in self.flat))]
        self.groups += [self.shapes[i] for i in self.tall]

    def message(self, come, own, places, lead=1, packed=0):
        wide = self.cube.wide
        split = 2
        n_grads, n_groups = len(self.grads), len(self.groups)
        n_ins = n_grads + len(come)
        widths = [n for _, n in self.groups]
        stack = [-(-r // self.own) for r, _ in self.groups]

        def kernel(sides_ref, *refs):
            ins, outs = refs[:n_ins], refs[n_ins:]
            flat = [ins[i][0, 0] for i in self.flat]
            values = [flat[0] if len(flat) == 1 else jnp.concatenate(flat, axis=1)]
            values += [ins[i][0, 0] for i in self.tall]
            for k, ref in enumerate(ins[n_grads:]):
                got = ref[...]
                got = got.reshape(got.shape[-2:])
                i = k % n_groups
                values[i] = values[i].astype(f32) + got.astype(f32)
            if not packed:
                for out_ref, value in zip(outs, values, strict=True):
                    out_ref[...] = value.astype(bf16).reshape(out_ref.shape)
                return
            at = 0
            for value, (r, n), high in zip(values, self.groups, stack, strict=True):
                value = value.astype(f32).reshape(wide // split, r, n)
                for c in range(high):
                    part = value[:, c * self.own : (c + 1) * self.own].astype(bf16)
                    if packed == 1:
                        outs[0][:, : part.shape[1], at : at + n] = part
                    else:
                        side = sides_ref[2]
                        for i in range(0, part.shape[0], 2):
                            for flip, out_ref in enumerate(outs):
                                out_ref[i // 2, : part.shape[1], at : at + n] = jnp.where(
                                    side == flip, part[i], part[i + 1]
                                )
                    at += n

        in_specs = [
            pl.BlockSpec((1, 1, wide * r // split, n), lambda i, j, s: (*own(i, s), j, 0))
            for r, n in self.shapes
        ]
        for k, value in enumerate(come):
            at = places[k // n_groups]
            r, n = self.groups[k % n_groups]
            in_specs.append(
                pl.BlockSpec(
                    (1,) * (value.ndim - 2) + (wide * r // split, n),
                    lambda i, j, s, at=at: (*at(s), j, 0),
                )
            )
        if packed:
            n = sum(w * high for w, high in zip(widths, stack, strict=True))
            high = wide // packed
            out_shape = [jax.ShapeDtypeStruct((high, self.own, n), bf16)] * packed
            out_specs = [
                pl.BlockSpec((high // split, self.own, n), lambda i, j, s: (j, 0, 0))
            ] * packed
        else:
            out_shape = [jax.ShapeDtypeStruct((lead, wide * r, n), bf16) for r, n in self.groups]
            out_specs = [
                pl.BlockSpec((1, wide * r // split, n), lambda i, j, s: (i, j, 0))
                for r, n in self.groups
            ]
        size = sum(int(np.prod(out.shape)) for out in out_shape)
        return pl.pallas_call(
            kernel,
            out_shape=out_shape,
            grid_spec=pltpu.PrefetchScalarGridSpec(
                num_scalar_prefetch=1,
                grid=(lead, split),
                in_specs=in_specs,
                out_specs=out_specs,
            ),
            cost_estimate=cost(
                flops=size, transcendentals=0, bytes_accessed=4 * size
            ),
            name="message",
        )(self.sides, *self.grads, *come)

    def swap(self, values, mask):
        return [self.cube.swap(value, mask) for value in values]

    def to_core(self):
        return self.message([], lambda i, s: (i, 1 - s[1]), [], lead=2)

    def to_x(self, one):
        return self.message(one, lambda i, s: (1 - s[0], s[1]), [lambda s: (1 - s[0],)])

    def to_wide(self, one, two, halved=False):
        places = [lambda s: (s[0],), lambda s: (0,)]
        return self.message(
            [*one, *two], lambda i, s: (s[0], s[1]), places, packed=1 + halved
        )

    def step(self, bit, mine, come):
        blocks, r, n = mine.shape

        def kernel(side_ref, *refs):
            keep_ref, send_ref = refs[-2:]
            side = side_ref[0]
            for i in range(blocks // 2):
                for out_ref, at in ((keep_ref, 2 * i + side), (send_ref, 2 * i + 1 - side)):
                    value = refs[0][at].astype(f32) + refs[1][at].astype(f32)
                    out_ref[i] = value.astype(bf16)

        whole = pl.BlockSpec(mine.shape, lambda i, s: (0, 0, 0))
        half = pl.BlockSpec((blocks // 2, r, n), lambda i, s: (0, 0, 0))
        return pl.pallas_call(
            kernel,
            out_shape=[jax.ShapeDtypeStruct((blocks // 2, r, n), bf16)] * 2,
            grid_spec=pltpu.PrefetchScalarGridSpec(
                num_scalar_prefetch=1,
                grid=(1,),
                in_specs=[whole, whole],
                out_specs=[half, half],
            ),
            cost_estimate=cost(
                flops=mine.size, transcendentals=0, bytes_accessed=6 * mine.size
            ),
            name="step",
        )(((self.cube.index >> bit) & 1).reshape(1), mine, come)

    def finish(self, *come):
        def kernel(*refs):
            ins, outs = refs[: len(come)], refs[len(come) :]
            blocks = [ref[i] for ref in ins for i in range(ref.shape[0])]
            value = blocks[0].astype(f32)
            for block in blocks[1:]:
                value = value + block.astype(f32)
            at = 0
            for i in self.flat:
                n = self.shapes[i][1]
                outs[i][...] = value[:, at : at + n]
                at += n
            for i in self.tall:
                r, n = self.shapes[i]
                for c in range(0, r, self.own):
                    high = min(self.own, r - c)
                    outs[i][c : c + high] = value[:high, at : at + n]
                    at += n

        size = sum(value.size for value in come)
        return pl.pallas_call(
            kernel,
            out_shape=tuple(jax.ShapeDtypeStruct(shape, f32) for shape in self.shapes),
            cost_estimate=cost(
                flops=size, transcendentals=0, bytes_accessed=4 * size
            ),
            name="finish",
        )(*come)


def tie(*values):
    return lax.optimization_barrier(values)


def pack_shards(parts, widths, rows):
    flat = [part for group in parts for part in group]

    def kernel(*refs):
        ins, outs = refs[: len(flat)], refs[len(flat) :]
        refs_of = iter(ins)
        for out_ref, group in zip(outs, parts, strict=True):
            at = 0
            for array, start, count in group:
                ref, n = next(refs_of), array.shape[1]
                out_ref[:count, at : at + n] = ref[start : start + count, :]
                if count < rows:
                    out_ref[count:, at : at + n] = jnp.zeros((rows - count, n), bf16)
                at += n

    return pl.pallas_call(
        kernel,
        out_shape=tuple(jax.ShapeDtypeStruct((rows, n), bf16) for n in widths),
        name="pack",
    )(*[part[0] for part in flat])


def rms_norm(value, gain):
    return value * lax.rsqrt(jnp.mean(value * value, axis=-1, keepdims=True) + epsilon) * gain


def gelu_tanh(value):
    return jax.nn.gelu(value, approximate=True)


def on_device(
    targets,
    memory,
    cotangent,
    target_len,
    memory_len,
    self_query,
    self_key,
    self_value,
    self_out,
    cross_query,
    cross_key,
    cross_value,
    cross_out,
    ff_gate,
    ff_up,
    ff_down,
    self_gain,
    cross_gain,
    ff_gain,
    position_bias,
    narrow,
    wide,
):
    cube = Cube(narrow, wide)
    pairs, length, width = targets.shape
    slots = pairs * length
    own, own_ff = self_query.shape[0], ff_down.shape[0]
    inner = ff_gate.shape[1]
    devices = cube.size
    stepped = narrow == 4 and wide == 8 and own % 8 == 0

    gains = jnp.stack([self_gain, cross_gain, ff_gain], axis=1)
    gains = jnp.pad(gains, ((0, 0), (0, LANES - 3)))
    stack = -(-own_ff // own)
    whole = lambda *arrays: [(array, 0, own) for array in arrays]
    self_shard, cross_shard, ff_shard = pack_shards(
        [
            whole(self_query, self_key, self_value, self_out, gains),
            whole(cross_query, cross_key, cross_value, cross_out),
            whole(ff_gate, ff_up)
            + [(ff_down, c * own, min(own, own_ff - c * own)) for c in range(stack)],
        ],
        [4 * width + LANES, 4 * width, 2 * inner + stack * width],
        own,
    )
    places = jnp.arange(length)
    apart = places[:, None] - places[None, :]
    bucket = bucket_of_distance(length, BUCKETS, REACH)
    starts = [int(np.argmax(bucket >= b)) for b in range(1, int(bucket[-1]) + 1)]
    bucket_matrix = sum((apart >= start).astype(jnp.int32) for start in starts)
    onehot = (bucket_matrix[:, :, None] == jnp.arange(BUCKETS)[None, None, :]).astype(bf16)
    bias = jnp.einsum("ijb,bh->hij", onehot, position_bias, preferred_element_type=f32)
    bias = jnp.where((apart >= 0)[None], bias, negative).astype(bf16)

    exchange = lambda value: lax.all_to_all(
        value, "wide", split_axis=0, concat_axis=0, tiled=True
    )
    gathered = lax.all_gather(self_shard, BOTH, axis=0, tiled=True)
    ff = lax.all_gather(ff_shard, BOTH, axis=0, tiled=True)
    if stepped:
        cross_gather = Gather(cube, cross_shard, 2 * width)
        one, two, bias = cross_gather.half(bias)
        most = cross_gather.most(one, two)
        memory, most[0] = tie(memory, most[0])
        gathered, *most = tie(gathered, *most)
        c_query_key, c_value_out = cross_gather.finish(most)
    else:
        cross = lax.all_gather(cross_shard, BOTH, axis=0, tiled=True)
        c_query_key, c_value_out = cross[:, : 2 * width], cross[:, 2 * width :]
    memory_rows = exchange(memory).reshape(wide, pairs, -1, width)
    w_qkv, s_out = gathered[:, : 3 * width], gathered[:, 3 * width : 4 * width]
    c_query, c_out = c_query_key[:, :width], c_value_out[:, width:]

    gains = gathered[:, 4 * width : 4 * width + 3].astype(f32).T
    gain_one, gain_two, gain_three = gains[0], gains[1], gains[2]
    f_gate_up = ff[:, : 2 * inner]
    f_down = jnp.concatenate(
        [
            ff[:, 2 * inner + c * width : 2 * inner + (c + 1) * width].reshape(devices, own, width)
            for c in range(stack)
        ],
        axis=1,
    )[:, :own_ff].reshape(inner, width)

    live = (places[None, :] < target_len[:, None]).astype(f32).reshape(slots, 1)
    inputs = targets.astype(f32).reshape(slots, width)

    normed_one = rms_norm(inputs, gain_one).astype(bf16)
    cube_of = lambda value: value.reshape(pairs, length, -1)
    qkv_one = cube_of(dot(normed_one, w_qkv, NN).astype(bf16))
    mixed_one, total_one = self_forward(qkv_one, bias)
    mixed_one = mixed_one.reshape(slots, width)
    first = inputs + dot(mixed_one, s_out, NN)
    normed_two = rms_norm(first, gain_two).astype(bf16)
    query_two = cube_of(dot(normed_two, c_query, NN).astype(bf16))
    held = ()
    for p in range(pairs):
        held = cross_forward(
            p, query_two, memory_rows, c_query_key, c_value_out, memory_len, held
        )
    mixed_two, total_two, key_two, value_two = held
    mixed_two = mixed_two.reshape(slots, width)
    second = first + dot(mixed_two, c_out, NN)
    normed_three = rms_norm(second, gain_three).astype(bf16)
    gate = dot(normed_three, f_gate_up[:, :inner], NN)
    upward = dot(normed_three, f_gate_up[:, inner:], NN)
    activated, gelu_pull = jax.vjp(gelu_tanh, gate)
    hidden = (activated * upward).astype(bf16)
    third = second + dot(hidden, f_down, NN)
    layer_out = (third * live).astype(bf16).reshape(pairs, length, width)

    grad_third = cotangent.astype(f32).reshape(slots, width) * live
    branch_ff = grad_third.astype(bf16)
    d_down = dot(hidden, branch_ff, TN).astype(bf16)
    grad_hidden = dot(branch_ff, f_down, NT)
    grad_gate = gelu_pull(grad_hidden * upward)[0].astype(bf16)
    grad_up = (grad_hidden * activated).astype(bf16)
    d_gate = dot(normed_three, grad_gate, TN).astype(bf16)
    d_up = dot(normed_three, grad_up, TN).astype(bf16)
    grad_normed_three = dot(grad_gate, f_gate_up[:, :inner], NT) + dot(
        grad_up, f_gate_up[:, inner:], NT
    )
    d_down = d_down.reshape(devices, own_ff, width)
    d_down = jnp.pad(d_down, ((0, 0), (0, stack * own - own_ff), (0, 0)))
    d_down = [
        d_down[:, c * own : (c + 1) * own].reshape(devices * own, width) for c in range(stack)
    ]
    ff_grads = lax.psum_scatter(
        jnp.concatenate([d_gate, d_up] + d_down, axis=1),
        BOTH,
        scatter_dimension=0,
        tiled=True,
    )
    _, norm_three = jax.vjp(rms_norm, second, gain_three)
    back_three, d_gain_three = norm_three(grad_normed_three)
    grad_second = grad_third + back_three

    branch_cross = grad_second.astype(bf16)
    d_cross_out = dot(mixed_two, branch_cross, TN).astype(bf16)
    grad_mixed_two = cube_of(dot(branch_cross, c_out, NT).astype(bf16))
    held, grad_memory = (), []
    for p in range(pairs):
        grad_query_two, rows_grad, *sums = cross_backward(
            p,
            query_two,
            key_two,
            value_two,
            memory_len,
            total_two,
            grad_mixed_two,
            memory_rows,
            c_query_key,
            c_value_out,
            held,
        )
        held = (*sums, grad_query_two)
        if p < pairs - 1:
            grad_memory.append(exchange(rows_grad))
    d_cross_key, d_cross_value = sums
    if stepped:
        grad_query_two, *grad_memory = tie(grad_query_two, *grad_memory)
    grad_memory.append(exchange(rows_grad))
    grad_query_two = grad_query_two.reshape(slots, width)
    d_cross_query = dot(normed_two, grad_query_two, TN).astype(bf16)
    _, norm_two = jax.vjp(rms_norm, first, gain_two)
    back_two, d_gain_two = norm_two(dot(grad_query_two, c_query, NT))
    grad_first = grad_second + back_two

    branch_self = grad_first.astype(bf16)
    d_self_out = dot(mixed_one, branch_self, TN).astype(bf16)
    grad_mixed_one = cube_of(dot(branch_self, s_out, NT).astype(bf16))
    middle = [d_cross_query, d_cross_key, d_cross_value, d_cross_out, d_self_out]
    if stepped:
        middle_sum = Scatter(cube, middle)
        middle_one = middle_sum.swap(middle_sum.to_core(), 8)
        middle_send = middle_sum.to_x(middle_one)
        grad_mixed_one, *middle_send = tie(grad_mixed_one, *middle_send)
        middle_two = middle_sum.swap(middle_send, 16)
    grads_one, diagonals = self_backward(qkv_one, bias, total_one, grad_mixed_one)
    grads_one = grads_one.reshape(slots, 3 * width)
    if stepped:
        grads_one, diagonals, *middle_two = tie(grads_one, diagonals, *middle_two)
        middle_keep, middle_send = middle_sum.to_wide(middle_one, middle_two, halved=True)
        grads_one, middle_send = tie(grads_one, middle_send)
        middle_come = cube.swap(middle_send, 1)
    d_qkv = dot(normed_one, grads_one, TN).astype(bf16)
    if stepped:
        last_sum = Scatter(cube, [d_qkv])
        last_send = last_sum.to_core()
        grads_one, *last_send = tie(grads_one, *last_send)
        last_one = last_sum.swap(last_send, 8)
    grad_normed_one = dot(grads_one, w_qkv, NT)
    _, norm_one = jax.vjp(rms_norm, inputs, gain_one)
    back_one, d_gain_one = norm_one(grad_normed_one)
    if stepped:
        last_one[0], d_gain_one = tie(last_one[0], d_gain_one)
        last_send = last_sum.to_x(last_one)
        middle_come, grad_memory[-1], *last_send = tie(
            middle_come, grad_memory[-1], *last_send
        )
        last_two = last_sum.swap(last_send, 16)
        middle_keep, middle_send = middle_sum.step(1, middle_keep, middle_come)
        middle_come = cube.swap(middle_send, 2)
    grad_targets = (grad_first + back_one).reshape(pairs, length, width)

    padded = diagonals.shape[-1]
    column = (padded - np.arange(length)) % padded
    to_bucket = np.zeros((padded, BUCKETS), np.float32)
    to_bucket[column, bucket] = 1.0
    diagonals = jnp.sum(diagonals, axis=2).reshape(HEADS, padded)
    d_position = jnp.einsum(
        "hc,cb->bh", diagonals, jnp.asarray(to_bucket), precision=lax.Precision.HIGHEST
    )
    small = jnp.concatenate(
        [d_gain_one, d_gain_two, d_gain_three, d_position.reshape(-1)]
    ).reshape(-1, LANES)
    small = jnp.pad(small, ((0, -small.shape[0] % 8), (0, 0)))
    far = [b for b in range(cube.bits) if 0 < b < wide.bit_length() - 1]
    near = [b for b in range(cube.bits) if b not in far]
    small = cube.total(small, far)
    if stepped:
        middle_keep, middle_send = middle_sum.step(2, middle_keep, middle_come)
        last_two[0], middle_send = tie(last_two[0], middle_send)
        middle_come = cube.swap(middle_send, 4)
        (last_send,) = last_sum.to_wide(last_one, last_two)
        last_send, small, middle_come, ff_grads = tie(last_send, small, middle_come, ff_grads)
        last_three = exchange(last_send)
        middle_grads = middle_sum.finish(middle_keep, middle_come)
        (d_qkv,) = last_sum.finish(last_three)
    else:
        scatter = lambda value: lax.psum_scatter(
            value, BOTH, scatter_dimension=0, tiled=True
        ).astype(f32)
        middle_grads = [scatter(value) for value in middle]
        d_qkv = scatter(d_qkv)
    small = cube.total(small, near).reshape(-1)
    gain_grads = small[: 3 * width].reshape(3, devices, width // devices)
    gain_grads = lax.dynamic_index_in_dim(gain_grads, cube.index, 1, keepdims=False)
    grad_position = small[3 * width : 3 * width + BUCKETS * HEADS].reshape(BUCKETS, HEADS)

    ff_grads = ff_grads.astype(f32)
    d_down = jnp.concatenate(
        [ff_grads[:, 2 * inner + c * width : 2 * inner + (c + 1) * width] for c in range(stack)],
        axis=0,
    )[:own_ff]
    return (
        layer_out,
        grad_targets,
        jnp.stack(grad_memory, axis=1).reshape(memory.shape).astype(f32),
        d_qkv[:, :width],
        d_qkv[:, width : 2 * width],
        d_qkv[:, 2 * width :],
        middle_grads[4],
        *middle_grads[:4],
        ff_grads[:, :inner],
        ff_grads[:, inner : 2 * inner],
        d_down,
        gain_grads[0],
        gain_grads[1],
        gain_grads[2],
        grad_position,
    )


def solution(mesh):
    rows = P(BOTH, None)
    slots = P(BOTH, None, None)
    one = P(BOTH)
    source = P("narrow", "wide", None)
    in_specs = (slots, source, slots, one, one) + (rows,) * 11 + (one,) * 3 + (P(),)
    out_specs = (slots, slots, source) + (rows,) * 11 + (one,) * 3 + (P(),)
    narrow, wide = mesh.shape["narrow"], mesh.shape["wide"]

    def body(*args):
        return on_device(*args, narrow=narrow, wide=wide)

    return jax.shard_map(body, mesh=mesh, in_specs=in_specs, out_specs=out_specs, check_vma=False)
```

time: 575 us -> 524 us (0.911)
  Pallas kernels: 91.6 us -> 195 us
  waiting for transfers between devices: 230 us -> 132 us
  local copies, waits for them, and re-layouts: 59.8 us -> 25.6 us
  matrix products: 102 us -> 83.2 us
  other arithmetic: 30.4 us -> 21.6 us
  starting transfers between devices: 38.9 us -> 45.3 us
    pallas_call x2 -> x22, Pallas kernels: 54.2 us -> 158 us  [the longest x2 63.9 us: cross_backward(): pl.pallas_call(functools.partial(cross_backward_kernel, pair, last), out_...]
    all_to_all x2 -> x4, waiting for transfers between devices: 85 us -> 29 us  [on_device(): lax.all_to_all(value, 'wide', split_axis=0, concat_axis=0, tiled=True)]
    all_gather x1, waiting for transfers between devices: 21.5 us -> 0.01 us  [on_device(): gathered = lax.all_gather(self_shard, BOTH, axis=0, tiled=True)]
    dot_general x24 -> x21, matrix products: 99.2 us -> 80.1 us  [dot(): return lax.dot_general(left, right, dims, preferred_element_type=f32)]
    ppermute x25 -> x21, waiting for transfers between devices: 103 us -> 87.4 us  [swap(): return lax.ppermute(value, BOTH, pairs)]
    convert_element_type x2 -> x1, local copies, waits for them, and re-layouts: 12.2 us -> 3.31 us  [on_device(): jnp.stack(grad_memory, axis=1).reshape(memory.shape).astype(f32)]
    all_to_all x2 -> x4, starting transfers between devices: 11.1 us -> 19.7 us  [on_device(): lax.all_to_all(value, 'wide', split_axis=0, concat_axis=0, tiled=True)]
    convert_element_type x17 -> x2, other arithmetic: 10.1 us -> 2.56 us  [the longest x1 2.29 us: on_device(): jnp.stack(grad_memory, axis=1).reshape(memory.shape).astype(f32)]
  transfers between devices with their start and end apart: 30 -> 28, of which waited for: 17 -> 16; matrix products, arithmetic and copies ran while one was open for 22% -> 16% of each run, Pallas kernels for 6% -> 37%
where the time goes in v2:
time: 524 us; the launch traced here: 517 us
  Pallas kernels  195 us (37%)
  waiting for transfers between devices  132 us (25%)
  matrix products  83.2 us (16%)
  starting transfers between devices  45.3 us (9%)
  local copies, waits for them, and re-layouts  25.6 us (5%)
  other arithmetic  21.6 us (4%)
  between operations  14.5 us (3%)
    ppermute x21, waiting for transfers between devices, swap(): return lax.ppermute(value, BOTH, pairs)  87.4 us
    dot_general x21, matrix products, dot(): return lax.dot_general(left, right, dims, preferred_element_type=f32)  80.1 us
    pallas_call x2, Pallas kernels, cross_backward(): pl.pallas_call(functools.partial(cross_backward_kernel, pair, last), out_...  63.9 us
    pallas_call x2, Pallas kernels, cross_forward(): pl.pallas_call(functools.partial(cross_forward_kernel, pair), out_shape=(...  38.1 us
    all_to_all x4, waiting for transfers between devices, on_device(): lax.all_to_all(value, 'wide', split_axis=0, concat_axis=0, tiled=True)  29 us
    ppermute x21, starting transfers between devices, swap(): return lax.ppermute(value, BOTH, pairs)  25.4 us
    pallas_call x6, Pallas kernels, message(): pl.pallas_call(kernel, out_shape=out_shape, grid_spec=pltpu.PrefetchScala...  23.9 us
    pallas_call x1, Pallas kernels, self_backward(): pl.pallas_call(self_backward_kernel, out_shape=(jax.ShapeDtypeStruct(qkv....  22.2 us
  transfers between devices with their start and end apart: 28, of which 16 were waited for; matrix products, arithmetic and copies ran while one was open for 16% of the time, Pallas kernels for 37%

profile of v2, /device:TPU:0, one launch (start us, length us, event | category | flops | bytes accessed | tf_op | source)
XLA Modules:
  0.0 517.4 jit_solution(1890152463008774873)
XLA Ops:
  21.0 9.1 %collective-permute-done.1.refs_2_ = bf16[24,3072]{1,0:T(8,128)(2,1)} collective-permute-done((bf16[24,3072]{1,0:T(8,128)(2,1)}, bf16[24,3072]{1,0:T(8,128)(2,1)}, u32[]{:S(2)}, u32[]{:S(2)}) %collective-permute-start.1) | collective-permute-done | bytes 147488 | tf_op jit(solution)/shard_map/ppermute | solution.py:359
  45.6 13.2 %collective-permute-done.5.come_ref = bf16[1,192,1536]{2,1,0:T(8,128)(2,1)S(1)} collective-permute-done((bf16[1,192,1536]{2,1,0:T(8,128)(2,1)}, bf16[1,192,1536]{2,1,0:T(8,128)(2,1)S(1)}, u32[]{:S(2)}, u32[]{:S(2)}) %collective-permute-start.5) | collective-permute-done | bytes 589856 | tf_op jit(solution)/shard_map/ppermute | solution.py:359
  61.6 6.0 %all-to-all-start = ((bf16[16,128,768]{2,1,0:T(8,128)(2,1)}), bf16[16,128,768]{2,1,0:T(8,128)(2,1)S(1)}, u32[]{:S(2)}, u32[]{:S(2)}) async-start(bf16[16,128,768]{2,1,0:T(8,128)(2,1)} %param.22), calls=%async_computation | async-start | bytes 6291456 | tf_op jit(solution)/shard_map/all_to_all | solution.py:715
  75.7 33.6 %collective-permute-done.6.come_ref = bf16[8,24,1536]{2,1,0:T(8,128)(2,1)} collective-permute-done((bf16[8,24,1536]{2,1,0:T(8,128)(2,1)}, bf16[8,24,1536]{2,1,0:T(8,128)(2,1)}, u32[]{:S(2)}, u32[]{:S(2)}) %collective-permute-start.6) | collective-permute-done | bytes 589856 | tf_op jit(solution)/shard_map/ppermute | solution.py:359
  109.3 5.3 %merge_two.9 = bf16[8,2,24,1536]{3,2,1,0:T(8,128)(2,1)} custom-call(s32[1]{0:T(128)} %bitcast.5.side_ref, bf16[8,24,1536]{2,1,0:T(8,128)(2,1)} %bitcast.165, bf16[8,24,1536]{2,1,0:T(8,128)(2,1)} %collective-permute-done.6.come_ref), custom_call_target="tpu_custom_call" | custom-call | bytes 294912 | tf_op jit(solution)/shard_map/merge_two/pallas_call | solution.py:405
  117.0 6.0 %convolution_convert_fusion.1 = bf16[576,2304]{1,0:T(8,128)(2,1)} fusion(bf16[576,768]{1,0:T(8,128)(2,1)S(1)} %multiply_convert_fusion.6, bf16[768,3200]{1,0:T(8,128)(2,1)} %all-gather.3.cloned.1.call-done), kind=kOutput, calls=%fused_computation.17 | convolution fusion | flops 2039758848 | bytes 7077888 | tf_op jit(solution)/shard_map/dot_general | solution.py:38
  123.0 14.8 %self_forward.1 = (bf16[2,288,768]{2,1,0:T(8,128)(2,1)}, f32[2,288,768]{2,1,0:T(8,128)}) custom-call(bf16[2,288,2304]{2,1,0:T(8,128)(2,1)} %bitcast.100, bf16[2,288,2304]{2,1,0:T(8,128)(2,1)} %bitcast.101, bf16[2,288,2304]{2,1,0:T(8,128)(2,1)} %bitcast.102, bf16[12,288,288]{2,1,0:T(8,128)(2,1)} %fusion.23.bias_ref), custom_call_target="tpu_custom_call" | custom-call | flops 63700992 | bytes 663552 | tf_op jit(solution)/shard_map/self_forward/pallas_call | solution.py:76
  137.8 4.0 multiply_reduce_fusion.7
  141.8 4.0 merge_two.10
  145.7 4.0 merge_two.11
  155.0 19.0 %cross_forward.2 = (bf16[2,288,768]{2,1,0:T(8,128)(2,1)}, f32[2,288,768]{2,1,0:T(8,128)}, bf16[2,1024,768]{2,1,0:T(8,128)(2,1)}, bf16[2,1024,768]{2,1,0:T(8,128)(2,1)}) custom-call(s32[2]{0:T(128)} %len_ref.7, bf16[2,288,768]{2,1,0:T(8,128)(2,1)} %bitcast.125, bf16[8,2,128,768]{3,2,1,0:T(8,128)(2,1)} %bitcast.106, bf16[768,1536]{1,0:T(8,128)(2,1)} %bitcast.117, ...), custom_call_target="tpu_custom_call" | custom-call | flops 415236096 | bytes 811008 | tf_op jit(solution)/shard_map/cross_forward/pallas_call | solution.py:216
  174.0 19.1 %cross_forward.3 = (bf16[2,288,768]{2,1,0:T(8,128)(2,1)}, f32[2,288,768]{2,1,0:T(8,128)}, bf16[2,1024,768]{2,1,0:T(8,128)(2,1)}, bf16[2,1024,768]{2,1,0:T(8,128)(2,1)}) custom-call(s32[2]{0:T(128)} %len_ref.7, bf16[2,288,768]{2,1,0:T(8,128)(2,1)} %bitcast.126, ...), custom_call_target="tpu_custom_call", output_to_operand_aliasing={{0}: (5, {}), {1}: (6, {}), {2}: (7, {}), {3}: (8, {})} | custom-call | flops 415236096 | bytes 811008 | tf_op jit(solution)/shard_map/cross_forward/pallas_call | solution.py:216
  197.3 14.6 %all-gather.5.cloned.1.call-done = bf16[768,6400]{1,0:T(8,128)(2,1)} async-done(((bf16[24,6400]{1,0:T(8,128)(2,1)}), bf16[768,6400]{1,0:T(8,128)(2,1)}) %all-gather.5.cloned.1.call-update) | async-done | bytes 9830416 | tf_op jit(solution)/shard_map/all_gather | solution.py:719
  220.3 6.1 %fusion.9 = (bf16[576,2048]{1,0:T(8,128)(2,1)S(1)}, bf16[576,2048]{1,0:T(8,128)(2,1)S(1)}, bf16[576,2048]{1,0:T(8,128)(2,1)S(1)}) fusion(f32[576,2048]{1,0:T(8,128)S(1)} %fusion.84, f32[576,2048]{1,0:T(8,128)S(1)} %fusion.17, bf16[576,768]{1,0:T(8,128)(2,1)S(1)} %multiply_convert_fusion.4, bf16[768,6400]{1,0:T(8,128)(2,1)S(1)} %bitcast.170), kind=kOutput, calls=%fused_computation.14 | convolution fusion | flops 1842610176 | bytes 20545536 | tf_op jit(solution)/shard_map/dot_general | solution.py:38
  226.3 4.1 fusion.11
  235.4 4.0 fusion.10
  251.5 31.8 %cross_backward.2 = (bf16[2,288,768]{2,1,0:T(8,128)(2,1)}, bf16[8,128,768]{2,1,0:T(8,128)(2,1)}, f32[6,768,256]{2,1,0:T(8,128)}) custom-call(s32[2]{0:T(128)} %len_ref.7, bf16[2,288,768]{2,1,0:T(8,128)(2,1)} %bitcast.127, bf16[2,1024,768]{2,1,0:T(8,128)(2,1)} %get-tuple-element.102.k_ref, bf16[2,1024,768]{2,1,0:T(8,128)(2,1)} %get-tuple-element.103.v_ref, ...), custom_call_target="tpu_custom_call" | custom-call | flops 887095296 | bytes 1062912 | tf_op jit(solution)/shard_map/cross_backward/pallas_call | solution.py:329
  283.2 4.3 all-to-all-start.1
  288.2 32.2 %cross_backward.3 = (bf16[2,288,768]{2,1,0:T(8,128)(2,1)}, bf16[8,128,768]{2,1,0:T(8,128)(2,1)}, bf16[768,768]{1,0:T(8,128)(2,1)}, bf16[768,768]{1,0:T(8,128)(2,1)}) custom-call(s32[2]{0:T(128)} %len_ref.7, bf16[2,288,768]{2,1,0:T(8,128)(2,1)} %bitcast.128, bf16[2,1024,768]{2,1,0:T(8,128)(2,1)} %get-tuple-element.102.k_ref, ...), custom_call_target="tpu_custom_call", output_to_operand_aliasing={{0}: (10, {})} | custom-call | flops 887095296 | bytes 1062912 | tf_op jit(solution)/shard_map/cross_backward/pallas_call | solution.py:329
  320.3 3.8 convolution_convert_fusion.6
  324.1 25.5 %all-to-all-done.1 = bf16[8,128,768]{2,1,0:T(8,128)(2,1)} async-done(((bf16[8,128,768]{2,1,0:T(8,128)(2,1)}), bf16[8,128,768]{2,1,0:T(8,128)(2,1)}, u32[]{:S(2)}, u32[]{:S(2)}) %all-to-all-start.1) | async-done | bytes 1572896 | tf_op jit(solution)/shard_map/all_to_all | solution.py:715
  359.0 4.9 message.6
  376.1 5.8 %all-to-all-start.2 = ((bf16[8,128,768]{2,1,0:T(8,128)(2,1)}), bf16[8,128,768]{2,1,0:T(8,128)(2,1)}, u32[]{:S(2)}, u32[]{:S(2)}) async-start(bf16[8,128,768]{2,1,0:T(8,128)(2,1)} %get-tuple-element.124), calls=%async_computation.2 | async-start | bytes 3145728 | tf_op jit(solution)/shard_map/all_to_all | solution.py:715
  382.0 22.2 %self_backward.1 = (bf16[2,288,2304]{2,1,0:T(8,128)(2,1)}, f32[6,2,8,384]{3,2,1,0:T(8,128)}) custom-call(bf16[2,288,2304]{2,1,0:T(8,128)(2,1)} %bitcast.103, bf16[2,288,2304]{2,1,0:T(8,128)(2,1)} %bitcast.104, bf16[2,288,2304]{2,1,0:T(8,128)(2,1)} %bitcast.105, bf16[12,288,288]{2,1,0:T(8,128)(2,1)} %fusion.23.bias_ref, ...), custom_call_target="tpu_custom_call" | custom-call | flops 159252480 | bytes 995328 | tf_op jit(solution)/shard_map/self_backward/pallas_call | solution.py:152
  404.2 7.3 %collective-permute-done.10.refs_6_ = bf16[1,192,3840]{2,1,0:T(8,128)(2,1)S(1)} collective-permute-done((bf16[1,192,3840]{2,1,0:T(8,128)(2,1)}, bf16[1,192,3840]{2,1,0:T(8,128)(2,1)S(1)}, u32[]{:S(2)}, u32[]{:S(2)}) %collective-permute-start.10) | collective-permute-done | bytes 1474592 | tf_op jit(solution)/shard_map/ppermute | solution.py:359
  412.6 4.3 message.8
  416.9 6.2 %convolution_convert_fusion = bf16[768,2304]{1,0:T(8,128)(2,1)} fusion(bf16[576,768]{1,0:T(8,128)(2,1)S(1)} %copy-done.23, bf16[576,2304]{1,0:T(8,128)(2,1)} %bitcast.181), kind=kOutput, calls=%fused_computation.7 | convolution fusion | flops 2040201216 | bytes 7077888 | tf_op jit(solution)/shard_map/dot_general | solution.py:38
  423.1 4.5 message.9
  430.7 7.0 %multiply_reduce_fusion.2 = (f32[768]{0:T(1024)}, f32[576]{0:T(1024)S(1)}, f32[576,768]{1,0:T(8,128)}) fusion(f32[576]{0:T(1024)S(1)} %rsqrt.33, bf16[2,288,768]{2,1,0:T(8,128)(2,1)S(1)} %copy-done.10, f32[768]{0:T(1024)S(1)} %get-tuple-element.192, bf16[576,2304]{1,0:T(8,128)(2,1)} %bitcast.182, bf16[768,3200]{1,0:T(8,128)(2,1)} %all-gather.3.cloned.1.call-done, ...), kind=kOutput, calls=%fused_computation.49 | convolution fusion | flops 2041969408 | bytes 9742848 | tf_op jit(solution)/shard_map/dot_general | solution.py:38
  442.0 5.5 %collective-permute-done.11.refs_1_ = bf16[4,24,3840]{2,1,0:T(8,128)(2,1)} collective-permute-done((bf16[4,24,3840]{2,1,0:T(8,128)(2,1)}, bf16[4,24,3840]{2,1,0:T(8,128)(2,1)}, u32[]{:S(2)}, u32[]{:S(2)}) %collective-permute-start.11) | collective-permute-done | bytes 737312 | tf_op jit(solution)/shard_map/ppermute | solution.py:359
  454.1 5.5 %multiply_convert_fusion.3 = bf16[576,768]{1,0:T(8,128)(2,1)} fusion(f32[576,768]{1,0:T(8,128)S(1)} %copy-done.7, bf16[576,2048]{1,0:T(8,128)(2,1)} %copy-done.35, bf16[2048,768]{1,0:T(8,128)(2,1)} %bitcast.163, f32[576]{0:T(1024)S(1)} %reshape.441), kind=kOutput, calls=%fused_computation.54 | convolution fusion | flops 1813266432 | bytes 8161536 | tf_op jit(solution)/shard_map/dot_general | solution.py:38
  473.5 6.4 %collective-permute-done.17.refs_1_ = bf16[1,24,3840]{2,1,0:T(8,128)(2,1)} collective-permute-done((bf16[1,24,3840]{2,1,0:T(8,128)(2,1)}, bf16[1,24,3840]{2,1,0:T(8,128)(2,1)}, u32[]{:S(2)}, u32[]{:S(2)}) %collective-permute-start.17) | collective-permute-done | bytes 184352 | tf_op jit(solution)/shard_map/ppermute | solution.py:359
  (206 shorter events, 159.2 us)
Async XLA Ops:
  7.2 107.4 %all-gather.3.cloned.1.call-start = ((), (), s32[]{:S(2)}) async-start(), calls=%async_computation.5 | async-start | bytes 5068800 | tf_op jit(solution)/shard_map/all_gather | solution.py:718
  10.8 201.2 %all-gather.5.cloned.1.call-start = ((), (), s32[]{:S(2)}) async-start(), calls=%async_computation.6 | async-start | bytes 10137600 | tf_op jit(solution)/shard_map/all_gather | solution.py:719
  11.5 9.5 %collective-permute-start = (bf16[24,3072]{1,0:T(8,128)(2,1)}, bf16[24,3072]{1,0:T(8,128)(2,1)}, u32[]{:S(2)}, u32[]{:S(2)}) collective-permute-start(bf16[24,3072]{1,0:T(8,128)(2,1)} %get-tuple-element.84.refs_0_), channel_id=1, source_target_pairs={{0,2},{1,3},{2,0},{3,1},{4,6},{5,7},{6,4},{7,5},{8,10},{9,11},{10,... | collective-permute-start | bytes 442376 | tf_op jit(solution)/shard_map/ppermute | solution.py:359
  14.6 15.5 %collective-permute-start.1 = (bf16[24,3072]{1,0:T(8,128)(2,1)}, bf16[24,3072]{1,0:T(8,128)(2,1)}, u32[]{:S(2)}, u32[]{:S(2)}) collective-permute-start(bf16[24,3072]{1,0:T(8,128)(2,1)} %get-tuple-element.84.refs_0_), channel_id=1, source_target_pairs={{0,4},{1,5},{2,6},{3,7},{4,0},{5,1},{6,2},{7,3},{8,12},{9,13},{10,... | collective-permute-start | bytes 442376 | tf_op jit(solution)/shard_map/ppermute | solution.py:359
  17.2 12.9 %collective-permute-start.2 = (bf16[24,3072]{1,0:T(8,128)(2,1)}, bf16[24,3072]{1,0:T(8,128)(2,1)}, u32[]{:S(2)}, u32[]{:S(2)}) collective-permute-start(bf16[24,3072]{1,0:T(8,128)(2,1)} %get-tuple-element.84.refs_0_), channel_id=1, source_target_pairs={{0,6},{1,7},{2,4},{3,5},{4,2},{5,3},{6,0},{7,1},{8,14},{9,15},{10,... | collective-permute-start | bytes 442376 | tf_op jit(solution)/shard_map/ppermute | solution.py:359
  32.1 7.0 %collective-permute-start.3 = (bf16[4,24,1536]{2,1,0:T(8,128)(2,1)}, bf16[4,24,1536]{2,1,0:T(8,128)(2,1)}, u32[]{:S(2)}, u32[]{:S(2)}) collective-permute-start(bf16[4,24,1536]{2,1,0:T(8,128)(2,1)} %get-tuple-element.85.mine_ref), channel_id=1, source_target_pairs={{0,1},{1,0},{2,3},{3,2},{4,5},{5,4},{6,7},{7,6},{8,9},{9,8},{10,11... | collective-permute-start | bytes 884744 | tf_op jit(solution)/shard_map/ppermute | solution.py:359
  33.7 7.0 %collective-permute-start.4 = (bf16[1,96,1536]{2,1,0:T(8,128)(2,1)}, bf16[1,96,1536]{2,1,0:T(8,128)(2,1)}, u32[]{:S(2)}, u32[]{:S(2)}) collective-permute-start(bf16[1,96,1536]{2,1,0:T(8,128)(2,1)} %bitcast.175), channel_id=1, source_target_pairs={{0,16},{1,17},{2,18},{3,19},{4,20},{5,21},{6,22},{7,23},{8,24},{9,... | collective-permute-start | bytes 884744 | tf_op jit(solution)/shard_map/ppermute | solution.py:359
  43.9 14.8 %collective-permute-start.5 = (bf16[1,192,1536]{2,1,0:T(8,128)(2,1)}, bf16[1,192,1536]{2,1,0:T(8,128)(2,1)S(1)}, u32[]{:S(2)}, u32[]{:S(2)}) collective-permute-start(bf16[1,192,1536]{2,1,0:T(8,128)(2,1)} %bitcast.166), channel_id=1, source_target_pairs={{0,16},{1,17},{2,18},{3,19},{4,20},{5,21},{6,22},{7,23},{8,24},{9,... | collective-permute-start | bytes 1769480 | tf_op jit(solution)/shard_map/ppermute | solution.py:359
  61.6 91.7 %all-to-all-start = ((bf16[16,128,768]{2,1,0:T(8,128)(2,1)}), bf16[16,128,768]{2,1,0:T(8,128)(2,1)S(1)}, u32[]{:S(2)}, u32[]{:S(2)}) async-start(bf16[16,128,768]{2,1,0:T(8,128)(2,1)} %param.22), calls=%async_computation | async-start | bytes 6291456 | tf_op jit(solution)/shard_map/all_to_all | solution.py:715
  67.6 412.3 %reduce-scatter.2.cloned.1.call-start = ((), (), s32[]{:S(2)}) async-start(), calls=%async_computation.7 | async-start | bytes 10137600 | tf_op jit(solution)/shard_map/reduce_scatter | solution.py:788
  71.2 38.1 %collective-permute-start.6 = (bf16[8,24,1536]{2,1,0:T(8,128)(2,1)}, bf16[8,24,1536]{2,1,0:T(8,128)(2,1)}, u32[]{:S(2)}, u32[]{:S(2)}) collective-permute-start(bf16[8,24,1536]{2,1,0:T(8,128)(2,1)} %bitcast.164), channel_id=1, source_target_pairs={{0,1},{1,0},{2,3},{3,2},{4,5},{5,4},{6,7},{7,6},{8,9},{9,8},{10,11... | collective-permute-start | bytes 1769480 | tf_op jit(solution)/shard_map/ppermute | solution.py:359
  73.2 357.4 %copy-start.32 = (f32[576]{0:T(1024)}, f32[576]{0:T(1024)S(1)}, u32[]{:S(2)}) copy-start(f32[576]{0:T(1024)S(1)} %rsqrt.33) | copy-start | bytes 6916
  114.6 27.2 %collective-permute-start.7 = (bf16[2,192,1536]{2,1,0:T(8,128)(2,1)}, bf16[2,192,1536]{2,1,0:T(8,128)(2,1)}, u32[]{:S(2)}, u32[]{:S(2)}) collective-permute-start(bf16[2,192,1536]{2,1,0:T(8,128)(2,1)} %bitcast.154), channel_id=1, source_target_pairs={{0,8},{1,9},{2,10},{3,11},{4,12},{5,13},{6,14},{7,15},{8,0},{9,1},... | collective-permute-start | bytes 3538952 | tf_op jit(solution)/shard_map/ppermute | solution.py:359
  114.6 31.1 %collective-permute-start.8 = (bf16[2,192,1536]{2,1,0:T(8,128)(2,1)}, bf16[2,192,1536]{2,1,0:T(8,128)(2,1)}, u32[]{:S(2)}, u32[]{:S(2)}) collective-permute-start(bf16[2,192,1536]{2,1,0:T(8,128)(2,1)} %bitcast.156), channel_id=1, source_target_pairs={{0,8},{1,9},{2,10},{3,11},{4,12},{5,13},{6,14},{7,15},{8,0},{9,1},... | collective-permute-start | bytes 3538952 | tf_op jit(solution)/shard_map/ppermute | solution.py:359
  116.6 314.0 %copy-start.30 = (f32[768]{0:T(1024)}, f32[768]{0:T(1024)S(1)}, u32[]{:S(2)}) copy-start(f32[768]{0:T(1024)S(1)} %get-tuple-element.192) | copy-start | bytes 9220
  283.2 66.4 %all-to-all-start.1 = ((bf16[8,128,768]{2,1,0:T(8,128)(2,1)}), bf16[8,128,768]{2,1,0:T(8,128)(2,1)}, u32[]{:S(2)}, u32[]{:S(2)}) async-start(bf16[8,128,768]{2,1,0:T(8,128)(2,1)} %get-tuple-element.108), calls=%async_computation.1 | async-start | bytes 3145728 | tf_op jit(solution)/shard_map/all_to_all | solution.py:715
  288.2 32.2 %copy-start.18 = (bf16[2,288,768]{2,1,0:T(8,128)(2,1)S(1)}, bf16[2,288,768]{2,1,0:T(8,128)(2,1)}, u32[]{:S(2)}) copy-start(bf16[2,288,768]{2,1,0:T(8,128)(2,1)} %get-tuple-element.100) | copy-start | bytes 2654212
  320.3 29.3 %copy-start.4 = (bf16[2,2,192,1536]{3,2,1,0:T(8,128)(2,1)S(1)}, bf16[2,2,192,1536]{3,2,1,0:T(8,128)(2,1)}, u32[]{:S(2)}) copy-start(bf16[2,2,192,1536]{3,2,1,0:T(8,128)(2,1)} %merge_two.10) | copy-start | bytes 7077892
  363.8 5.6 %collective-permute-start.9 = (bf16[2,192,3840]{2,1,0:T(8,128)(2,1)}, bf16[2,192,3840]{2,1,0:T(8,128)(2,1)S(1)}, u32[]{:S(2)}, u32[]{:S(2)}) collective-permute-start(bf16[2,192,3840]{2,1,0:T(8,128)(2,1)} %message.6), channel_id=1, source_target_pairs={{0,8},{1,9},{2,10},{3,11},{4,12},{5,13},{6,14},{7,15},{8,0},{9,1},... | collective-permute-start | bytes 8847368 | tf_op jit(solution)/shard_map/ppermute | solution.py:359
  374.7 36.7 %collective-permute-start.10 = (bf16[1,192,3840]{2,1,0:T(8,128)(2,1)}, bf16[1,192,3840]{2,1,0:T(8,128)(2,1)S(1)}, u32[]{:S(2)}, u32[]{:S(2)}) collective-permute-start(bf16[1,192,3840]{2,1,0:T(8,128)(2,1)} %message.7), channel_id=1, source_target_pairs={{0,16},{1,17},{2,18},{3,19},{4,20},{5,21},{6,22},{7,23},{8,24},{9,... | collective-permute-start | bytes 4423688 | tf_op jit(solution)/shard_map/ppermute | solution.py:359
  376.1 65.9 %all-to-all-start.2 = ((bf16[8,128,768]{2,1,0:T(8,128)(2,1)}), bf16[8,128,768]{2,1,0:T(8,128)(2,1)}, u32[]{:S(2)}, u32[]{:S(2)}) async-start(bf16[8,128,768]{2,1,0:T(8,128)(2,1)} %get-tuple-element.124), calls=%async_computation.2 | async-start | bytes 3145728 | tf_op jit(solution)/shard_map/all_to_all | solution.py:715
  427.5 10.1 %collective-permute-start.12 = (bf16[2,192,2304]{2,1,0:T(8,128)(2,1)}, bf16[2,192,2304]{2,1,0:T(8,128)(2,1)S(1)}, u32[]{:S(2)}, u32[]{:S(2)}) collective-permute-start(bf16[2,192,2304]{2,1,0:T(8,128)(2,1)} %message.9), channel_id=1, source_target_pairs={{0,8},{1,9},{2,10},{3,11},{4,12},{5,13},{6,14},{7,15},{8,0},{9,1},... | collective-permute-start | bytes 5308424 | tf_op jit(solution)/shard_map/ppermute | solution.py:359
  427.5 19.9 %collective-permute-start.11 = (bf16[4,24,3840]{2,1,0:T(8,128)(2,1)}, bf16[4,24,3840]{2,1,0:T(8,128)(2,1)}, u32[]{:S(2)}, u32[]{:S(2)}) collective-permute-start(bf16[4,24,3840]{2,1,0:T(8,128)(2,1)} %get-tuple-element.123), channel_id=1, source_target_pairs={{0,1},{1,0},{2,3},{3,2},{4,5},{5,4},{6,7},{7,6},{8,9},{9,8},{10,11... | collective-permute-start | bytes 2211848 | tf_op jit(solution)/shard_map/ppermute | solution.py:359
  447.5 21.7 %collective-permute-start.13 = (bf16[1,192,2304]{2,1,0:T(8,128)(2,1)}, bf16[1,192,2304]{2,1,0:T(8,128)(2,1)S(1)}, u32[]{:S(2)}, u32[]{:S(2)}) collective-permute-start(bf16[1,192,2304]{2,1,0:T(8,128)(2,1)} %message.10), channel_id=1, source_target_pairs={{0,16},{1,17},{2,18},{3,19},{4,20},{5,21},{6,22},{7,23},{8,24},{9,... | collective-permute-start | bytes 2654216 | tf_op jit(solution)/shard_map/ppermute | solution.py:359
  451.3 12.2 %collective-permute-start.14 = (bf16[2,24,3840]{2,1,0:T(8,128)(2,1)}, bf16[2,24,3840]{2,1,0:T(8,128)(2,1)}, u32[]{:S(2)}, u32[]{:S(2)}) collective-permute-start(bf16[2,24,3840]{2,1,0:T(8,128)(2,1)} %get-tuple-element.132), channel_id=1, source_target_pairs={{0,2},{1,3},{2,0},{3,1},{4,6},{5,7},{6,4},{7,5},{8,10},{9,11},{10,... | collective-permute-start | bytes 1105928 | tf_op jit(solution)/shard_map/ppermute | solution.py:359
  452.0 9.9 %collective-permute-start.15 = (f32[24,128]{1,0:T(8,128)S(1)}, f32[24,128]{1,0:T(8,128)S(1)}, u32[]{:S(2)}, u32[]{:S(2)}) collective-permute-start(f32[24,128]{1,0:T(8,128)S(1)} %pad.13), channel_id=1, source_target_pairs={{0,2},{1,3},{2,0},{3,1},{4,6},{5,7},{6,4},{7,5},{8,10},{9,11},{10,... | collective-permute-start | bytes 36872 | tf_op jit(solution)/shard_map/ppermute | solution.py:359
  461.9 7.9 %collective-permute-start.16 = (f32[24,128]{1,0:T(8,128)S(1)}, f32[24,128]{1,0:T(8,128)S(1)}, u32[]{:S(2)}, u32[]{:S(2)}) collective-permute-start(f32[24,128]{1,0:T(8,128)S(1)} %pad_add_fusion.1), channel_id=1, source_target_pairs={{0,4},{1,5},{2,6},{3,7},{4,0},{5,1},{6,2},{7,3},{8,12},{9,13},{10,... | collective-permute-start | bytes 36872 | tf_op jit(solution)/shard_map/ppermute | solution.py:359
  469.2 10.7 %collective-permute-start.17 = (bf16[1,24,3840]{2,1,0:T(8,128)(2,1)}, bf16[1,24,3840]{2,1,0:T(8,128)(2,1)}, u32[]{:S(2)}, u32[]{:S(2)}) collective-permute-start(bf16[1,24,3840]{2,1,0:T(8,128)(2,1)} %get-tuple-element.137), channel_id=1, source_target_pairs={{0,4},{1,5},{2,6},{3,7},{4,0},{5,1},{6,2},{7,3},{8,12},{9,13},{10,... | collective-permute-start | bytes 552968 | tf_op jit(solution)/shard_map/ppermute | solution.py:359
  479.9 26.2 %all-to-all-start.3 = ((bf16[8,24,2304]{2,1,0:T(8,128)(2,1)}), bf16[8,24,2304]{2,1,0:T(8,128)(2,1)S(1)}, u32[]{:S(2)}, u32[]{:S(2)}) async-start(bf16[8,24,2304]{2,1,0:T(8,128)(2,1)} %message.11), calls=%async_computation.4 | async-start | bytes 1769472 | tf_op jit(solution)/shard_map/all_to_all | solution.py:715
  492.3 3.8 collective-permute-start.18
  496.1 1.2 collective-permute-start.19
  497.3 3.9 collective-permute-start.20
  (35 other events, 202.1 us)
Sparse Core Ops, SparseCore 0:
  11.5 91.1 all-gather.2
  105.6 106.3 all-gather.4
  248.2 183.5 reduce-scatter.1

commit v3 on v2

--- a/solution.py
+++ b/solution.py
@@ -49,23 +49,43 @@
     return np.where(apart < exact, apart, far).astype(np.int32)
 
 
-def of_head(h, first, value):
-    return jnp.where(first if h == 0 else ~first, value, jnp.zeros_like(value))
+def stack_heads(value):
+    first = lax.broadcasted_iota(jnp.int32, value.shape, 1) < HEAD_DIM
+    zero = jnp.zeros_like(value)
+    return jnp.concatenate([jnp.where(first, value, zero), jnp.where(first, zero, value)], axis=0)
+
+
+def join_heads(value):
+    half = value.shape[0] // 2
+    first = lax.broadcasted_iota(jnp.int32, (half, value.shape[1]), 1) < HEAD_DIM
+    return jnp.where(first, value[:half], value[half:])
+
+
+def stack_columns(total):
+    return jnp.concatenate([total[:, :1], total[:, HEAD_DIM : HEAD_DIM + 1]], axis=0)
+
+
+def attend(scores, v, mixed_ref, total_ref):
+    top = jnp.max(scores, axis=1, keepdims=True)
+    grown = jnp.exp(scores - top)
+    total = jnp.sum(grown, axis=1, keepdims=True)
+    mixed = dot(grown.astype(bf16), v, NN) * (1.0 / total)
+    mixed_ref[0] = join_heads(mixed).astype(bf16)
+    total_ref[0] = join_heads(jnp.broadcast_to(top + jnp.log(total), mixed.shape))
+
+
+def attend_back(scores, total, grad, v):
+    probs = jnp.exp(scores - stack_columns(total))
+    grad_probs = dot(grad, v, NT)
+    inner = jnp.sum(probs * grad_probs, axis=1, keepdims=True)
+    return probs.astype(bf16), (probs * (grad_probs - inner)).astype(bf16)
 
 
 def self_forward_kernel(q_ref, k_ref, v_ref, bias_ref, mixed_ref, total_ref):
-    q, k, v = q_ref[0], k_ref[0], v_ref[0]
-    first = lax.broadcasted_iota(jnp.int32, q.shape, 1) < HEAD_DIM
-    mixed, totals = [], []
-    for h in range(2):
-        scores = dot(of_head(h, first, q), k, NT) + bias_ref[h].astype(f32)
-        top = jnp.max(scores, axis=1, keepdims=True)
-        grown = jnp.exp(scores - top)
-        total = jnp.sum(grown, axis=1, keepdims=True)
-        mixed.append(dot((grown * (1.0 / total)).astype(bf16), v, NN))
-        totals.append(top + jnp.log(total))
-    mixed_ref[0] = jnp.where(first, mixed[0], mixed[1]).astype(bf16)
-    total_ref[0] = jnp.where(first, totals[0], totals[1])
+    length = q_ref.shape[1]
+    bias = bias_ref[...].reshape(2 * length, length).astype(f32)
+    scores = dot(stack_heads(q_ref[0]), k_ref[0], NT) + bias
+    attend(scores, v_ref[0], mixed_ref, total_ref)
 
 
 def self_forward(qkv, bias):
@@ -101,33 +121,22 @@
 ):
     p, hp = pl.program_id(0), pl.program_id(1)
     steps = pl.num_programs(1)
-    q, k, v, grad, total = q_ref[0], k_ref[0], v_ref[0], grad_ref[0], total_ref[0]
-    length, padded = q.shape[0], sum_ref.shape[-1]
-    first = lax.broadcasted_iota(jnp.int32, q.shape, 1) < HEAD_DIM
+    length, padded = q_ref.shape[1], sum_ref.shape[-1]
+    q, grad, k = stack_heads(q_ref[0]), stack_heads(grad_ref[0]), k_ref[0]
 
     @pl.when(p == 0)
     def _():
         sum_ref[hp] = jnp.zeros(sum_ref.shape[1:], f32)
 
-    found = []
-    for h in range(2):
-        scores = dot(of_head(h, first, q), k, NT) + bias_ref[h].astype(f32)
-        probs = jnp.exp(scores - total[:, HEAD_DIM * h : HEAD_DIM * h + 1])
-        grad_probs = dot(of_head(h, first, grad), v, NT)
-        inner = jnp.sum(probs * grad_probs, axis=1, keepdims=True)
-        grad_scores = (probs * (grad_probs - inner)).astype(bf16)
-        sum_ref[hp, h, :, :length] += grad_scores.astype(f32)
-        found.append(
-            (
-                dot(grad_scores, k, NN),
-                dot(grad_scores, q, TN),
-                dot(probs.astype(bf16), grad, TN),
-            )
-        )
+    bias = bias_ref[...].reshape(2 * length, length).astype(f32)
+    scores = dot(q, k, NT) + bias
+    probs, grad_scores = attend_back(scores, total_ref[0], grad, v_ref[0])
+    sum_ref[hp, :, :, :length] += grad_scores.astype(f32).reshape(2, length, length)
+    found = join_heads(dot(grad_scores, k, NN)), dot(grad_scores, q, TN), dot(probs, grad, TN)
     for c in range(3):
-        grads_ref[0, :, pl.ds(pl.multiple_of((hp + c * steps) * LANES, LANES), LANES)] = (
-            jnp.where(first, found[0][c], found[1][c]).astype(bf16)
-        )
+        grads_ref[0, :, pl.ds(pl.multiple_of((hp + c * steps) * LANES, LANES), LANES)] = found[
+            c
+        ].astype(bf16)
 
     @pl.when(p == pl.num_programs(0) - 1)
     def _():
@@ -185,24 +194,13 @@
 
 def cross_forward_kernel(pair, len_ref, q_ref, memory_ref, wk_ref, wv_ref, *refs):
     mixed_ref, total_ref, k_ref, v_ref = refs[-4:]
-    q = q_ref[0]
     rows = k_ref.shape[1]
     memory = memory_ref[...].reshape(rows, -1)
     kv = dot(memory, jnp.concatenate([wk_ref[...], wv_ref[...]], axis=1), NN).astype(bf16)
     k, v = kv[:, :LANES], kv[:, LANES:]
     k_ref[0], v_ref[0] = k, v
-    first = lax.broadcasted_iota(jnp.int32, q.shape, 1) < HEAD_DIM
-    dead = dead_rows(len_ref[pair], rows)
-    mixed, totals = [], []
-    for h in range(2):
-        scores = dot(of_head(h, first, q), k, NT) + dead
-        top = jnp.max(scores, axis=1, keepdims=True)
-        grown = jnp.exp(scores - top)
-        total = jnp.sum(grown, axis=1, keepdims=True)
-        mixed.append(dot((grown * (1.0 / total)).astype(bf16), v, NN))
-        totals.append(top + jnp.log(total))
-    mixed_ref[0] = jnp.where(first, mixed[0], mixed[1]).astype(bf16)
-    total_ref[0] = jnp.where(first, totals[0], totals[1])
+    scores = dot(stack_heads(q_ref[0]), k, NT) + dead_rows(len_ref[pair], rows)
+    attend(scores, v, mixed_ref, total_ref)
 
 
 def cross_forward(pair, query, memory, query_key, value_out, lens, before):
@@ -244,67 +242,51 @@
 
 
 def cross_backward_kernel(
-    pair, last, len_ref, q_ref, k_ref, v_ref, total_ref, grad_ref, memory_ref, wk_ref, wv_ref, *refs
+    pair, last, len_ref, q_ref, k_ref, v_ref, total_ref, grad_ref, memory_ref, qk_ref, vo_ref, *refs
 ):
-    turned_ref, rows_ref = refs[-2:]
+    *refs, grads_ref, held_ref, weight_ref, sems = refs
     hp, steps = pl.program_id(0), pl.num_programs(0)
-    q, k, v, grad, total = q_ref[0], k_ref[0], v_ref[0], grad_ref[0], total_ref[0]
-    rows = k.shape[0]
-    first = lax.broadcasted_iota(jnp.int32, q.shape, 1) < HEAD_DIM
-    first_row = lax.broadcasted_iota(jnp.int32, k.shape, 1) < HEAD_DIM
-    dead = dead_rows(len_ref[pair], rows)
-    if pair:
-        before_ref, _, *refs = refs
+    rows, width = k_ref.shape[1], weight_ref.shape[0]
+    before = pair if last else 0
+    before_refs, refs = refs[:before], refs[pair + (pair > 0) :]
+    grad_query_ref, grad_memory_ref, *outs = refs
+
+    moves = [
+        (qk_ref.at[:, width:], weight_ref.at[:, :width]),
+        (vo_ref.at[:, :width], weight_ref.at[:, width:]),
+    ]
     if last:
-        grad_query_ref, grad_memory_ref, d_key_ref, d_value_ref = refs[:4]
-    else:
-        grad_query_ref, grad_memory_ref, sum_ref = refs[:3]
+        moves += [(memory_ref.at[:, p], held_ref.at[p]) for p in range(pair + 1)]
+        moves += [(ref, grads_ref.at[p]) for p, ref in enumerate(before_refs)]
+    copies = [pltpu.make_async_copy(*move, sems.at[i]) for i, move in enumerate(moves)]
 
     @pl.when(hp == 0)
     def _():
-        turned_ref[...] = memory_ref[...].reshape(rows, -1).T
-
-    found = []
-    for h in range(2):
-        scores = dot(of_head(h, first, q), k, NT) + dead
-        probs = jnp.exp(scores - total[:, HEAD_DIM * h : HEAD_DIM * h + 1])
-        grad_probs = dot(of_head(h, first, grad), v, NT)
-        inner = jnp.sum(probs * grad_probs, axis=1, keepdims=True)
-        grad_scores = (probs * (grad_probs - inner)).astype(bf16)
-        found.append(
-            (
-                dot(grad_scores, k, NN),
-                dot(grad_scores, q, TN),
-                dot(probs.astype(bf16), grad, TN),
-            )
-        )
-    grad_query_ref[0] = jnp.where(first, found[0][0], found[1][0]).astype(bf16)
-    grad_kv = jnp.concatenate(
-        [jnp.where(first_row, found[0][c], found[1][c]).astype(bf16) for c in (1, 2)], axis=1
-    )
-    weight = jnp.concatenate([wk_ref[...], wv_ref[...]], axis=1)
-    back = dot(grad_kv, weight, NT)
-
-    @pl.when(hp == 0)
-    def _():
-        rows_ref[...] = back
-
-    @pl.when(hp > 0)
-    def _():
-        rows_ref[...] += back
+        for copy in copies:
+            copy.start()
+
+    q, grad, k = stack_heads(q_ref[0]), stack_heads(grad_ref[0]), k_ref[0]
+    scores = dot(q, k, NT) + dead_rows(len_ref[pair], rows)
+    probs, grad_scores = attend_back(scores, total_ref[0], grad, v_ref[0])
+    grad_query_ref[0] = join_heads(dot(grad_scores, k, NN)).astype(bf16)
+    for c, value in enumerate((dot(grad_scores, q, TN), dot(probs, grad, TN))):
+        at = pl.ds(pl.multiple_of((hp + c * steps) * LANES, LANES), LANES)
+        grads_ref[before, :, at] = value.astype(bf16)
 
     @pl.when(hp == steps - 1)
     def _():
-        grad_memory_ref[...] = rows_ref[...].astype(bf16).reshape(grad_memory_ref.shape)
-
-    d_kv = dot(turned_ref[...], grad_kv, NN)
-    if pair:
-        d_kv = d_kv + before_ref[0]
-    if last:
-        d_key_ref[...] = d_kv[:, :LANES].astype(bf16)
-        d_value_ref[...] = d_kv[:, LANES:].astype(bf16)
-    else:
-        sum_ref[0] = d_kv
+        for copy in copies:
+            copy.wait()
+        back = dot(grads_ref[before], weight_ref[...], NT).astype(bf16)
+        grad_memory_ref[...] = back.reshape(grad_memory_ref.shape)
+        if last:
+            d_kv = sum(
+                dot(held_ref[p].reshape(rows, width), grads_ref[p], TN) for p in range(pair + 1)
+            )
+            outs[0][...] = d_kv[:, :width].astype(bf16)
+            outs[1][...] = d_kv[:, width:].astype(bf16)
+        else:
+            outs[0][...] = grads_ref[0]
 
 
 def cross_backward(
@@ -315,29 +297,35 @@
     rows = sources * part
     steps = width // LANES
     last = pair == pairs - 1
+    held = pairs if last else 1
     target = pl.BlockSpec((1, length, LANES), lambda h, n: (pair, 0, h))
     source = pl.BlockSpec((1, rows, LANES), lambda h, n: (pair, 0, h))
-    weight = lambda c: pl.BlockSpec((width, LANES), lambda h, n: (0, h + c * steps))
-    held = pl.BlockSpec((sources, 1, part, width), lambda h, n: (0, pair, 0, 0))
-    given = pl.BlockSpec((sources, part, width), lambda h, n: (0, 0, 0))
-    sums = pl.BlockSpec((1, width, 2 * LANES), lambda h, n: (h, 0, 0))
-    out_shape = [jax.ShapeDtypeStruct(query.shape, bf16), jax.ShapeDtypeStruct((sources, part, width), bf16)]
+    anywhere = pl.BlockSpec(memory_space=pl.ANY)
+    whole = lambda *shape: pl.BlockSpec(shape, lambda h, n: (0,) * len(shape))
+    out_shape = [
+        jax.ShapeDtypeStruct(query.shape, bf16),
+        jax.ShapeDtypeStruct((sources, part, width), bf16),
+    ]
     if last:
         out_shape += [jax.ShapeDtypeStruct((width, width), bf16)] * 2
     else:
-        out_shape += [jax.ShapeDtypeStruct((steps, width, 2 * LANES), f32)]
+        out_shape += [jax.ShapeDtypeStruct((rows, 2 * width), bf16)]
     return pl.pallas_call(
         functools.partial(cross_backward_kernel, pair, last),
         out_shape=out_shape,
         grid_spec=pltpu.PrefetchScalarGridSpec(
             num_scalar_prefetch=1,
             grid=(steps,),
-            in_specs=[target, source, source, target, target, held, weight(1), weight(0)]
-            + [sums, pl.BlockSpec(memory_space=pl.ANY)][: len(before)],
-            out_specs=[target, given] + ([weight(0)] * 2 if last else [sums]),
-            scratch_shapes=[pltpu.VMEM((width, rows), bf16), pltpu.VMEM((rows, width), f32)],
-        ),
-        input_output_aliases={10: 0} if pair else {},
+            in_specs=[target, source, source, target, target] + [anywhere] * (3 + len(before)),
+            out_specs=[target] + [whole(*out.shape) for out in out_shape[1:]],
+            scratch_shapes=[
+                pltpu.VMEM((held, rows, 2 * width), bf16),
+                pltpu.VMEM((held, sources, part, width), bf16),
+                pltpu.VMEM((width, 2 * width), bf16),
+                pltpu.SemaphoreType.DMA((2 + 2 * pairs,)),
+            ],
+        ),
+        input_output_aliases={8 + len(before): 0} if pair else {},
         cost_estimate=cost(
             flops=rows * width * (length * 10 + width * 8),
             transcendentals=HEADS * length * rows,
@@ -800,7 +788,7 @@
     grad_mixed_two = cube_of(dot(branch_cross, c_out, NT).astype(bf16))
     held, grad_memory = (), []
     for p in range(pairs):
-        grad_query_two, rows_grad, *sums = cross_backward(
+        grad_query_two, rows_grad, *found = cross_backward(
             p,
             query_two,
             key_two,
@@ -813,17 +801,17 @@
             c_value_out,
             held,
         )
-        held = (*sums, grad_query_two)
+        held = (*held[:-1], *found, grad_query_two)
         if p < pairs - 1:
             grad_memory.append(exchange(rows_grad))
-    d_cross_key, d_cross_value = sums
-    if stepped:
-        grad_query_two, *grad_memory = tie(grad_query_two, *grad_memory)
-    grad_memory.append(exchange(rows_grad))
+    d_cross_key, d_cross_value = found
     grad_query_two = grad_query_two.reshape(slots, width)
     d_cross_query = dot(normed_two, grad_query_two, TN).astype(bf16)
     _, norm_two = jax.vjp(rms_norm, first, gain_two)
     back_two, d_gain_two = norm_two(dot(grad_query_two, c_query, NT))
+    if stepped:
+        back_two, *grad_memory = tie(back_two, *grad_memory)
+    grad_memory.append(exchange(rows_grad))
     grad_first = grad_second + back_two
 
     branch_self = grad_first.astype(bf16)
@@ -838,29 +826,24 @@
         middle_two = middle_sum.swap(middle_send, 16)
     grads_one, diagonals = self_backward(qkv_one, bias, total_one, grad_mixed_one)
     grads_one = grads_one.reshape(slots, 3 * width)
-    if stepped:
-        grads_one, diagonals, *middle_two = tie(grads_one, diagonals, *middle_two)
-        middle_keep, middle_send = middle_sum.to_wide(middle_one, middle_two, halved=True)
-        grads_one, middle_send = tie(grads_one, middle_send)
-        middle_come = cube.swap(middle_send, 1)
     d_qkv = dot(normed_one, grads_one, TN).astype(bf16)
     if stepped:
         last_sum = Scatter(cube, [d_qkv])
         last_send = last_sum.to_core()
-        grads_one, *last_send = tie(grads_one, *last_send)
+        grads_one, diagonals, *tied = tie(grads_one, diagonals, *middle_two, *last_send)
+        middle_two, last_send = tied[: len(middle_two)], tied[len(middle_two) :]
         last_one = last_sum.swap(last_send, 8)
+        (middle_send,) = middle_sum.to_wide(middle_one, middle_two)
+        grads_one, middle_send = tie(grads_one, middle_send)
+        middle_three = exchange(middle_send)
     grad_normed_one = dot(grads_one, w_qkv, NT)
     _, norm_one = jax.vjp(rms_norm, inputs, gain_one)
     back_one, d_gain_one = norm_one(grad_normed_one)
     if stepped:
         last_one[0], d_gain_one = tie(last_one[0], d_gain_one)
         last_send = last_sum.to_x(last_one)
-        middle_come, grad_memory[-1], *last_send = tie(
-            middle_come, grad_memory[-1], *last_send
-        )
+        grad_memory[-1], *last_send = tie(grad_memory[-1], *last_send)
         last_two = last_sum.swap(last_send, 16)
-        middle_keep, middle_send = middle_sum.step(1, middle_keep, middle_come)
-        middle_come = cube.swap(middle_send, 2)
     grad_targets = (grad_first + back_one).reshape(pairs, length, width)
 
     padded = diagonals.shape[-1]
@@ -879,13 +862,11 @@
     near = [b for b in range(cube.bits) if b not in far]
     small = cube.total(small, far)
     if stepped:
-        middle_keep, middle_send = middle_sum.step(2, middle_keep, middle_come)
-        last_two[0], middle_send = tie(last_two[0], middle_send)
-        middle_come = cube.swap(middle_send, 4)
+        last_two[0], middle_three = tie(last_two[0], middle_three)
         (last_send,) = last_sum.to_wide(last_one, last_two)
-        last_send, small, middle_come, ff_grads = tie(last_send, small, middle_come, ff_grads)
+        last_send, ff_grads = tie(last_send, ff_grads)
         last_three = exchange(last_send)
-        middle_grads = middle_sum.finish(middle_keep, middle_come)
+        middle_grads = middle_sum.finish(middle_three)
         (d_qkv,) = last_sum.finish(last_three)
     else:
         scatter = lambda value: lax.psum_scatter(

time: 524 us -> 495 us (0.945)
  Pallas kernels: 195 us -> 165 us
    pallas_call x2, Pallas kernels: 63.9 us -> 44.1 us  [cross_backward(): pl.pallas_call(functools.partial(cross_backward_kernel, pair, last), out_...]
    ppermute x21 -> x18, waiting for transfers between devices: 87.4 us -> 77.1 us  [swap(): return lax.ppermute(value, BOTH, pairs)]
    all_gather x1, waiting for transfers between devices: 14.6 us -> 20 us  [on_device(): ff = lax.all_gather(ff_shard, BOTH, axis=0, tiled=True)]
    all_to_all x4 -> x5, starting transfers between devices: 19.7 us -> 24.6 us  [on_device(): lax.all_to_all(value, 'wide', split_axis=0, concat_axis=0, tiled=True)]
    all_to_all x4 -> x5, waiting for transfers between devices: 29 us -> 31.7 us  [on_device(): lax.all_to_all(value, 'wide', split_axis=0, concat_axis=0, tiled=True)]
    ppermute x21 -> x18, starting transfers between devices: 25.4 us -> 24.6 us  [swap(): return lax.ppermute(value, BOTH, pairs)]
    unnamed x81 -> x97, local copies, waits for them, and re-layouts: 13.8 us -> 13.6 us
  transfers between devices with their start and end apart: 28 -> 26, of which waited for: 16 -> 13; matrix products, arithmetic and copies ran while one was open for 16% -> 17% of each run, Pallas kernels for 37% -> 33%
where the time goes in v3:
time: 495 us; the launch traced here: 488 us
  Pallas kernels  165 us (33%)
  waiting for transfers between devices  129 us (26%)
  matrix products  81.3 us (16%)
  starting transfers between devices  49.5 us (10%)
  local copies, waits for them, and re-layouts  26 us (5%)
  other arithmetic  22.7 us (5%)
  between operations  14.6 us (3%)
    dot_general x21, matrix products, dot(): return lax.dot_general(left, right, dims, preferred_element_type=f32)  78.1 us
    ppermute x18, waiting for transfers between devices, swap(): return lax.ppermute(value, BOTH, pairs)  77.1 us
    pallas_call x2, Pallas kernels, cross_backward(): pl.pallas_call(functools.partial(cross_backward_kernel, pair, last), out_...  44.1 us
    pallas_call x2, Pallas kernels, cross_forward(): pl.pallas_call(functools.partial(cross_forward_kernel, pair), out_shape=(...  33.8 us
    all_to_all x5, waiting for transfers between devices, on_device(): lax.all_to_all(value, 'wide', split_axis=0, concat_axis=0, tiled=True)  31.7 us
    ppermute x18, starting transfers between devices, swap(): return lax.ppermute(value, BOTH, pairs)  24.6 us
    all_to_all x5, starting transfers between devices, on_device(): lax.all_to_all(value, 'wide', split_axis=0, concat_axis=0, tiled=True)  24.6 us
    pallas_call x6, Pallas kernels, message(): pl.pallas_call(kernel, out_shape=out_shape, grid_spec=pltpu.PrefetchScala...  23.7 us
  transfers between devices with their start and end apart: 26, of which 13 were waited for; matrix products, arithmetic and copies ran while one was open for 17% of the time, Pallas kernels for 33%

profile of v3, /device:TPU:0, one launch (start us, length us, event | category | flops | bytes accessed | tf_op | source)
XLA Modules:
  0.0 488.1 jit_solution(17284986843093824668)
XLA Ops:
  21.0 9.1 %collective-permute-done.1.refs_2_ = bf16[24,3072]{1,0:T(8,128)(2,1)} collective-permute-done((bf16[24,3072]{1,0:T(8,128)(2,1)}, bf16[24,3072]{1,0:T(8,128)(2,1)}, u32[]{:S(2)}, u32[]{:S(2)}) %collective-permute-start.1) | collective-permute-done | bytes 147488 | tf_op jit(solution)/shard_map/ppermute | solution.py:347
  45.6 13.2 %collective-permute-done.5.come_ref = bf16[1,192,1536]{2,1,0:T(8,128)(2,1)S(1)} collective-permute-done((bf16[1,192,1536]{2,1,0:T(8,128)(2,1)}, bf16[1,192,1536]{2,1,0:T(8,128)(2,1)S(1)}, u32[]{:S(2)}, u32[]{:S(2)}) %collective-permute-start.5) | collective-permute-done | bytes 589856 | tf_op jit(solution)/shard_map/ppermute | solution.py:347
  61.6 5.8 %all-to-all-start = ((bf16[16,128,768]{2,1,0:T(8,128)(2,1)}), bf16[16,128,768]{2,1,0:T(8,128)(2,1)S(1)}, u32[]{:S(2)}, u32[]{:S(2)}) async-start(bf16[16,128,768]{2,1,0:T(8,128)(2,1)} %param.22), calls=%async_computation | async-start | bytes 6291456 | tf_op jit(solution)/shard_map/all_to_all | solution.py:703
  76.1 33.2 %collective-permute-done.6.come_ref = bf16[8,24,1536]{2,1,0:T(8,128)(2,1)} collective-permute-done((bf16[8,24,1536]{2,1,0:T(8,128)(2,1)}, bf16[8,24,1536]{2,1,0:T(8,128)(2,1)}, u32[]{:S(2)}, u32[]{:S(2)}) %collective-permute-start.6) | collective-permute-done | bytes 589856 | tf_op jit(solution)/shard_map/ppermute | solution.py:347
  109.3 5.3 %merge_two.9 = bf16[8,2,24,1536]{3,2,1,0:T(8,128)(2,1)} custom-call(s32[1]{0:T(128)} %bitcast.5.side_ref, bf16[8,24,1536]{2,1,0:T(8,128)(2,1)} %bitcast.163, bf16[8,24,1536]{2,1,0:T(8,128)(2,1)} %collective-permute-done.6.come_ref), custom_call_target="tpu_custom_call" | custom-call | bytes 294912 | tf_op jit(solution)/shard_map/merge_two/pallas_call | solution.py:393
  116.8 5.8 %convolution_convert_fusion = bf16[576,2304]{1,0:T(8,128)(2,1)} fusion(bf16[768,3200]{1,0:T(8,128)(2,1)} %all-gather.3.cloned.1.call-done, f32[768]{0:T(1024)S(1)} %get-tuple-element.172, f32[576]{0:T(1024)S(1)} %rsqrt.36, bf16[576,768]{1,0:T(8,128)(2,1)S(1)} %bitcast.156), kind=kOutput, calls=%fused_computation.17 | convolution fusion | flops 2041528320 | bytes 7083264 | tf_op jit(solution)/shard_map/dot_general | solution.py:38
  122.6 11.8 %self_forward.1 = (bf16[2,288,768]{2,1,0:T(8,128)(2,1)}, f32[2,288,768]{2,1,0:T(8,128)}) custom-call(bf16[2,288,2304]{2,1,0:T(8,128)(2,1)} %bitcast.97, bf16[2,288,2304]{2,1,0:T(8,128)(2,1)} %bitcast.98, bf16[2,288,2304]{2,1,0:T(8,128)(2,1)} %bitcast.99, bf16[12,288,288]{2,1,0:T(8,128)(2,1)} %fusion.23.bias_ref), custom_call_target="tpu_custom_call" | custom-call | flops 63700992 | bytes 663552 | tf_op jit(solution)/shard_map/self_forward/pallas_call | solution.py:96
  138.3 4.0 merge_two.11
  142.3 3.9 merge_two.10
  153.8 16.9 %cross_forward.2 = (bf16[2,288,768]{2,1,0:T(8,128)(2,1)}, f32[2,288,768]{2,1,0:T(8,128)}, bf16[2,1024,768]{2,1,0:T(8,128)(2,1)}, bf16[2,1024,768]{2,1,0:T(8,128)(2,1)}) custom-call(s32[2]{0:T(128)} %len_ref.7, bf16[2,288,768]{2,1,0:T(8,128)(2,1)} %bitcast.122, bf16[8,2,128,768]{3,2,1,0:T(8,128)(2,1)} %bitcast.103, bf16[768,1536]{1,0:T(8,128)(2,1)} %bitcast.114, ...), custom_call_target="tpu_custom_call" | custom-call | flops 415236096 | bytes 811008 | tf_op jit(solution)/shard_map/cross_forward/pallas_call | solution.py:214
  170.8 16.9 %cross_forward.3 = (bf16[2,288,768]{2,1,0:T(8,128)(2,1)}, f32[2,288,768]{2,1,0:T(8,128)}, bf16[2,1024,768]{2,1,0:T(8,128)(2,1)}, bf16[2,1024,768]{2,1,0:T(8,128)(2,1)}) custom-call(s32[2]{0:T(128)} %len_ref.7, bf16[2,288,768]{2,1,0:T(8,128)(2,1)} %bitcast.123, ...), custom_call_target="tpu_custom_call", output_to_operand_aliasing={{0}: (5, {}), {1}: (6, {}), {2}: (7, {}), {3}: (8, {})} | custom-call | flops 415236096 | bytes 811008 | tf_op jit(solution)/shard_map/cross_forward/pallas_call | solution.py:214
  191.9 20.0 %all-gather.5.cloned.1.call-done = bf16[768,6400]{1,0:T(8,128)(2,1)} async-done(((bf16[24,6400]{1,0:T(8,128)(2,1)}), bf16[768,6400]{1,0:T(8,128)(2,1)}) %all-gather.5.cloned.1.call-update) | async-done | bytes 9830416 | tf_op jit(solution)/shard_map/all_gather | solution.py:707
  220.3 6.1 %fusion.9 = (bf16[576,2048]{1,0:T(8,128)(2,1)S(1)}, bf16[576,2048]{1,0:T(8,128)(2,1)S(1)}, bf16[576,2048]{1,0:T(8,128)(2,1)S(1)}) fusion(f32[576,2048]{1,0:T(8,128)S(1)} %fusion.90, f32[576,2048]{1,0:T(8,128)S(1)} %fusion.17, bf16[576,768]{1,0:T(8,128)(2,1)S(1)} %multiply_convert_fusion.5, bf16[768,6400]{1,0:T(8,128)(2,1)S(1)} %bitcast.168), kind=kOutput, calls=%fused_computation.14 | convolution fusion | flops 1842610176 | bytes 20545536 | tf_op jit(solution)/shard_map/dot_general | solution.py:38
  226.3 4.1 fusion.11
  240.3 4.1 fusion.10
  251.1 19.4 %cross_backward.2 = (bf16[2,288,768]{2,1,0:T(8,128)(2,1)}, bf16[8,128,768]{2,1,0:T(8,128)(2,1)}, bf16[1024,1536]{1,0:T(8,128)(2,1)}) custom-call(s32[2]{0:T(128)} %len_ref.7, bf16[2,288,768]{2,1,0:T(8,128)(2,1)} %bitcast.124, bf16[2,1024,768]{2,1,0:T(8,128)(2,1)} %get-tuple-element.92.k_ref, bf16[2,1024,768]{2,1,0:T(8,128)(2,1)} %get-tuple-element.93.v_ref, ...), custom_call_target="tpu_custom_call" | custom-call | flops 887095296 | bytes 1062912 | tf_op jit(solution)/shard_map/cross_backward/pallas_call | solution.py:313
  270.5 4.5 all-to-all-start.1
  275.6 24.6 %cross_backward.3 = (bf16[2,288,768]{2,1,0:T(8,128)(2,1)}, bf16[8,128,768]{2,1,0:T(8,128)(2,1)}, bf16[768,768]{1,0:T(8,128)(2,1)}, bf16[768,768]{1,0:T(8,128)(2,1)}) custom-call(s32[2]{0:T(128)} %len_ref.7, bf16[2,288,768]{2,1,0:T(8,128)(2,1)} %bitcast.125, bf16[2,1024,768]{2,1,0:T(8,128)(2,1)} %get-tuple-element.92.k_ref, ...), custom_call_target="tpu_custom_call", output_to_operand_aliasing={{0}: (10, {})} | custom-call | flops 887095296 | bytes 1062912 | tf_op jit(solution)/shard_map/cross_backward/pallas_call | solution.py:313
  308.7 22.6 %all-to-all-done.1 = bf16[8,128,768]{2,1,0:T(8,128)(2,1)} async-done(((bf16[8,128,768]{2,1,0:T(8,128)(2,1)}), bf16[8,128,768]{2,1,0:T(8,128)(2,1)}, u32[]{:S(2)}, u32[]{:S(2)}) %all-to-all-start.1) | async-done | bytes 1572896 | tf_op jit(solution)/shard_map/all_to_all | solution.py:703
  334.7 4.9 %message.6 = bf16[2,192,3840]{2,1,0:T(8,128)(2,1)} custom-call(s32[3]{0:T(128)} %pad_add_fusion.sides_ref, bf16[2,2,192,768]{3,2,1,0:T(8,128)(2,1)} %bitcast.135, bf16[2,2,192,768]{3,2,1,0:T(8,128)(2,1)} %bitcast.126, bf16[2,2,192,768]{3,2,1,0:T(8,128)(2,1)} %bitcast.129, bf16[2,2,192,768]{3,2,1,0:T(8,128)(2,1)} %bitcast.132, bf16[2,2,192,768]{3,2,1,0:T(8,128)(2,1)} %bitcast.138), custom_call_target="tpu_custom_call" | custom-call | flops 184320 | bytes 737280 | tf_op jit(solution)/shard_map/message/pallas_call | solution.py:526
  339.6 4.5 all-to-all-start.2
  354.7 22.6 %self_backward.1 = (bf16[2,288,2304]{2,1,0:T(8,128)(2,1)}, f32[6,2,8,384]{3,2,1,0:T(8,128)}) custom-call(bf16[2,288,2304]{2,1,0:T(8,128)(2,1)} %bitcast.100, bf16[2,288,2304]{2,1,0:T(8,128)(2,1)} %bitcast.101, bf16[2,288,2304]{2,1,0:T(8,128)(2,1)} %bitcast.102, bf16[12,288,288]{2,1,0:T(8,128)(2,1)} %fusion.23.bias_ref, ...), custom_call_target="tpu_custom_call" | custom-call | flops 159252480 | bytes 995328 | tf_op jit(solution)/shard_map/self_backward/pallas_call | solution.py:161
  377.3 6.3 %bitcast_convert_fusion = bf16[768,2304]{1,0:T(8,128)(2,1)} fusion(bf16[2,288,2304]{2,1,0:T(8,128)(2,1)} %get-tuple-element.104, f32[768]{0:T(1024)S(1)} %get-tuple-element.172, f32[2,288]{1,0:T(2,128)S(1)} %copy-done.40, bf16[2,288,768]{2,1,0:T(8,128)(2,1)S(1)} %copy-done.19), kind=kOutput, calls=%fused_computation.2 | convolution fusion | flops 2041970688 | bytes 7083264 | tf_op jit(solution)/shard_map/dot_general | solution.py:38
  383.6 4.4 message.8
  388.0 4.3 collective-permute-done.10.refs_6_
  393.4 4.1 message.9
  397.6 5.8 %all-to-all-start.3 = ((bf16[8,24,3840]{2,1,0:T(8,128)(2,1)}), bf16[8,24,3840]{2,1,0:T(8,128)(2,1)}, u32[]{:S(2)}, u32[]{:S(2)}) async-start(bf16[8,24,3840]{2,1,0:T(8,128)(2,1)} %message.9), calls=%async_computation.3 | async-start | bytes 2949120 | tf_op jit(solution)/shard_map/all_to_all | solution.py:703
  404.2 7.1 %multiply_reduce_fusion.2 = (f32[768]{0:T(1024)S(1)}, f32[576]{0:T(1024)}, f32[576,768]{1,0:T(8,128)}) fusion(f32[576]{0:T(1024)S(1)} %copy-done.36, bf16[2,288,768]{2,1,0:T(8,128)(2,1)S(1)} %copy-done.19, f32[768]{0:T(1024)S(1)} %get-tuple-element.172, bf16[576,2304]{1,0:T(8,128)(2,1)} %bitcast.179, bf16[768,3200]{1,0:T(8,128)(2,1)} %all-gather.3.cloned.1.call-done, ...), kind=kOutput, calls=%fused_computation.48 | convolution fusion | flops 2041969408 | bytes 9742848 | tf_op jit(solution)/shard_map/dot_general | solution.py:38
  418.8 12.9 %collective-permute-done.13 = f32[24,128]{1,0:T(8,128)} collective-permute-done((f32[24,128]{1,0:T(8,128)}, f32[24,128]{1,0:T(8,128)}, u32[]{:S(2)}, u32[]{:S(2)}) %collective-permute-start.13) | collective-permute-done | bytes 12320 | tf_op jit(solution)/shard_map/ppermute | solution.py:347
  435.6 5.5 %multiply_convert_fusion.4 = bf16[576,768]{1,0:T(8,128)(2,1)} fusion(f32[576,768]{1,0:T(8,128)S(1)} %copy-done.7, bf16[576,2048]{1,0:T(8,128)(2,1)} %copy-done.43, bf16[2048,768]{1,0:T(8,128)(2,1)} %bitcast.161, f32[576]{0:T(1024)} %copy-done.32), kind=kOutput, calls=%fused_computation.54 | convolution fusion | flops 1813266432 | bytes 8161536 | tf_op jit(solution)/shard_map/dot_general | solution.py:38
  449.9 4.0 all-to-all-start.4
  470.0 6.8 %all-to-all-done.4.refs_0_ = bf16[8,24,2304]{2,1,0:T(8,128)(2,1)S(1)} async-done(((bf16[8,24,2304]{2,1,0:T(8,128)(2,1)}), bf16[8,24,2304]{2,1,0:T(8,128)(2,1)S(1)}, u32[]{:S(2)}, u32[]{:S(2)}) %all-to-all-start.4) | async-done | bytes 884768 | tf_op jit(solution)/shard_map/all_to_all | solution.py:703
  (216 shorter events, 149.0 us)
Async XLA Ops:
  7.2 107.4 %all-gather.3.cloned.1.call-start = ((), (), s32[]{:S(2)}) async-start(), calls=%async_computation.6 | async-start | bytes 5068800 | tf_op jit(solution)/shard_map/all_gather | solution.py:706
  10.8 201.2 %all-gather.5.cloned.1.call-start = ((), (), s32[]{:S(2)}) async-start(), calls=%async_computation.7 | async-start | bytes 10137600 | tf_op jit(solution)/shard_map/all_gather | solution.py:707
  11.5 9.5 %collective-permute-start = (bf16[24,3072]{1,0:T(8,128)(2,1)}, bf16[24,3072]{1,0:T(8,128)(2,1)}, u32[]{:S(2)}, u32[]{:S(2)}) collective-permute-start(bf16[24,3072]{1,0:T(8,128)(2,1)} %get-tuple-element.74.refs_0_), channel_id=1, source_target_pairs={{0,2},{1,3},{2,0},{3,1},{4,6},{5,7},{6,4},{7,5},{8,10},{9,11},{10,... | collective-permute-start | bytes 442376 | tf_op jit(solution)/shard_map/ppermute | solution.py:347
  14.6 15.5 %collective-permute-start.1 = (bf16[24,3072]{1,0:T(8,128)(2,1)}, bf16[24,3072]{1,0:T(8,128)(2,1)}, u32[]{:S(2)}, u32[]{:S(2)}) collective-permute-start(bf16[24,3072]{1,0:T(8,128)(2,1)} %get-tuple-element.74.refs_0_), channel_id=1, source_target_pairs={{0,4},{1,5},{2,6},{3,7},{4,0},{5,1},{6,2},{7,3},{8,12},{9,13},{10,... | collective-permute-start | bytes 442376 | tf_op jit(solution)/shard_map/ppermute | solution.py:347
  17.2 12.9 %collective-permute-start.2 = (bf16[24,3072]{1,0:T(8,128)(2,1)}, bf16[24,3072]{1,0:T(8,128)(2,1)}, u32[]{:S(2)}, u32[]{:S(2)}) collective-permute-start(bf16[24,3072]{1,0:T(8,128)(2,1)} %get-tuple-element.74.refs_0_), channel_id=1, source_target_pairs={{0,6},{1,7},{2,4},{3,5},{4,2},{5,3},{6,0},{7,1},{8,14},{9,15},{10,... | collective-permute-start | bytes 442376 | tf_op jit(solution)/shard_map/ppermute | solution.py:347
  32.1 7.0 %collective-permute-start.3 = (bf16[4,24,1536]{2,1,0:T(8,128)(2,1)}, bf16[4,24,1536]{2,1,0:T(8,128)(2,1)}, u32[]{:S(2)}, u32[]{:S(2)}) collective-permute-start(bf16[4,24,1536]{2,1,0:T(8,128)(2,1)} %get-tuple-element.75.mine_ref), channel_id=1, source_target_pairs={{0,1},{1,0},{2,3},{3,2},{4,5},{5,4},{6,7},{7,6},{8,9},{9,8},{10,11... | collective-permute-start | bytes 884744 | tf_op jit(solution)/shard_map/ppermute | solution.py:347
  33.7 7.0 %collective-permute-start.4 = (bf16[1,96,1536]{2,1,0:T(8,128)(2,1)}, bf16[1,96,1536]{2,1,0:T(8,128)(2,1)}, u32[]{:S(2)}, u32[]{:S(2)}) collective-permute-start(bf16[1,96,1536]{2,1,0:T(8,128)(2,1)} %bitcast.173), channel_id=1, source_target_pairs={{0,16},{1,17},{2,18},{3,19},{4,20},{5,21},{6,22},{7,23},{8,24},{9,... | collective-permute-start | bytes 884744 | tf_op jit(solution)/shard_map/ppermute | solution.py:347
  43.9 14.8 %collective-permute-start.5 = (bf16[1,192,1536]{2,1,0:T(8,128)(2,1)}, bf16[1,192,1536]{2,1,0:T(8,128)(2,1)S(1)}, u32[]{:S(2)}, u32[]{:S(2)}) collective-permute-start(bf16[1,192,1536]{2,1,0:T(8,128)(2,1)} %bitcast.164), channel_id=1, source_target_pairs={{0,16},{1,17},{2,18},{3,19},{4,20},{5,21},{6,22},{7,23},{8,24},{9,... | collective-permute-start | bytes 1769480 | tf_op jit(solution)/shard_map/ppermute | solution.py:347
  61.6 90.5 %all-to-all-start = ((bf16[16,128,768]{2,1,0:T(8,128)(2,1)}), bf16[16,128,768]{2,1,0:T(8,128)(2,1)S(1)}, u32[]{:S(2)}, u32[]{:S(2)}) async-start(bf16[16,128,768]{2,1,0:T(8,128)(2,1)} %param.22), calls=%async_computation | async-start | bytes 6291456 | tf_op jit(solution)/shard_map/all_to_all | solution.py:703
  67.5 382.4 %reduce-scatter.2.cloned.1.call-start = ((), (), s32[]{:S(2)}) async-start(), calls=%async_computation.8 | async-start | bytes 10137600 | tf_op jit(solution)/shard_map/reduce_scatter | solution.py:776
  71.1 38.3 %collective-permute-start.6 = (bf16[8,24,1536]{2,1,0:T(8,128)(2,1)}, bf16[8,24,1536]{2,1,0:T(8,128)(2,1)}, u32[]{:S(2)}, u32[]{:S(2)}) collective-permute-start(bf16[8,24,1536]{2,1,0:T(8,128)(2,1)} %bitcast.162), channel_id=1, source_target_pairs={{0,1},{1,0},{2,3},{3,2},{4,5},{5,4},{6,7},{7,6},{8,9},{9,8},{10,11... | collective-permute-start | bytes 1769480 | tf_op jit(solution)/shard_map/ppermute | solution.py:347
  73.7 41.0 %copy-start.30 = (f32[576]{0:T(1024)}, f32[576]{0:T(1024)S(1)}, u32[]{:S(2)}) copy-start(f32[576]{0:T(1024)S(1)} %add.306) | copy-start | bytes 6916
  73.7 43.1 %copy-start.35 = (f32[576]{0:T(1024)}, f32[576]{0:T(1024)S(1)}, u32[]{:S(2)}) copy-start(f32[576]{0:T(1024)S(1)} %rsqrt.36) | copy-start | bytes 6916
  73.8 161.5 %copy-start.32 = (f32[576]{0:T(1024)}, f32[576]{0:T(1024)S(1)}, u32[]{:S(2)}) copy-start(f32[576]{0:T(1024)S(1)} %reshape.444) | copy-start | bytes 6916
  114.6 23.7 %collective-permute-start.8 = (bf16[2,192,1536]{2,1,0:T(8,128)(2,1)}, bf16[2,192,1536]{2,1,0:T(8,128)(2,1)}, u32[]{:S(2)}, u32[]{:S(2)}) collective-permute-start(bf16[2,192,1536]{2,1,0:T(8,128)(2,1)} %bitcast.151), channel_id=1, source_target_pairs={{0,8},{1,9},{2,10},{3,11},{4,12},{5,13},{6,14},{7,15},{8,0},{9,1},... | collective-permute-start | bytes 3538952 | tf_op jit(solution)/shard_map/ppermute | solution.py:347
  114.7 27.6 %collective-permute-start.7 = (bf16[2,192,1536]{2,1,0:T(8,128)(2,1)}, bf16[2,192,1536]{2,1,0:T(8,128)(2,1)}, u32[]{:S(2)}, u32[]{:S(2)}) collective-permute-start(bf16[2,192,1536]{2,1,0:T(8,128)(2,1)} %bitcast.149), channel_id=1, source_target_pairs={{0,8},{1,9},{2,10},{3,11},{4,12},{5,13},{6,14},{7,15},{8,0},{9,1},... | collective-permute-start | bytes 3538952 | tf_op jit(solution)/shard_map/ppermute | solution.py:347
  116.8 287.4 %copy-start.33 = (f32[768]{0:T(1024)}, f32[768]{0:T(1024)S(1)}, u32[]{:S(2)}) copy-start(f32[768]{0:T(1024)S(1)} %get-tuple-element.172) | copy-start | bytes 9220
  270.5 60.8 %all-to-all-start.1 = ((bf16[8,128,768]{2,1,0:T(8,128)(2,1)}), bf16[8,128,768]{2,1,0:T(8,128)(2,1)}, u32[]{:S(2)}, u32[]{:S(2)}) async-start(bf16[8,128,768]{2,1,0:T(8,128)(2,1)} %get-tuple-element.98), calls=%async_computation.1 | async-start | bytes 3145728 | tf_op jit(solution)/shard_map/all_to_all | solution.py:703
  275.6 24.6 %copy-start.4 = (bf16[2,2,192,1536]{3,2,1,0:T(8,128)(2,1)S(1)}, bf16[2,2,192,1536]{3,2,1,0:T(8,128)(2,1)}, u32[]{:S(2)}) copy-start(bf16[2,2,192,1536]{3,2,1,0:T(8,128)(2,1)} %merge_two.10) | copy-start | bytes 7077892
  308.4 23.0 %copy-start.12 = (f32[576,768]{1,0:T(8,128)S(1)}, f32[576,768]{1,0:T(8,128)}, u32[]{:S(2)}) copy-start(f32[576,768]{1,0:T(8,128)} %get-tuple-element.183) | copy-start | bytes 5308420
  339.6 8.1 %collective-permute-start.9 = (bf16[2,192,3840]{2,1,0:T(8,128)(2,1)}, bf16[2,192,3840]{2,1,0:T(8,128)(2,1)S(1)}, u32[]{:S(2)}, u32[]{:S(2)}) collective-permute-start(bf16[2,192,3840]{2,1,0:T(8,128)(2,1)} %message.6), channel_id=1, source_target_pairs={{0,8},{1,9},{2,10},{3,11},{4,12},{5,13},{6,14},{7,15},{8,0},{9,1},... | collective-permute-start | bytes 8847368 | tf_op jit(solution)/shard_map/ppermute | solution.py:347
  339.6 58.0 %all-to-all-start.2 = ((bf16[8,128,768]{2,1,0:T(8,128)(2,1)}), bf16[8,128,768]{2,1,0:T(8,128)(2,1)}, u32[]{:S(2)}, u32[]{:S(2)}) async-start(bf16[8,128,768]{2,1,0:T(8,128)(2,1)} %get-tuple-element.111), calls=%async_computation.2 | async-start | bytes 3145728 | tf_op jit(solution)/shard_map/all_to_all | solution.py:703
  353.1 39.2 %collective-permute-start.10 = (bf16[1,192,3840]{2,1,0:T(8,128)(2,1)}, bf16[1,192,3840]{2,1,0:T(8,128)(2,1)S(1)}, u32[]{:S(2)}, u32[]{:S(2)}) collective-permute-start(bf16[1,192,3840]{2,1,0:T(8,128)(2,1)} %message.7), channel_id=1, source_target_pairs={{0,16},{1,17},{2,18},{3,19},{4,20},{5,21},{6,22},{7,23},{8,24},{9,... | collective-permute-start | bytes 4423688 | tf_op jit(solution)/shard_map/ppermute | solution.py:347
  393.4 17.8 %collective-permute-start.11 = (bf16[2,192,2304]{2,1,0:T(8,128)(2,1)}, bf16[2,192,2304]{2,1,0:T(8,128)(2,1)S(1)}, u32[]{:S(2)}, u32[]{:S(2)}) collective-permute-start(bf16[2,192,2304]{2,1,0:T(8,128)(2,1)} %message.8), channel_id=1, source_target_pairs={{0,8},{1,9},{2,10},{3,11},{4,12},{5,13},{6,14},{7,15},{8,0},{9,1},... | collective-permute-start | bytes 5308424 | tf_op jit(solution)/shard_map/ppermute | solution.py:347
  397.6 47.9 %all-to-all-start.3 = ((bf16[8,24,3840]{2,1,0:T(8,128)(2,1)}), bf16[8,24,3840]{2,1,0:T(8,128)(2,1)}, u32[]{:S(2)}, u32[]{:S(2)}) async-start(bf16[8,24,3840]{2,1,0:T(8,128)(2,1)} %message.9), calls=%async_computation.3 | async-start | bytes 2949120 | tf_op jit(solution)/shard_map/all_to_all | solution.py:703
  411.9 19.7 %collective-permute-start.13 = (f32[24,128]{1,0:T(8,128)}, f32[24,128]{1,0:T(8,128)}, u32[]{:S(2)}, u32[]{:S(2)}) collective-permute-start(f32[24,128]{1,0:T(8,128)} %pad.14), channel_id=1, source_target_pairs={{0,2},{1,3},{2,0},{3,1},{4,6},{5,7},{6,4},{7,5},{8,10},{9,11},{10,... | collective-permute-start | bytes 36872 | tf_op jit(solution)/shard_map/ppermute | solution.py:347
  417.1 28.4 %collective-permute-start.12 = (bf16[1,192,2304]{2,1,0:T(8,128)(2,1)}, bf16[1,192,2304]{2,1,0:T(8,128)(2,1)S(1)}, u32[]{:S(2)}, u32[]{:S(2)}) collective-permute-start(bf16[1,192,2304]{2,1,0:T(8,128)(2,1)} %message.10), channel_id=1, source_target_pairs={{0,16},{1,17},{2,18},{3,19},{4,20},{5,21},{6,22},{7,23},{8,24},{9,... | collective-permute-start | bytes 2654216 | tf_op jit(solution)/shard_map/ppermute | solution.py:347
  432.4 9.4 %collective-permute-start.14 = (f32[24,128]{1,0:T(8,128)S(1)}, f32[24,128]{1,0:T(8,128)S(1)}, u32[]{:S(2)}, u32[]{:S(2)}) collective-permute-start(f32[24,128]{1,0:T(8,128)S(1)} %pad_add_fusion.1), channel_id=1, source_target_pairs={{0,4},{1,5},{2,6},{3,7},{4,0},{5,1},{6,2},{7,3},{8,12},{9,13},{10,... | collective-permute-start | bytes 36872 | tf_op jit(solution)/shard_map/ppermute | solution.py:347
  441.8 3.7 collective-permute-start.15
  445.5 11.6 %collective-permute-start.16 = (f32[24,128]{1,0:T(8,128)S(1)}, f32[24,128]{1,0:T(8,128)}, u32[]{:S(2)}, u32[]{:S(2)}) collective-permute-start(f32[24,128]{1,0:T(8,128)S(1)} %add.351), channel_id=1, source_target_pairs={{0,8},{1,9},{2,10},{3,11},{4,12},{5,13},{6,14},{7,15},{8,0},{9,1},... | collective-permute-start | bytes 36872 | tf_op jit(solution)/shard_map/ppermute | solution.py:347
  449.9 26.9 %all-to-all-start.4 = ((bf16[8,24,2304]{2,1,0:T(8,128)(2,1)}), bf16[8,24,2304]{2,1,0:T(8,128)(2,1)S(1)}, u32[]{:S(2)}, u32[]{:S(2)}) async-start(bf16[8,24,2304]{2,1,0:T(8,128)(2,1)} %message.11), calls=%async_computation.5 | async-start | bytes 1769472 | tf_op jit(solution)/shard_map/all_to_all | solution.py:703
  457.8 7.1 %collective-permute-start.17 = (f32[24,128]{1,0:T(8,128)S(1)}, f32[24,128]{1,0:T(8,128)S(1)}, u32[]{:S(2)}, u32[]{:S(2)}) collective-permute-start(f32[24,128]{1,0:T(8,128)S(1)} %add.352), channel_id=1, source_target_pairs={{0,16},{1,17},{2,18},{3,19},{4,20},{5,21},{6,22},{7,23},{8,24},{9,... | collective-permute-start | bytes 36872 | tf_op jit(solution)/shard_map/ppermute | solution.py:347
  (41 other events, 251.9 us)
Sparse Core Ops, SparseCore 0:
  11.5 91.1 all-gather.2
  105.6 106.2 all-gather.4
  247.9 164.7 reduce-scatter.1

commit v4 on v3

--- a/solution.py
+++ b/solution.py
@@ -248,7 +248,7 @@
     hp, steps = pl.program_id(0), pl.num_programs(0)
     rows, width = k_ref.shape[1], weight_ref.shape[0]
     before = pair if last else 0
-    before_refs, refs = refs[:before], refs[pair + (pair > 0) :]
+    before_refs, refs = refs[:before], refs[pair + 2 * (pair > 0) :]
     grad_query_ref, grad_memory_ref, *outs = refs
 
     moves = [
@@ -304,8 +304,9 @@
     whole = lambda *shape: pl.BlockSpec(shape, lambda h, n: (0,) * len(shape))
     out_shape = [
         jax.ShapeDtypeStruct(query.shape, bf16),
-        jax.ShapeDtypeStruct((sources, part, width), bf16),
+        jax.ShapeDtypeStruct(memory.shape, bf16),
     ]
+    given = pl.BlockSpec((sources, 1, part, width), lambda h, n: (0, pair, 0, 0))
     if last:
         out_shape += [jax.ShapeDtypeStruct((width, width), bf16)] * 2
     else:
@@ -317,7 +318,7 @@
             num_scalar_prefetch=1,
             grid=(steps,),
             in_specs=[target, source, source, target, target] + [anywhere] * (3 + len(before)),
-            out_specs=[target] + [whole(*out.shape) for out in out_shape[1:]],
+            out_specs=[target, given] + [whole(*out.shape) for out in out_shape[2:]],
             scratch_shapes=[
                 pltpu.VMEM((held, rows, 2 * width), bf16),
                 pltpu.VMEM((held, sources, part, width), bf16),
@@ -325,7 +326,7 @@
                 pltpu.SemaphoreType.DMA((2 + 2 * pairs,)),
             ],
         ),
-        input_output_aliases={8 + len(before): 0} if pair else {},
+        input_output_aliases={7 + len(before): 0, 8 + len(before): 1} if pair else {},
         cost_estimate=cost(
             flops=rows * width * (length * 10 + width * 8),
             transcendentals=HEADS * length * rows,
@@ -333,6 +334,187 @@
         ),
         name="cross_backward",
     )(lens, query, key, value, total, grad, memory, query_key, value_out, *before)
+
+
+HIDDEN = 512
+SLOPE = float(np.sqrt(2 / np.pi))
+CUBIC = 0.044715
+
+
+def feed_forward_kernel(
+    own,
+    second_ref,
+    gain_ref,
+    live_ref,
+    cotangent_ref,
+    down_ref,
+    gate_low_ref,
+    gate_high_ref,
+    up_low_ref,
+    up_high_ref,
+    out_ref,
+    grad_second_ref,
+    d_gain_ref,
+    grads_ref,
+    normed_ref,
+    turned_ref,
+    branch_ref,
+    third_ref,
+    back_ref,
+    d_gate_ref,
+    d_up_ref,
+    d_down_ref,
+    sems,
+):
+    k, steps = pl.program_id(0), pl.num_programs(0)
+    width = second_ref.shape[1]
+    rows, stacked = d_down_ref.shape[1:]
+    tall = HIDDEN // (rows // own)
+    slot = k % 2
+
+    def copies(step):
+        at = step % 2
+        gate = pl.multiple_of(stacked + step * HIDDEN, 256)
+        up = pl.multiple_of(stacked + (steps + step) * HIDDEN, 256)
+        first = pl.multiple_of(step * rows, 8)
+        return [
+            pltpu.make_async_copy(
+                d_gate_ref.at[at], grads_ref.at[:, pl.ds(gate, HIDDEN)], sems.at[at, 0]
+            ),
+            pltpu.make_async_copy(
+                d_up_ref.at[at], grads_ref.at[:, pl.ds(up, HIDDEN)], sems.at[at, 1]
+            ),
+            pltpu.make_async_copy(
+                d_down_ref.at[at],
+                grads_ref.at[pl.ds(first, rows), pl.ds(0, stacked)],
+                sems.at[at, 2],
+            ),
+        ]
+
+    @pl.when(k == 0)
+    def _():
+        second = second_ref[...]
+        scale = lax.rsqrt(jnp.mean(second * second, axis=1, keepdims=True) + epsilon)
+        normed = (second * scale * gain_ref[...]).astype(bf16)
+        normed_ref[...] = normed
+        turned_ref[...] = normed.T
+        branch_ref[...] = (cotangent_ref[...].astype(f32) * live_ref[...]).astype(bf16)
+        third_ref[...] = second
+        back_ref[...] = jnp.zeros(back_ref.shape, f32)
+
+    @pl.when(k >= 2)
+    def _():
+        for copy in copies(k - 2):
+            copy.wait()
+
+    packed = down_ref[...].astype(f32)
+    pieces = []
+    for i in range(rows // own):
+        for c in range(stacked // width):
+            high = min(own, tall - c * own)
+            pieces.append(packed[i * own : i * own + high, c * width : (c + 1) * width])
+    down = jnp.concatenate(pieces, axis=0).astype(bf16)
+    gate_weight = jnp.concatenate([gate_low_ref[...], gate_high_ref[...]], axis=1)
+    up_weight = jnp.concatenate([up_low_ref[...], up_high_ref[...]], axis=1)
+
+    normed, branch = normed_ref[...], branch_ref[...]
+    gate = dot(normed, gate_weight, NN)
+    up = dot(normed, up_weight, NN)
+    square = gate * gate
+    bent = jnp.tanh(SLOPE * gate * (1.0 + CUBIC * square))
+    half = 0.5 * (1.0 + bent)
+    active = gate * half
+    slope = half + 0.5 * gate * (1.0 - bent * bent) * (SLOPE * (1.0 + 3.0 * CUBIC * square))
+    hidden = (active * up).astype(bf16)
+    grad_hidden = dot(branch, down, NT)
+    grad_gate = (grad_hidden * up * slope).astype(bf16)
+    grad_up = (grad_hidden * active).astype(bf16)
+    third_ref[...] += dot(hidden, down, NN)
+    back_ref[...] += dot(grad_gate, gate_weight, NT) + dot(grad_up, up_weight, NT)
+    d_gate_ref[slot] = dot(turned_ref[...], grad_gate, NN).astype(bf16)
+    d_up_ref[slot] = dot(turned_ref[...], grad_up, NN).astype(bf16)
+    d_down = dot(hidden, branch, TN)
+    for i in range(rows // own):
+        for c in range(stacked // width):
+            high = min(own, tall - c * own)
+            part = d_down[i * tall + c * own : i * tall + c * own + high].astype(bf16)
+            at = i * own
+            d_down_ref[slot, at : at + high, c * width : (c + 1) * width] = part
+            if high < own:
+                d_down_ref[slot, at + high : at + own, c * width : (c + 1) * width] = jnp.zeros(
+                    (own - high, width), bf16
+                )
+    for copy in copies(k):
+        copy.start()
+
+    @pl.when(k == steps - 1)
+    def _():
+        second, back = second_ref[...], back_ref[...]
+        out_ref[...] = (third_ref[...] * live_ref[...]).astype(bf16)
+        scale = lax.rsqrt(jnp.mean(second * second, axis=1, keepdims=True) + epsilon)
+        d_gain_ref[...] = jnp.sum(back * second * scale, axis=0, keepdims=True)
+        back = back * gain_ref[...]
+        inner = jnp.mean(back * second, axis=1, keepdims=True)
+        back = scale * back - second * (scale * scale * scale * inner)
+        grad_second_ref[...] = cotangent_ref[...].astype(f32) * live_ref[...] + back
+        for step in (k - 1, k):
+            for copy in copies(step):
+                copy.wait()
+
+
+def feed_forward(second, gain, live, cotangent, weights, inner, own):
+    slots, width = second.shape
+    steps = inner // HIDDEN
+    stacked = weights.shape[1] - 2 * inner
+    rows = weights.shape[0] // steps
+    whole = lambda *shape: pl.BlockSpec(shape, lambda k: (0,) * len(shape))
+    unit = HIDDEN // 2
+    column = lambda first: pl.BlockSpec((width, unit), lambda k: (0, first + 2 * k))
+    at = stacked // unit
+    return pl.pallas_call(
+        functools.partial(feed_forward_kernel, own),
+        out_shape=(
+            jax.ShapeDtypeStruct((slots, width), bf16),
+            jax.ShapeDtypeStruct((slots, width), f32),
+            jax.ShapeDtypeStruct((1, width), f32),
+            jax.ShapeDtypeStruct(weights.shape, bf16),
+        ),
+        grid=(steps,),
+        in_specs=[
+            whole(slots, width),
+            whole(1, width),
+            whole(slots, 1),
+            whole(slots, width),
+            pl.BlockSpec((rows, stacked), lambda k: (k, 0)),
+            column(at),
+            column(at + 1),
+            column(at + 2 * steps),
+            column(at + 2 * steps + 1),
+        ],
+        out_specs=[
+            whole(slots, width),
+            whole(slots, width),
+            whole(1, width),
+            pl.BlockSpec(memory_space=pl.ANY),
+        ],
+        scratch_shapes=[
+            pltpu.VMEM((slots, width), bf16),
+            pltpu.VMEM((width, slots), bf16),
+            pltpu.VMEM((slots, width), bf16),
+            pltpu.VMEM((slots, width), f32),
+            pltpu.VMEM((slots, width), f32),
+            pltpu.VMEM((2, width, HIDDEN), bf16),
+            pltpu.VMEM((2, width, HIDDEN), bf16),
+            pltpu.VMEM((2, rows, stacked), bf16),
+            pltpu.SemaphoreType.DMA((2, 3)),
+        ],
+        cost_estimate=cost(
+            flops=18 * slots * width * inner,
+            transcendentals=slots * inner,
+            bytes_accessed=4 * weights.size + 16 * slots * width,
+        ),
+        name="feed_forward",
+    )(second, gain.reshape(1, width), live, cotangent, weights, weights, weights, weights, weights)
 
 
 class Cube:
@@ -685,8 +867,8 @@
         [
             whole(self_query, self_key, self_value, self_out, gains),
             whole(cross_query, cross_key, cross_value, cross_out),
-            whole(ff_gate, ff_up)
-            + [(ff_down, c * own, min(own, own_ff - c * own)) for c in range(stack)],
+            [(ff_down, c * own, min(own, own_ff - c * own)) for c in range(stack)]
+            + whole(ff_gate, ff_up),
         ],
         [4 * width + LANES, 4 * width, 2 * inner + stack * width],
         own,
@@ -721,15 +903,6 @@
 
     gains = gathered[:, 4 * width : 4 * width + 3].astype(f32).T
     gain_one, gain_two, gain_three = gains[0], gains[1], gains[2]
-    f_gate_up = ff[:, : 2 * inner]
-    f_down = jnp.concatenate(
-        [
-            ff[:, 2 * inner + c * width : 2 * inner + (c + 1) * width].reshape(devices, own, width)
-            for c in range(stack)
-        ],
-        axis=1,
-    )[:, :own_ff].reshape(inner, width)
-
     live = (places[None, :] < target_len[:, None]).astype(f32).reshape(slots, 1)
     inputs = targets.astype(f32).reshape(slots, width)
 
@@ -749,44 +922,48 @@
     mixed_two, total_two, key_two, value_two = held
     mixed_two = mixed_two.reshape(slots, width)
     second = first + dot(mixed_two, c_out, NN)
-    normed_three = rms_norm(second, gain_three).astype(bf16)
-    gate = dot(normed_three, f_gate_up[:, :inner], NN)
-    upward = dot(normed_three, f_gate_up[:, inner:], NN)
-    activated, gelu_pull = jax.vjp(gelu_tanh, gate)
-    hidden = (activated * upward).astype(bf16)
-    third = second + dot(hidden, f_down, NN)
-    layer_out = (third * live).astype(bf16).reshape(pairs, length, width)
-
-    grad_third = cotangent.astype(f32).reshape(slots, width) * live
-    branch_ff = grad_third.astype(bf16)
-    d_down = dot(hidden, branch_ff, TN).astype(bf16)
-    grad_hidden = dot(branch_ff, f_down, NT)
-    grad_gate = gelu_pull(grad_hidden * upward)[0].astype(bf16)
-    grad_up = (grad_hidden * activated).astype(bf16)
-    d_gate = dot(normed_three, grad_gate, TN).astype(bf16)
-    d_up = dot(normed_three, grad_up, TN).astype(bf16)
-    grad_normed_three = dot(grad_gate, f_gate_up[:, :inner], NT) + dot(
-        grad_up, f_gate_up[:, inner:], NT
-    )
-    d_down = d_down.reshape(devices, own_ff, width)
-    d_down = jnp.pad(d_down, ((0, 0), (0, stack * own - own_ff), (0, 0)))
-    d_down = [
-        d_down[:, c * own : (c + 1) * own].reshape(devices * own, width) for c in range(stack)
-    ]
-    ff_grads = lax.psum_scatter(
-        jnp.concatenate([d_gate, d_up] + d_down, axis=1),
-        BOTH,
-        scatter_dimension=0,
-        tiled=True,
-    )
-    _, norm_three = jax.vjp(rms_norm, second, gain_three)
-    back_three, d_gain_three = norm_three(grad_normed_three)
-    grad_second = grad_third + back_three
+
+    stacked = stack * width
+    if stepped:
+        layer_out, grad_second, d_gain_three, ff_grads = feed_forward(
+            second, gain_three, live, cotangent.reshape(slots, width), ff, inner, own
+        )
+        d_gain_three = d_gain_three.reshape(width)
+    else:
+        f_gate, f_up = ff[:, stacked : stacked + inner], ff[:, stacked + inner :]
+        f_down = ff[:, :stacked].reshape(devices, own, stack, width).swapaxes(1, 2)
+        f_down = f_down.reshape(devices, -1, width)[:, :own_ff].reshape(inner, width)
+        normed_three = rms_norm(second, gain_three).astype(bf16)
+        gate = dot(normed_three, f_gate, NN)
+        upward = dot(normed_three, f_up, NN)
+        activated, gelu_pull = jax.vjp(gelu_tanh, gate)
+        hidden = (activated * upward).astype(bf16)
+        third = second + dot(hidden, f_down, NN)
+        layer_out = (third * live).astype(bf16)
+        grad_third = cotangent.astype(f32).reshape(slots, width) * live
+        branch_ff = grad_third.astype(bf16)
+        d_down = dot(hidden, branch_ff, TN).astype(bf16)
+        grad_hidden = dot(branch_ff, f_down, NT)
+        grad_gate = gelu_pull(grad_hidden * upward)[0].astype(bf16)
+        grad_up = (grad_hidden * activated).astype(bf16)
+        d_gate = dot(normed_three, grad_gate, TN).astype(bf16)
+        d_up = dot(normed_three, grad_up, TN).astype(bf16)
+        grad_normed_three = dot(grad_gate, f_gate, NT) + dot(grad_up, f_up, NT)
+        d_down = d_down.reshape(devices, own_ff, width)
+        d_down = jnp.pad(d_down, ((0, 0), (0, stack * own - own_ff), (0, 0)))
+        d_down = d_down.reshape(devices, stack, own, width).swapaxes(1, 2)
+        d_down = d_down.reshape(devices * own, stacked)
+        ff_grads = jnp.concatenate([d_down, d_gate, d_up], axis=1)
+        _, norm_three = jax.vjp(rms_norm, second, gain_three)
+        back_three, d_gain_three = norm_three(grad_normed_three)
+        grad_second = grad_third + back_three
+    layer_out = layer_out.reshape(pairs, length, width)
+    ff_grads = lax.psum_scatter(ff_grads, BOTH, scatter_dimension=0, tiled=True)
 
     branch_cross = grad_second.astype(bf16)
     d_cross_out = dot(mixed_two, branch_cross, TN).astype(bf16)
     grad_mixed_two = cube_of(dot(branch_cross, c_out, NT).astype(bf16))
-    held, grad_memory = (), []
+    held = ()
     for p in range(pairs):
         grad_query_two, rows_grad, *found = cross_backward(
             p,
@@ -801,17 +978,13 @@
             c_value_out,
             held,
         )
-        held = (*held[:-1], *found, grad_query_two)
-        if p < pairs - 1:
-            grad_memory.append(exchange(rows_grad))
+        held = (*held[:-2], *found, grad_query_two, rows_grad)
     d_cross_key, d_cross_value = found
+    grad_memory = exchange(rows_grad.reshape(memory.shape))
     grad_query_two = grad_query_two.reshape(slots, width)
     d_cross_query = dot(normed_two, grad_query_two, TN).astype(bf16)
     _, norm_two = jax.vjp(rms_norm, first, gain_two)
     back_two, d_gain_two = norm_two(dot(grad_query_two, c_query, NT))
-    if stepped:
-        back_two, *grad_memory = tie(back_two, *grad_memory)
-    grad_memory.append(exchange(rows_grad))
     grad_first = grad_second + back_two
 
     branch_self = grad_first.astype(bf16)
@@ -833,18 +1006,23 @@
         grads_one, diagonals, *tied = tie(grads_one, diagonals, *middle_two, *last_send)
         middle_two, last_send = tied[: len(middle_two)], tied[len(middle_two) :]
         last_one = last_sum.swap(last_send, 8)
-        (middle_send,) = middle_sum.to_wide(middle_one, middle_two)
+        middle_keep, middle_send = middle_sum.to_wide(middle_one, middle_two, halved=True)
         grads_one, middle_send = tie(grads_one, middle_send)
-        middle_three = exchange(middle_send)
+        middle_come = cube.swap(middle_send, 1)
     grad_normed_one = dot(grads_one, w_qkv, NT)
     _, norm_one = jax.vjp(rms_norm, inputs, gain_one)
     back_one, d_gain_one = norm_one(grad_normed_one)
     if stepped:
         last_one[0], d_gain_one = tie(last_one[0], d_gain_one)
         last_send = last_sum.to_x(last_one)
-        grad_memory[-1], *last_send = tie(grad_memory[-1], *last_send)
         last_two = last_sum.swap(last_send, 16)
     grad_targets = (grad_first + back_one).reshape(pairs, length, width)
+    if stepped:
+        last_two[0], middle_come, grad_memory, grad_targets = tie(
+            last_two[0], middle_come, grad_memory, grad_targets
+        )
+        middle_keep, middle_send = middle_sum.step(1, middle_keep, middle_come)
+        middle_come = cube.swap(middle_send, 2)
 
     padded = diagonals.shape[-1]
     column = (padded - np.arange(length)) % padded
@@ -858,43 +1036,48 @@
         [d_gain_one, d_gain_two, d_gain_three, d_position.reshape(-1)]
     ).reshape(-1, LANES)
     small = jnp.pad(small, ((0, -small.shape[0] % 8), (0, 0)))
-    far = [b for b in range(cube.bits) if 0 < b < wide.bit_length() - 1]
-    near = [b for b in range(cube.bits) if b not in far]
-    small = cube.total(small, far)
+    near = range(wide.bit_length() - 1, cube.bits)
+    far = range(wide.bit_length() - 1)
+    small = cube.total(small, near)
     if stepped:
-        last_two[0], middle_three = tie(last_two[0], middle_three)
-        (last_send,) = last_sum.to_wide(last_one, last_two)
-        last_send, ff_grads = tie(last_send, ff_grads)
-        last_three = exchange(last_send)
-        middle_grads = middle_sum.finish(middle_three)
-        (d_qkv,) = last_sum.finish(last_three)
+        last_two[0], small = tie(last_two[0], small)
+        last_keep, last_send = last_sum.to_wide(last_one, last_two, halved=True)
+        last_come = cube.swap(last_send, 1)
+        middle_keep, middle_send = middle_sum.step(2, middle_keep, middle_come)
+        middle_come = cube.swap(middle_send, 4)
+        last_keep, last_send = last_sum.step(1, last_keep, last_come)
+        last_come = cube.swap(last_send, 2)
+        middle_grads = middle_sum.finish(middle_keep, middle_come)
+        last_keep, last_send = last_sum.step(2, last_keep, last_come)
+        last_come = cube.swap(last_send, 4)
+        last_come, ff_grads = tie(last_come, ff_grads)
+        (d_qkv,) = last_sum.finish(last_keep, last_come)
     else:
         scatter = lambda value: lax.psum_scatter(
             value, BOTH, scatter_dimension=0, tiled=True
         ).astype(f32)
         middle_grads = [scatter(value) for value in middle]
         d_qkv = scatter(d_qkv)
-    small = cube.total(small, near).reshape(-1)
+    small = cube.total(small, far).reshape(-1)
     gain_grads = small[: 3 * width].reshape(3, devices, width // devices)
     gain_grads = lax.dynamic_index_in_dim(gain_grads, cube.index, 1, keepdims=False)
     grad_position = small[3 * width : 3 * width + BUCKETS * HEADS].reshape(BUCKETS, HEADS)
 
     ff_grads = ff_grads.astype(f32)
     d_down = jnp.concatenate(
-        [ff_grads[:, 2 * inner + c * width : 2 * inner + (c + 1) * width] for c in range(stack)],
-        axis=0,
+        [ff_grads[:, c * width : (c + 1) * width] for c in range(stack)], axis=0
     )[:own_ff]
     return (
         layer_out,
         grad_targets,
-        jnp.stack(grad_memory, axis=1).reshape(memory.shape).astype(f32),
+        grad_memory.astype(f32),
         d_qkv[:, :width],
         d_qkv[:, width : 2 * width],
         d_qkv[:, 2 * width :],
         middle_grads[4],
         *middle_grads[:4],
-        ff_grads[:, :inner],
-        ff_grads[:, inner : 2 * inner],
+        ff_grads[:, stacked : stacked + inner],
+        ff_grads[:, stacked + inner :],
         d_down,
         gain_grads[0],
         gain_grads[1],

time: 495 us -> 469 us (0.947)
  Pallas kernels: 165 us -> 198 us
  matrix products: 81.3 us -> 51 us
  waiting for transfers between devices: 129 us -> 118 us
  other arithmetic: 22.7 us -> 16.5 us
  local copies, waits for them, and re-layouts: 26 us -> 20.2 us
  starting transfers between devices: 49.5 us -> 43.9 us
    pallas_call x0 -> x5, Pallas kernels: none -> 34.5 us  [the longest x1 26.5 us: feed_forward(): pl.pallas_call(functools.partial(feed_forward_kernel, own), out_shape=(ja...]
    all_to_all x5 -> x2, waiting for transfers between devices: 31.7 us -> 0.01 us  [on_device(): lax.all_to_all(value, 'wide', split_axis=0, concat_axis=0, tiled=True)]
    dot_general x21 -> x12, matrix products: 78.1 us -> 47.9 us  [dot(): return lax.dot_general(left, right, dims, preferred_element_type=f32)]
    ppermute x18 -> x24, waiting for transfers between devices: 77.1 us -> 102 us  [swap(): return lax.ppermute(value, BOTH, pairs)]
    all_to_all x5 -> x2, starting transfers between devices: 24.6 us -> 9.89 us  [on_device(): lax.all_to_all(value, 'wide', split_axis=0, concat_axis=0, tiled=True)]
    ppermute x18 -> x24, starting transfers between devices: 24.6 us -> 33.4 us  [swap(): return lax.ppermute(value, BOTH, pairs)]
    unnamed x97 -> x39, local copies, waits for them, and re-layouts: 13.6 us -> 5.41 us
    optimization_barrier x0 -> x1, local copies, waits for them, and re-layouts: none -> 7.44 us  [tie(): return lax.optimization_barrier(values)]
  transfers between devices with their start and end apart: 26 -> 29, of which waited for: 13 -> 16; matrix products, arithmetic and copies ran while one was open for 17% -> 17% of each run, Pallas kernels for 33% -> 36%
where the time goes in v4:
time: 469 us; the launch traced here: 463 us
  Pallas kernels  198 us (42%)
  waiting for transfers between devices  118 us (25%)
  matrix products  51 us (11%)
  starting transfers between devices  43.9 us (9%)
  local copies, waits for them, and re-layouts  20.2 us (4%)
  other arithmetic  16.5 us (4%)
  between operations  14.5 us (3%)
    ppermute x24, waiting for transfers between devices, swap(): return lax.ppermute(value, BOTH, pairs)  102 us
    dot_general x12, matrix products, dot(): return lax.dot_general(left, right, dims, preferred_element_type=f32)  47.9 us
    pallas_call x2, Pallas kernels, cross_backward(): pl.pallas_call(functools.partial(cross_backward_kernel, pair, last), out_...  44.3 us
    pallas_call x2, Pallas kernels, cross_forward(): pl.pallas_call(functools.partial(cross_forward_kernel, pair), out_shape=(...  33.6 us
    ppermute x24, starting transfers between devices, swap(): return lax.ppermute(value, BOTH, pairs)  33.4 us
    pallas_call x1, Pallas kernels, feed_forward(): pl.pallas_call(functools.partial(feed_forward_kernel, own), out_shape=(ja...  26.5 us
    pallas_call x6, Pallas kernels, message(): pl.pallas_call(kernel, out_shape=out_shape, grid_spec=pltpu.PrefetchScala...  23.7 us
    pallas_call x1, Pallas kernels, self_backward(): pl.pallas_call(self_backward_kernel, out_shape=(jax.ShapeDtypeStruct(qkv....  22.5 us
  transfers between devices with their start and end apart: 29, of which 16 were waited for; matrix products, arithmetic and copies ran while one was open for 17% of the time, Pallas kernels for 36%

profile of v4, /device:TPU:0, one launch (start us, length us, event | category | flops | bytes accessed | tf_op | source)
XLA Modules:
  0.0 462.7 jit_solution(1124771925286885030)
XLA Ops:
  11.5 5.1 %collective-permute-start.2 = (bf16[24,3072]{1,0:T(8,128)(2,1)}, bf16[24,3072]{1,0:T(8,128)(2,1)}, u32[]{:S(2)}, u32[]{:S(2)}) collective-permute-start(bf16[24,3072]{1,0:T(8,128)(2,1)} %get-tuple-element.90.refs_0_), channel_id=1, source_target_pairs={{0,6},{1,7},{2,4},{3,5},{4,2},{5,3},{6,0},{7,1},{8,14},{9,15},{10,... | collective-permute-start | bytes 442376 | tf_op jit(solution)/shard_map/ppermute | solution.py:529
  21.7 9.3 %collective-permute-done.1.refs_2_ = bf16[24,3072]{1,0:T(8,128)(2,1)} collective-permute-done((bf16[24,3072]{1,0:T(8,128)(2,1)}, bf16[24,3072]{1,0:T(8,128)(2,1)}, u32[]{:S(2)}, u32[]{:S(2)}) %collective-permute-start.1) | collective-permute-done | bytes 147488 | tf_op jit(solution)/shard_map/ppermute | solution.py:529
  46.5 12.7 %collective-permute-done.5.come_ref = bf16[1,192,1536]{2,1,0:T(8,128)(2,1)S(1)} collective-permute-done((bf16[1,192,1536]{2,1,0:T(8,128)(2,1)}, bf16[1,192,1536]{2,1,0:T(8,128)(2,1)S(1)}, u32[]{:S(2)}, u32[]{:S(2)}) %collective-permute-start.5) | collective-permute-done | bytes 589856 | tf_op jit(solution)/shard_map/ppermute | solution.py:529
  62.2 5.5 %all-to-all-start = ((bf16[16,128,768]{2,1,0:T(8,128)(2,1)}), bf16[16,128,768]{2,1,0:T(8,128)(2,1)S(1)}, u32[]{:S(2)}, u32[]{:S(2)}) async-start(bf16[16,128,768]{2,1,0:T(8,128)(2,1)} %param.22), calls=%async_computation | async-start | bytes 6291456 | tf_op jit(solution)/shard_map/all_to_all | solution.py:885
  74.6 32.6 %collective-permute-done.6.come_ref = bf16[8,24,1536]{2,1,0:T(8,128)(2,1)} collective-permute-done((bf16[8,24,1536]{2,1,0:T(8,128)(2,1)}, bf16[8,24,1536]{2,1,0:T(8,128)(2,1)}, u32[]{:S(2)}, u32[]{:S(2)}) %collective-permute-start.6) | collective-permute-done | bytes 589856 | tf_op jit(solution)/shard_map/ppermute | solution.py:529
  107.2 5.3 %merge_two.9 = bf16[8,2,24,1536]{3,2,1,0:T(8,128)(2,1)} custom-call(s32[1]{0:T(128)} %bitcast.5.side_ref, bf16[8,24,1536]{2,1,0:T(8,128)(2,1)} %bitcast.126, bf16[8,24,1536]{2,1,0:T(8,128)(2,1)} %collective-permute-done.6.come_ref), custom_call_target="tpu_custom_call" | custom-call | bytes 294912 | tf_op jit(solution)/shard_map/merge_two/pallas_call | solution.py:575
  113.0 7.4 %copy.60 = bf16[768,3200]{0,1:T(8,128)(2,1)} copy(bf16[768,3200]{1,0:T(8,128)(2,1)} %all-gather.3.cloned.1.call-done) | data formatting | bytes 9830400 | tf_op jit(solution)/shard_map/optimization_barrier | solution.py:797
  121.8 6.1 %convolution_convert_fusion = bf16[576,2304]{1,0:T(8,128)(2,1)} fusion(bf16[768,3200]{1,0:T(8,128)(2,1)} %all-gather.3.cloned.1.call-done, f32[768]{0:T(1024)S(1)} %get-tuple-element.201, f32[576]{0:T(1024)S(1)} %rsqrt.25, bf16[576,768]{1,0:T(8,128)(2,1)} %bitcast.118), kind=kOutput, calls=%fused_computation.6 | convolution fusion | flops 2041528320 | bytes 7083264 | tf_op jit(solution)/shard_map/dot_general | solution.py:38
  127.9 11.7 %self_forward.1 = (bf16[2,288,768]{2,1,0:T(8,128)(2,1)}, f32[2,288,768]{2,1,0:T(8,128)}) custom-call(bf16[2,288,2304]{2,1,0:T(8,128)(2,1)} %bitcast.69, bf16[2,288,2304]{2,1,0:T(8,128)(2,1)} %bitcast.70, bf16[2,288,2304]{2,1,0:T(8,128)(2,1)} %bitcast.71, bf16[12,288,288]{2,1,0:T(8,128)(2,1)} %fusion.6.bias_ref), custom_call_target="tpu_custom_call" | custom-call | flops 63700992 | bytes 663552 | tf_op jit(solution)/shard_map/self_forward/pallas_call | solution.py:96
  139.6 3.9 multiply_reduce_fusion.4
  143.5 4.0 merge_two.10
  147.6 3.9 merge_two.11
  156.8 16.7 %cross_forward.2 = (bf16[2,288,768]{2,1,0:T(8,128)(2,1)}, f32[2,288,768]{2,1,0:T(8,128)}, bf16[2,1024,768]{2,1,0:T(8,128)(2,1)}, bf16[2,1024,768]{2,1,0:T(8,128)(2,1)}) custom-call(s32[2]{0:T(128)} %len_ref.7, bf16[2,288,768]{2,1,0:T(8,128)(2,1)} %bitcast.94, bf16[8,2,128,768]{3,2,1,0:T(8,128)(2,1)} %bitcast.75, bf16[768,1536]{1,0:T(8,128)(2,1)} %bitcast.86, ...), custom_call_target="tpu_custom_call" | custom-call | flops 415236096 | bytes 811008 | tf_op jit(solution)/shard_map/cross_forward/pallas_call | solution.py:214
  173.5 16.9 %cross_forward.3 = (bf16[2,288,768]{2,1,0:T(8,128)(2,1)}, f32[2,288,768]{2,1,0:T(8,128)}, bf16[2,1024,768]{2,1,0:T(8,128)(2,1)}, bf16[2,1024,768]{2,1,0:T(8,128)(2,1)}) custom-call(s32[2]{0:T(128)} %len_ref.7, bf16[2,288,768]{2,1,0:T(8,128)(2,1)} %bitcast.95, ...), custom_call_target="tpu_custom_call", output_to_operand_aliasing={{0}: (5, {}), {1}: (6, {}), {2}: (7, {}), {3}: (8, {})} | custom-call | flops 415236096 | bytes 811008 | tf_op jit(solution)/shard_map/cross_forward/pallas_call | solution.py:214
  190.4 3.9 convolution_add_fusion.second_ref
  194.3 16.1 %all-gather.5.cloned.1.call-done.down_ref.gate_low_ref.gate_high_ref.up_low_ref.up_high_ref = bf16[768,6400]{1,0:T(8,128)(2,1)} async-done(((bf16[24,6400]{1,0:T(8,128)(2,1)}), bf16[768,6400]{1,0:T(8,128)(2,1)}) %all-gather.5.cloned.1.call-update) | async-done | bytes 9830416 | tf_op jit(solution)/shard_map/all_gather | solution.py:889
  210.4 26.5 %feed_forward.1 = (bf16[576,768]{1,0:T(8,128)(2,1)}, f32[576,768]{1,0:T(8,128)}, f32[1,768]{1,0:T(1,128)}, bf16[768,6400]{1,0:T(8,128)(2,1)}) custom-call(f32[576,768]{1,0:T(8,128)} %convolution_add_fusion.second_ref, f32[1,768]{1,0:T(1,128)} %get-tuple-element.213.gain_ref, f32[576,1]{1,0:T(8,128)} %reshape.415.live_ref, bf16[576,768]{1,0:T(8,128)(2,1)} %bitcast.131, ...), custom_call_target="tpu_custom_call" | custom-call | flops 2038431744 | bytes 3342336 | tf_op jit(solution)/shard_map/feed_forward/pallas_call | solution.py:474
  240.8 19.5 %cross_backward.2 = (bf16[2,288,768]{2,1,0:T(8,128)(2,1)}, bf16[8,2,128,768]{3,2,1,0:T(8,128)(2,1)}, bf16[1024,1536]{1,0:T(8,128)(2,1)}) custom-call(s32[2]{0:T(128)} %len_ref.7, bf16[2,288,768]{2,1,0:T(8,128)(2,1)} %bitcast.96, bf16[2,1024,768]{2,1,0:T(8,128)(2,1)} %get-tuple-element.111.k_ref, bf16[2,1024,768]{2,1,0:T(8,128)(2,1)} %get-tuple-element.112.v_ref, ...), custom_call_target="tpu_custom_call" | custom-call | flops 887095296 | bytes 1062912 | tf_op jit(solution)/shard_map/cross_backward/pallas_call | solution.py:314
  260.3 24.9 %cross_backward.3 = (bf16[2,288,768]{2,1,0:T(8,128)(2,1)}, bf16[8,2,128,768]{3,2,1,0:T(8,128)(2,1)}, bf16[768,768]{1,0:T(8,128)(2,1)}, bf16[768,768]{1,0:T(8,128)(2,1)}) custom-call(s32[2]{0:T(128)} %len_ref.7, bf16[2,288,768]{2,1,0:T(8,128)(2,1)} %bitcast.97, ...), custom_call_target="tpu_custom_call", output_to_operand_aliasing={{0}: (10, {}), {1}: (11, {})} | custom-call | flops 887095296 | bytes 1062912 | tf_op jit(solution)/shard_map/cross_backward/pallas_call | solution.py:314
  296.1 4.9 %message.6 = bf16[2,192,3840]{2,1,0:T(8,128)(2,1)} custom-call(s32[3]{0:T(128)} %pad_add_fusion.sides_ref, bf16[2,2,192,768]{3,2,1,0:T(8,128)(2,1)} %bitcast.111, bf16[2,2,192,768]{3,2,1,0:T(8,128)(2,1)} %bitcast.99, bf16[2,2,192,768]{3,2,1,0:T(8,128)(2,1)} %bitcast.102, bf16[2,2,192,768]{3,2,1,0:T(8,128)(2,1)} %bitcast.105, bf16[2,2,192,768]{3,2,1,0:T(8,128)(2,1)} %bitcast.108), custom_call_target="tpu_custom_call" | custom-call | flops 184320 | bytes 737280 | tf_op jit(solution)/shard_map/message/pallas_call | solution.py:708
  301.2 4.4 all-to-all-start.1
  309.3 3.7 message.7
  313.9 22.5 %self_backward.1 = (bf16[2,288,2304]{2,1,0:T(8,128)(2,1)}, f32[6,2,8,384]{3,2,1,0:T(8,128)}) custom-call(bf16[2,288,2304]{2,1,0:T(8,128)(2,1)} %bitcast.72, bf16[2,288,2304]{2,1,0:T(8,128)(2,1)} %bitcast.73, bf16[2,288,2304]{2,1,0:T(8,128)(2,1)} %bitcast.74, bf16[12,288,288]{2,1,0:T(8,128)(2,1)} %fusion.6.bias_ref, ...), custom_call_target="tpu_custom_call" | custom-call | flops 159252480 | bytes 995328 | tf_op jit(solution)/shard_map/self_backward/pallas_call | solution.py:161
  336.4 6.9 %bitcast_convert_fusion = bf16[768,2304]{1,0:T(8,128)(2,1)} fusion(bf16[2,288,2304]{2,1,0:T(8,128)(2,1)} %get-tuple-element.121, f32[768]{0:T(1024)S(1)} %get-tuple-element.201, f32[2,288]{1,0:T(2,128)S(1)} %get-tuple-element.214, bf16[2,288,768]{2,1,0:T(8,128)(2,1)} %param.21), kind=kOutput, calls=%fused_computation.2 | convolution fusion | flops 2041970688 | bytes 7083264 | tf_op jit(solution)/shard_map/dot_general | solution.py:38
  343.3 4.5 message.8
  347.8 6.7 %collective-permute-done.10.refs_6_ = bf16[1,192,3840]{2,1,0:T(8,128)(2,1)} collective-permute-done((bf16[1,192,3840]{2,1,0:T(8,128)(2,1)}, bf16[1,192,3840]{2,1,0:T(8,128)(2,1)}, u32[]{:S(2)}, u32[]{:S(2)}) %collective-permute-start.10) | collective-permute-done | bytes 1474592 | tf_op jit(solution)/shard_map/ppermute | solution.py:529
  354.5 4.4 message.9
  362.0 6.8 %multiply_reduce_fusion.1 = (f32[576]{0:T(1024)S(1)}, f32[768]{0:T(1024)S(1)}, f32[576,768]{1,0:T(8,128)}) fusion(f32[768]{0:T(1024)S(1)} %get-tuple-element.201, f32[576]{0:T(1024)S(1)} %rsqrt.25, bf16[2,288,768]{2,1,0:T(8,128)(2,1)} %param.21, bf16[576,2304]{1,0:T(8,128)(2,1)} %bitcast.140, bf16[768,3200]{1,0:T(8,128)(2,1)} %all-gather.3.cloned.1.call-done, ...), kind=kOutput, calls=%fused_computation.16 | convolution fusion | flops 2041969408 | bytes 9742848 | tf_op jit(solution)/shard_map/dot_general | solution.py:38
  375.0 4.0 fusion.8
  379.1 19.3 %collective-permute-done.15 = f32[24,128]{1,0:T(8,128)S(1)} collective-permute-done((f32[24,128]{1,0:T(8,128)S(1)}, f32[24,128]{1,0:T(8,128)S(1)}, u32[]{:S(2)}, u32[]{:S(2)}) %collective-permute-start.15) | collective-permute-done | bytes 12320 | tf_op jit(solution)/shard_map/ppermute | solution.py:529
  406.5 9.4 %collective-permute-done.16.refs_1_ = bf16[4,24,2304]{2,1,0:T(8,128)(2,1)} collective-permute-done((bf16[4,24,2304]{2,1,0:T(8,128)(2,1)}, bf16[4,24,2304]{2,1,0:T(8,128)(2,1)}, u32[]{:S(2)}, u32[]{:S(2)}) %collective-permute-start.16) | collective-permute-done | bytes 442400 | tf_op jit(solution)/shard_map/ppermute | solution.py:529
  422.5 4.1 collective-permute-start.20
  (150 shorter events, 114.6 us)
Async XLA Ops:
  7.2 105.3 %all-gather.3.cloned.1.call-start = ((), (), s32[]{:S(2)}) async-start(), calls=%async_computation.3 | async-start | bytes 5068800 | tf_op jit(solution)/shard_map/all_gather | solution.py:888
  10.8 199.7 %all-gather.5.cloned.1.call-start = ((), (), s32[]{:S(2)}) async-start(), calls=%async_computation.4 | async-start | bytes 10137600 | tf_op jit(solution)/shard_map/all_gather | solution.py:889
  11.5 10.2 %collective-permute-start.2 = (bf16[24,3072]{1,0:T(8,128)(2,1)}, bf16[24,3072]{1,0:T(8,128)(2,1)}, u32[]{:S(2)}, u32[]{:S(2)}) collective-permute-start(bf16[24,3072]{1,0:T(8,128)(2,1)} %get-tuple-element.90.refs_0_), channel_id=1, source_target_pairs={{0,6},{1,7},{2,4},{3,5},{4,2},{5,3},{6,0},{7,1},{8,14},{9,15},{10,... | collective-permute-start | bytes 442376 | tf_op jit(solution)/shard_map/ppermute | solution.py:529
  16.6 14.4 %collective-permute-start.1 = (bf16[24,3072]{1,0:T(8,128)(2,1)}, bf16[24,3072]{1,0:T(8,128)(2,1)}, u32[]{:S(2)}, u32[]{:S(2)}) collective-permute-start(bf16[24,3072]{1,0:T(8,128)(2,1)} %get-tuple-element.90.refs_0_), channel_id=1, source_target_pairs={{0,4},{1,5},{2,6},{3,7},{4,0},{5,1},{6,2},{7,3},{8,12},{9,13},{10,... | collective-permute-start | bytes 442376 | tf_op jit(solution)/shard_map/ppermute | solution.py:529
  16.6 14.4 %collective-permute-start = (bf16[24,3072]{1,0:T(8,128)(2,1)}, bf16[24,3072]{1,0:T(8,128)(2,1)}, u32[]{:S(2)}, u32[]{:S(2)}) collective-permute-start(bf16[24,3072]{1,0:T(8,128)(2,1)} %get-tuple-element.90.refs_0_), channel_id=1, source_target_pairs={{0,2},{1,3},{2,0},{3,1},{4,6},{5,7},{6,4},{7,5},{8,10},{9,11},{10,... | collective-permute-start | bytes 442376 | tf_op jit(solution)/shard_map/ppermute | solution.py:529
  33.0 7.8 %collective-permute-start.4 = (bf16[1,96,1536]{2,1,0:T(8,128)(2,1)}, bf16[1,96,1536]{2,1,0:T(8,128)(2,1)}, u32[]{:S(2)}, u32[]{:S(2)}) collective-permute-start(bf16[1,96,1536]{2,1,0:T(8,128)(2,1)} %bitcast.134), channel_id=1, source_target_pairs={{0,16},{1,17},{2,18},{3,19},{4,20},{5,21},{6,22},{7,23},{8,24},{9,... | collective-permute-start | bytes 884744 | tf_op jit(solution)/shard_map/ppermute | solution.py:529
  34.6 8.6 %collective-permute-start.3 = (bf16[4,24,1536]{2,1,0:T(8,128)(2,1)}, bf16[4,24,1536]{2,1,0:T(8,128)(2,1)}, u32[]{:S(2)}, u32[]{:S(2)}) collective-permute-start(bf16[4,24,1536]{2,1,0:T(8,128)(2,1)} %get-tuple-element.91.mine_ref), channel_id=1, source_target_pairs={{0,1},{1,0},{2,3},{3,2},{4,5},{5,4},{6,7},{7,6},{8,9},{9,8},{10,11... | collective-permute-start | bytes 884744 | tf_op jit(solution)/shard_map/ppermute | solution.py:529
  46.5 12.7 %collective-permute-start.5 = (bf16[1,192,1536]{2,1,0:T(8,128)(2,1)}, bf16[1,192,1536]{2,1,0:T(8,128)(2,1)S(1)}, u32[]{:S(2)}, u32[]{:S(2)}) collective-permute-start(bf16[1,192,1536]{2,1,0:T(8,128)(2,1)} %bitcast.127), channel_id=1, source_target_pairs={{0,16},{1,17},{2,18},{3,19},{4,20},{5,21},{6,22},{7,23},{8,24},{9,... | collective-permute-start | bytes 1769480 | tf_op jit(solution)/shard_map/ppermute | solution.py:529
  62.2 93.0 %all-to-all-start = ((bf16[16,128,768]{2,1,0:T(8,128)(2,1)}), bf16[16,128,768]{2,1,0:T(8,128)(2,1)S(1)}, u32[]{:S(2)}, u32[]{:S(2)}) async-start(bf16[16,128,768]{2,1,0:T(8,128)(2,1)} %param.22), calls=%async_computation | async-start | bytes 6291456 | tf_op jit(solution)/shard_map/all_to_all | solution.py:885
  67.7 381.5 %reduce-scatter.2.cloned.1.call-start = ((), (), s32[]{:S(2)}) async-start(), calls=%async_computation.5 | async-start | bytes 10137600 | tf_op jit(solution)/shard_map/reduce_scatter | solution.py:961
  70.1 37.1 %collective-permute-start.6 = (bf16[8,24,1536]{2,1,0:T(8,128)(2,1)}, bf16[8,24,1536]{2,1,0:T(8,128)(2,1)}, u32[]{:S(2)}, u32[]{:S(2)}) collective-permute-start(bf16[8,24,1536]{2,1,0:T(8,128)(2,1)} %bitcast.125), channel_id=1, source_target_pairs={{0,1},{1,0},{2,3},{3,2},{4,5},{5,4},{6,7},{7,6},{8,9},{9,8},{10,11... | collective-permute-start | bytes 1769480 | tf_op jit(solution)/shard_map/ppermute | solution.py:529
  112.5 31.0 %collective-permute-start.7 = (bf16[2,192,1536]{2,1,0:T(8,128)(2,1)}, bf16[2,192,1536]{2,1,0:T(8,128)(2,1)}, u32[]{:S(2)}, u32[]{:S(2)}) collective-permute-start(bf16[2,192,1536]{2,1,0:T(8,128)(2,1)} %bitcast.114), channel_id=1, source_target_pairs={{0,8},{1,9},{2,10},{3,11},{4,12},{5,13},{6,14},{7,15},{8,0},{9,1},... | collective-permute-start | bytes 3538952 | tf_op jit(solution)/shard_map/ppermute | solution.py:529
  112.5 35.0 %collective-permute-start.8 = (bf16[2,192,1536]{2,1,0:T(8,128)(2,1)}, bf16[2,192,1536]{2,1,0:T(8,128)(2,1)}, u32[]{:S(2)}, u32[]{:S(2)}) collective-permute-start(bf16[2,192,1536]{2,1,0:T(8,128)(2,1)} %bitcast.116), channel_id=1, source_target_pairs={{0,8},{1,9},{2,10},{3,11},{4,12},{5,13},{6,14},{7,15},{8,0},{9,1},... | collective-permute-start | bytes 3538952 | tf_op jit(solution)/shard_map/ppermute | solution.py:529
  173.5 16.9 %copy-start.3 = (bf16[2,2,192,1536]{3,2,1,0:T(8,128)(2,1)S(1)}, bf16[2,2,192,1536]{3,2,1,0:T(8,128)(2,1)}, u32[]{:S(2)}) copy-start(bf16[2,2,192,1536]{3,2,1,0:T(8,128)(2,1)} %merge_two.11) | copy-start | bytes 7077892
  260.3 24.9 %copy-start.4 = (bf16[2,2,192,1536]{3,2,1,0:T(8,128)(2,1)S(1)}, bf16[2,2,192,1536]{3,2,1,0:T(8,128)(2,1)}, u32[]{:S(2)}) copy-start(bf16[2,2,192,1536]{3,2,1,0:T(8,128)(2,1)} %merge_two.10) | copy-start | bytes 7077892
  301.0 8.3 %collective-permute-start.9 = (bf16[2,192,3840]{2,1,0:T(8,128)(2,1)}, bf16[2,192,3840]{2,1,0:T(8,128)(2,1)}, u32[]{:S(2)}, u32[]{:S(2)}) collective-permute-start(bf16[2,192,3840]{2,1,0:T(8,128)(2,1)} %message.6), channel_id=1, source_target_pairs={{0,8},{1,9},{2,10},{3,11},{4,12},{5,13},{6,14},{7,15},{8,0},{9,1},... | collective-permute-start | bytes 8847368 | tf_op jit(solution)/shard_map/ppermute | solution.py:529
  301.2 97.2 %all-to-all-start.1 = ((bf16[16,128,768]{2,1,0:T(8,128)(2,1)}), bf16[16,128,768]{2,1,0:T(8,128)(2,1)S(1)}, u32[]{:S(2)}, u32[]{:S(2)}) async-start(bf16[16,128,768]{2,1,0:T(8,128)(2,1)} %bitcast.98), calls=%async_computation.1 | async-start | bytes 6291456 | tf_op jit(solution)/shard_map/all_to_all | solution.py:885
  312.9 41.5 %collective-permute-start.10 = (bf16[1,192,3840]{2,1,0:T(8,128)(2,1)}, bf16[1,192,3840]{2,1,0:T(8,128)(2,1)}, u32[]{:S(2)}, u32[]{:S(2)}) collective-permute-start(bf16[1,192,3840]{2,1,0:T(8,128)(2,1)} %message.7), channel_id=1, source_target_pairs={{0,16},{1,17},{2,18},{3,19},{4,20},{5,21},{6,22},{7,23},{8,24},{9,... | collective-permute-start | bytes 4423688 | tf_op jit(solution)/shard_map/ppermute | solution.py:529
  354.4 14.3 %collective-permute-start.11 = (bf16[2,192,2304]{2,1,0:T(8,128)(2,1)}, bf16[2,192,2304]{2,1,0:T(8,128)(2,1)}, u32[]{:S(2)}, u32[]{:S(2)}) collective-permute-start(bf16[2,192,2304]{2,1,0:T(8,128)(2,1)} %message.8), channel_id=1, source_target_pairs={{0,8},{1,9},{2,10},{3,11},{4,12},{5,13},{6,14},{7,15},{8,0},{9,1},... | collective-permute-start | bytes 5308424 | tf_op jit(solution)/shard_map/ppermute | solution.py:529
  359.5 38.9 %collective-permute-start.13 = (bf16[4,24,3840]{2,1,0:T(8,128)(2,1)}, bf16[4,24,3840]{2,1,0:T(8,128)(2,1)}, u32[]{:S(2)}, u32[]{:S(2)}) collective-permute-start(bf16[4,24,3840]{2,1,0:T(8,128)(2,1)} %get-tuple-element.130), channel_id=1, source_target_pairs={{0,1},{1,0},{2,3},{3,2},{4,5},{5,4},{6,7},{7,6},{8,9},{9,8},{10,11... | collective-permute-start | bytes 2211848 | tf_op jit(solution)/shard_map/ppermute | solution.py:529
  371.8 26.7 %collective-permute-start.12 = (bf16[1,192,2304]{2,1,0:T(8,128)(2,1)}, bf16[1,192,2304]{2,1,0:T(8,128)(2,1)}, u32[]{:S(2)}, u32[]{:S(2)}) collective-permute-start(bf16[1,192,2304]{2,1,0:T(8,128)(2,1)} %message.10), channel_id=1, source_target_pairs={{0,16},{1,17},{2,18},{3,19},{4,20},{5,21},{6,22},{7,23},{8,24},{9,... | collective-permute-start | bytes 2654216 | tf_op jit(solution)/shard_map/ppermute | solution.py:529
  372.1 1.2 collective-permute-start.14
  373.4 25.0 %collective-permute-start.15 = (f32[24,128]{1,0:T(8,128)S(1)}, f32[24,128]{1,0:T(8,128)S(1)}, u32[]{:S(2)}, u32[]{:S(2)}) collective-permute-start(f32[24,128]{1,0:T(8,128)S(1)} %pad_add_fusion.1), channel_id=1, source_target_pairs={{0,16},{1,17},{2,18},{3,19},{4,20},{5,21},{6,22},{7,23},{8,24},{9,... | collective-permute-start | bytes 36872 | tf_op jit(solution)/shard_map/ppermute | solution.py:529
  401.8 14.1 %collective-permute-start.16 = (bf16[4,24,2304]{2,1,0:T(8,128)(2,1)}, bf16[4,24,2304]{2,1,0:T(8,128)(2,1)}, u32[]{:S(2)}, u32[]{:S(2)}) collective-permute-start(bf16[4,24,2304]{2,1,0:T(8,128)(2,1)} %get-tuple-element.140), channel_id=1, source_target_pairs={{0,1},{1,0},{2,3},{3,2},{4,5},{5,4},{6,7},{7,6},{8,9},{9,8},{10,11... | collective-permute-start | bytes 1327112 | tf_op jit(solution)/shard_map/ppermute | solution.py:529
  404.4 15.5 %collective-permute-start.19 = (bf16[2,24,3840]{2,1,0:T(8,128)(2,1)}, bf16[2,24,3840]{2,1,0:T(8,128)(2,1)S(1)}, u32[]{:S(2)}, u32[]{:S(2)}) collective-permute-start(bf16[2,24,3840]{2,1,0:T(8,128)(2,1)} %get-tuple-element.150), channel_id=1, source_target_pairs={{0,2},{1,3},{2,0},{3,1},{4,6},{5,7},{6,4},{7,5},{8,10},{9,11},{10,... | collective-permute-start | bytes 1105928 | tf_op jit(solution)/shard_map/ppermute | solution.py:529
  417.9 23.6 %collective-permute-start.17 = (bf16[2,24,2304]{2,1,0:T(8,128)(2,1)}, bf16[2,24,2304]{2,1,0:T(8,128)(2,1)}, u32[]{:S(2)}, u32[]{:S(2)}) collective-permute-start(bf16[2,24,2304]{2,1,0:T(8,128)(2,1)} %get-tuple-element.142), channel_id=1, source_target_pairs={{0,2},{1,3},{2,0},{3,1},{4,6},{5,7},{6,4},{7,5},{8,10},{9,11},{10,... | collective-permute-start | bytes 663560 | tf_op jit(solution)/shard_map/ppermute | solution.py:529
  422.5 23.0 %collective-permute-start.20 = (bf16[1,24,3840]{2,1,0:T(8,128)(2,1)}, bf16[1,24,3840]{2,1,0:T(8,128)(2,1)S(1)}, u32[]{:S(2)}, u32[]{:S(2)}) collective-permute-start(bf16[1,24,3840]{2,1,0:T(8,128)(2,1)} %get-tuple-element.152), channel_id=1, source_target_pairs={{0,4},{1,5},{2,6},{3,7},{4,0},{5,1},{6,2},{7,3},{8,12},{9,13},{10,... | collective-permute-start | bytes 552968 | tf_op jit(solution)/shard_map/ppermute | solution.py:529
  426.7 4.5 collective-permute-start.21
  431.2 4.8 %collective-permute-start.22 = (f32[24,128]{1,0:T(8,128)S(1)}, f32[24,128]{1,0:T(8,128)S(1)}, u32[]{:S(2)}, u32[]{:S(2)}) collective-permute-start(f32[24,128]{1,0:T(8,128)S(1)} %add.316), channel_id=1, source_target_pairs={{0,2},{1,3},{2,0},{3,1},{4,6},{5,7},{6,4},{7,5},{8,10},{9,11},{10,... | collective-permute-start | bytes 36872 | tf_op jit(solution)/shard_map/ppermute | solution.py:529
  436.1 4.6 collective-permute-start.23
  436.1 19.7 %copy-start.1 = (bf16[32,12]{0,1:T(8,128)(2,1)S(1)}, bf16[32,12]{0,1:T(8,128)(2,1)}, u32[]{:S(2)}) copy-start(bf16[32,12]{0,1:T(8,128)(2,1)} %param.40) | copy-start | bytes 2308
  443.3 5.9 %collective-permute-start.18 = (bf16[1,24,2304]{2,1,0:T(8,128)(2,1)}, bf16[1,24,2304]{2,1,0:T(8,128)(2,1)S(1)}, u32[]{:S(2)}, u32[]{:S(2)}) collective-permute-start(bf16[1,24,2304]{2,1,0:T(8,128)(2,1)} %get-tuple-element.144), channel_id=1, source_target_pairs={{0,4},{1,5},{2,6},{3,7},{4,0},{5,1},{6,2},{7,3},{8,12},{9,13},{10,... | collective-permute-start | bytes 331784 | tf_op jit(solution)/shard_map/ppermute | solution.py:529
  (16 other events, 56.8 us)
Sparse Core Ops, SparseCore 0:
  11.5 86.1 all-gather.2
  100.5 109.8 all-gather.4
  237.1 190.6 reduce-scatter.1

commit v5 on v4

--- a/solution.py
+++ b/solution.py
@@ -65,13 +65,13 @@
     return jnp.concatenate([total[:, :1], total[:, HEAD_DIM : HEAD_DIM + 1]], axis=0)
 
 
-def attend(scores, v, mixed_ref, total_ref):
+def attend(scores, v, mixed_ref, total_ref, pair=0):
     top = jnp.max(scores, axis=1, keepdims=True)
     grown = jnp.exp(scores - top)
     total = jnp.sum(grown, axis=1, keepdims=True)
     mixed = dot(grown.astype(bf16), v, NN) * (1.0 / total)
-    mixed_ref[0] = join_heads(mixed).astype(bf16)
-    total_ref[0] = join_heads(jnp.broadcast_to(top + jnp.log(total), mixed.shape))
+    mixed_ref[pair] = join_heads(mixed).astype(bf16)
+    total_ref[pair] = join_heads(jnp.broadcast_to(top + jnp.log(total), mixed.shape))
 
 
 def attend_back(scores, total, grad, v):
@@ -82,29 +82,30 @@
 
 
 def self_forward_kernel(q_ref, k_ref, v_ref, bias_ref, mixed_ref, total_ref):
-    length = q_ref.shape[1]
+    pairs, length, _ = q_ref.shape
     bias = bias_ref[...].reshape(2 * length, length).astype(f32)
-    scores = dot(stack_heads(q_ref[0]), k_ref[0], NT) + bias
-    attend(scores, v_ref[0], mixed_ref, total_ref)
+    for p in range(pairs):
+        scores = dot(stack_heads(q_ref[p]), k_ref[p], NT) + bias
+        attend(scores, v_ref[p], mixed_ref, total_ref, p)
 
 
 def self_forward(qkv, bias):
     pairs, length, width = qkv.shape
     width //= 3
     steps = width // LANES
-    part = lambda c: pl.BlockSpec((1, length, LANES), lambda p, h: (p, 0, h + c * steps))
+    part = lambda c: pl.BlockSpec((pairs, length, LANES), lambda h: (0, 0, h + c * steps))
     return pl.pallas_call(
         self_forward_kernel,
         out_shape=(
             jax.ShapeDtypeStruct((pairs, length, width), bf16),
             jax.ShapeDtypeStruct((pairs, length, width), f32),
         ),
-        grid=(pairs, steps),
+        grid=(steps,),
         in_specs=[
             part(0),
             part(1),
             part(2),
-            pl.BlockSpec((2, length, length), lambda p, h: (h, 0, 0)),
+            pl.BlockSpec((2, length, length), lambda h: (h, 0, 0)),
         ],
         out_specs=[part(0), part(0)],
         cost_estimate=cost(
@@ -119,37 +120,35 @@
 def self_backward_kernel(
     q_ref, k_ref, v_ref, bias_ref, total_ref, grad_ref, grads_ref, diagonal_ref, sum_ref
 ):
-    p, hp = pl.program_id(0), pl.program_id(1)
-    steps = pl.num_programs(1)
-    length, padded = q_ref.shape[1], sum_ref.shape[-1]
-    q, grad, k = stack_heads(q_ref[0]), stack_heads(grad_ref[0]), k_ref[0]
-
-    @pl.when(p == 0)
+    hp, steps = pl.program_id(0), pl.num_programs(0)
+    pairs, length, _ = q_ref.shape
+    padded = sum_ref.shape[-1]
+    bias = bias_ref[...].reshape(2 * length, length).astype(f32)
+
+    @pl.when(hp == 0)
     def _():
-        sum_ref[hp] = jnp.zeros(sum_ref.shape[1:], f32)
-
-    bias = bias_ref[...].reshape(2 * length, length).astype(f32)
-    scores = dot(q, k, NT) + bias
-    probs, grad_scores = attend_back(scores, total_ref[0], grad, v_ref[0])
-    sum_ref[hp, :, :, :length] += grad_scores.astype(f32).reshape(2, length, length)
-    found = join_heads(dot(grad_scores, k, NN)), dot(grad_scores, q, TN), dot(probs, grad, TN)
-    for c in range(3):
-        grads_ref[0, :, pl.ds(pl.multiple_of((hp + c * steps) * LANES, LANES), LANES)] = found[
-            c
-        ].astype(bf16)
-
-    @pl.when(p == pl.num_programs(0) - 1)
-    def _():
-        rows = lax.broadcasted_iota(jnp.int32, (8, padded), 0)
-        for h in range(2):
-            held = sum_ref[hp, h, 0:8, :]
-            for i in range(8, length, 8):
-                held = held + pltpu.roll(sum_ref[hp, h, i : i + 8, :], padded - i, 1)
-            for bit in (1, 2, 4):
-                held = jnp.where(
-                    (rows // bit) % 2 == 1, pltpu.roll(held, padded - bit, 1), held
-                )
-            diagonal_ref[0, h] = held
+        sum_ref[...] = jnp.zeros(sum_ref.shape, f32)
+
+    summed = 0.0
+    for p in range(pairs):
+        q, grad, k = stack_heads(q_ref[p]), stack_heads(grad_ref[p]), k_ref[p]
+        scores = dot(q, k, NT) + bias
+        probs, grad_scores = attend_back(scores, total_ref[p], grad, v_ref[p])
+        summed = summed + grad_scores.astype(f32)
+        found = join_heads(dot(grad_scores, k, NN)), dot(grad_scores, q, TN), dot(probs, grad, TN)
+        for c in range(3):
+            at = pl.ds(pl.multiple_of((hp + c * steps) * LANES, LANES), LANES)
+            grads_ref[p, :, at] = found[c].astype(bf16)
+    sum_ref[:, :, :length] = summed.reshape(2, length, length)
+
+    rows = lax.broadcasted_iota(jnp.int32, (8, padded), 0)
+    for h in range(2):
+        held = sum_ref[h, 0:8, :]
+        for i in range(8, length, 8):
+            held = held + pltpu.roll(sum_ref[h, i : i + 8, :], padded - i, 1)
+        for bit in (1, 2, 4):
+            held = jnp.where((rows // bit) % 2 == 1, pltpu.roll(held, padded - bit, 1), held)
+        diagonal_ref[0, h] = held
 
 
 def self_backward(qkv, bias, total, grad):
@@ -157,27 +156,27 @@
     width //= 3
     steps = width // LANES
     padded = -(-length // LANES) * LANES
-    part = lambda c: pl.BlockSpec((1, length, LANES), lambda p, h: (p, 0, h + c * steps))
+    part = lambda c: pl.BlockSpec((pairs, length, LANES), lambda h: (0, 0, h + c * steps))
     return pl.pallas_call(
         self_backward_kernel,
         out_shape=(
             jax.ShapeDtypeStruct(qkv.shape, bf16),
             jax.ShapeDtypeStruct((steps, 2, 8, padded), f32),
         ),
-        grid=(pairs, steps),
+        grid=(steps,),
         in_specs=[
             part(0),
             part(1),
             part(2),
-            pl.BlockSpec((2, length, length), lambda p, h: (h, 0, 0)),
+            pl.BlockSpec((2, length, length), lambda h: (h, 0, 0)),
             part(0),
             part(0),
         ],
         out_specs=[
-            pl.BlockSpec((1, length, 3 * width), lambda p, h: (p, 0, 0)),
-            pl.BlockSpec((1, 2, 8, padded), lambda p, h: (h, 0, 0, 0)),
+            pl.BlockSpec((pairs, length, 3 * width), lambda h: (0, 0, 0)),
+            pl.BlockSpec((1, 2, 8, padded), lambda h: (h, 0, 0, 0)),
         ],
-        scratch_shapes=[pltpu.VMEM((steps, 2, length, padded), f32)],
+        scratch_shapes=[pltpu.VMEM((2, length, padded), f32)],
         cost_estimate=cost(
             flops=pairs * HEADS * length * length * HEAD_DIM * 10,
             transcendentals=pairs * HEADS * length * length,
@@ -1009,13 +1008,13 @@
         middle_keep, middle_send = middle_sum.to_wide(middle_one, middle_two, halved=True)
         grads_one, middle_send = tie(grads_one, middle_send)
         middle_come = cube.swap(middle_send, 1)
+    if stepped:
+        last_send = last_sum.to_x(last_one)
+        grads_one, *last_send = tie(grads_one, *last_send)
+        last_two = last_sum.swap(last_send, 16)
     grad_normed_one = dot(grads_one, w_qkv, NT)
     _, norm_one = jax.vjp(rms_norm, inputs, gain_one)
     back_one, d_gain_one = norm_one(grad_normed_one)
-    if stepped:
-        last_one[0], d_gain_one = tie(last_one[0], d_gain_one)
-        last_send = last_sum.to_x(last_one)
-        last_two = last_sum.swap(last_send, 16)
     grad_targets = (grad_first + back_one).reshape(pairs, length, width)
     if stepped:
         last_two[0], middle_come, grad_memory, grad_targets = tie(

time: 469 us -> 466 us (level)
  waiting for transfers between devices: 118 us -> 128 us
  Pallas kernels: 198 us -> 191 us
    ppermute x24, waiting for transfers between devices: 102 us -> 108 us  [swap(): return lax.ppermute(value, BOTH, pairs)]
    pallas_call x1, Pallas kernels: 22.5 us -> 17.7 us  [self_backward(): pl.pallas_call(self_backward_kernel, out_shape=(jax.ShapeDtypeStruct(qkv....]
  transfers between devices with their start and end apart: 29 -> 29, of which waited for: 16 -> 17; matrix products, arithmetic and copies ran while one was open for 17% -> 16% of each run, Pallas kernels for 36% -> 35%
where the time goes in v5:
time: 466 us; the launch traced here: 460 us
  Pallas kernels  191 us (41%)
  waiting for transfers between devices  128 us (27%)
  matrix products  50.1 us (11%)
  starting transfers between devices  42 us (9%)
  local copies, waits for them, and re-layouts  20.2 us (4%)
  between operations  14.5 us (3%)
  other arithmetic  14.1 us (3%)
    ppermute x24, waiting for transfers between devices, swap(): return lax.ppermute(value, BOTH, pairs)  108 us
    dot_general x12, matrix products, dot(): return lax.dot_general(left, right, dims, preferred_element_type=f32)  47 us
    pallas_call x2, Pallas kernels, cross_backward(): pl.pallas_call(functools.partial(cross_backward_kernel, pair, last), out_...  44.2 us
    pallas_call x2, Pallas kernels, cross_forward(): pl.pallas_call(functools.partial(cross_forward_kernel, pair), out_shape=(...  33.6 us
    ppermute x24, starting transfers between devices, swap(): return lax.ppermute(value, BOTH, pairs)  31.5 us
    pallas_call x1, Pallas kernels, feed_forward(): pl.pallas_call(functools.partial(feed_forward_kernel, own), out_shape=(ja...  26.5 us
    pallas_call x6, Pallas kernels, message(): pl.pallas_call(kernel, out_shape=out_shape, grid_spec=pltpu.PrefetchScala...  23.7 us
    pallas_call x6, Pallas kernels, merge_two(): pl.pallas_call(kernel, out_shape=jax.ShapeDtypeStruct((a, 2, rows, n), bf...  20.5 us
  transfers between devices with their start and end apart: 29, of which 17 were waited for; matrix products, arithmetic and copies ran while one was open for 16% of the time, Pallas kernels for 35%

profile of v5, /device:TPU:0, one launch (start us, length us, event | category | flops | bytes accessed | tf_op | source)
XLA Modules:
  0.0 459.8 jit_solution(478407401822063310)
XLA Ops:
  11.5 5.1 %collective-permute-start.2 = (bf16[24,3072]{1,0:T(8,128)(2,1)}, bf16[24,3072]{1,0:T(8,128)(2,1)}, u32[]{:S(2)}, u32[]{:S(2)}) collective-permute-start(bf16[24,3072]{1,0:T(8,128)(2,1)} %get-tuple-element.90.refs_0_), channel_id=1, source_target_pairs={{0,6},{1,7},{2,4},{3,5},{4,2},{5,3},{6,0},{7,1},{8,14},{9,15},{10,... | collective-permute-start | bytes 442376 | tf_op jit(solution)/shard_map/ppermute | solution.py:528
  21.7 9.3 %collective-permute-done.1.refs_2_ = bf16[24,3072]{1,0:T(8,128)(2,1)} collective-permute-done((bf16[24,3072]{1,0:T(8,128)(2,1)}, bf16[24,3072]{1,0:T(8,128)(2,1)}, u32[]{:S(2)}, u32[]{:S(2)}) %collective-permute-start.1) | collective-permute-done | bytes 147488 | tf_op jit(solution)/shard_map/ppermute | solution.py:528
  46.4 12.8 %collective-permute-done.5.come_ref = bf16[1,192,1536]{2,1,0:T(8,128)(2,1)S(1)} collective-permute-done((bf16[1,192,1536]{2,1,0:T(8,128)(2,1)}, bf16[1,192,1536]{2,1,0:T(8,128)(2,1)S(1)}, u32[]{:S(2)}, u32[]{:S(2)}) %collective-permute-start.5) | collective-permute-done | bytes 589856 | tf_op jit(solution)/shard_map/ppermute | solution.py:528
  62.2 5.5 %all-to-all-start = ((bf16[16,128,768]{2,1,0:T(8,128)(2,1)}), bf16[16,128,768]{2,1,0:T(8,128)(2,1)S(1)}, u32[]{:S(2)}, u32[]{:S(2)}) async-start(bf16[16,128,768]{2,1,0:T(8,128)(2,1)} %param.22), calls=%async_computation | async-start | bytes 6291456 | tf_op jit(solution)/shard_map/all_to_all | solution.py:884
  74.7 32.5 %collective-permute-done.6.come_ref = bf16[8,24,1536]{2,1,0:T(8,128)(2,1)} collective-permute-done((bf16[8,24,1536]{2,1,0:T(8,128)(2,1)}, bf16[8,24,1536]{2,1,0:T(8,128)(2,1)}, u32[]{:S(2)}, u32[]{:S(2)}) %collective-permute-start.6) | collective-permute-done | bytes 589856 | tf_op jit(solution)/shard_map/ppermute | solution.py:528
  107.2 5.3 %merge_two.9 = bf16[8,2,24,1536]{3,2,1,0:T(8,128)(2,1)} custom-call(s32[1]{0:T(128)} %bitcast.5.side_ref, bf16[8,24,1536]{2,1,0:T(8,128)(2,1)} %bitcast.126, bf16[8,24,1536]{2,1,0:T(8,128)(2,1)} %collective-permute-done.6.come_ref), custom_call_target="tpu_custom_call" | custom-call | bytes 294912 | tf_op jit(solution)/shard_map/merge_two/pallas_call | solution.py:574
  113.0 7.4 %copy.60 = bf16[768,3200]{0,1:T(8,128)(2,1)} copy(bf16[768,3200]{1,0:T(8,128)(2,1)} %all-gather.3.cloned.1.call-done) | data formatting | bytes 9830400 | tf_op jit(solution)/shard_map/optimization_barrier | solution.py:796
  121.7 6.2 %convolution_convert_fusion = bf16[576,2304]{1,0:T(8,128)(2,1)} fusion(bf16[768,3200]{1,0:T(8,128)(2,1)} %all-gather.3.cloned.1.call-done, f32[768]{0:T(1024)S(1)} %get-tuple-element.201, f32[576]{0:T(1024)S(1)} %rsqrt.25, bf16[576,768]{1,0:T(8,128)(2,1)} %bitcast.118), kind=kOutput, calls=%fused_computation.6 | convolution fusion | flops 2041528320 | bytes 7083264 | tf_op jit(solution)/shard_map/dot_general | solution.py:38
  127.9 8.8 %self_forward.1 = (bf16[2,288,768]{2,1,0:T(8,128)(2,1)}, f32[2,288,768]{2,1,0:T(8,128)}) custom-call(bf16[2,288,2304]{2,1,0:T(8,128)(2,1)} %bitcast.69, bf16[2,288,2304]{2,1,0:T(8,128)(2,1)} %bitcast.70, bf16[2,288,2304]{2,1,0:T(8,128)(2,1)} %bitcast.71, bf16[12,288,288]{2,1,0:T(8,128)(2,1)} %fusion.6.bias_ref), custom_call_target="tpu_custom_call" | custom-call | flops 63700992 | bytes 663552 | tf_op jit(solution)/shard_map/self_forward/pallas_call | solution.py:97
  136.8 3.9 multiply_reduce_fusion.4
  140.7 3.9 merge_two.10
  144.6 3.9 merge_two.11
  153.9 16.7 %cross_forward.2 = (bf16[2,288,768]{2,1,0:T(8,128)(2,1)}, f32[2,288,768]{2,1,0:T(8,128)}, bf16[2,1024,768]{2,1,0:T(8,128)(2,1)}, bf16[2,1024,768]{2,1,0:T(8,128)(2,1)}) custom-call(s32[2]{0:T(128)} %len_ref.7, bf16[2,288,768]{2,1,0:T(8,128)(2,1)} %bitcast.94, bf16[8,2,128,768]{3,2,1,0:T(8,128)(2,1)} %bitcast.75, bf16[768,1536]{1,0:T(8,128)(2,1)} %bitcast.86, ...), custom_call_target="tpu_custom_call" | custom-call | flops 415236096 | bytes 811008 | tf_op jit(solution)/shard_map/cross_forward/pallas_call | solution.py:213
  170.6 16.8 %cross_forward.3 = (bf16[2,288,768]{2,1,0:T(8,128)(2,1)}, f32[2,288,768]{2,1,0:T(8,128)}, bf16[2,1024,768]{2,1,0:T(8,128)(2,1)}, bf16[2,1024,768]{2,1,0:T(8,128)(2,1)}) custom-call(s32[2]{0:T(128)} %len_ref.7, bf16[2,288,768]{2,1,0:T(8,128)(2,1)} %bitcast.95, ...), custom_call_target="tpu_custom_call", output_to_operand_aliasing={{0}: (5, {}), {1}: (6, {}), {2}: (7, {}), {3}: (8, {})} | custom-call | flops 415236096 | bytes 811008 | tf_op jit(solution)/shard_map/cross_forward/pallas_call | solution.py:213
  187.5 3.9 convolution_add_fusion.second_ref
  191.3 19.1 %all-gather.5.cloned.1.call-done.down_ref.gate_low_ref.gate_high_ref.up_low_ref.up_high_ref = bf16[768,6400]{1,0:T(8,128)(2,1)} async-done(((bf16[24,6400]{1,0:T(8,128)(2,1)}), bf16[768,6400]{1,0:T(8,128)(2,1)}) %all-gather.5.cloned.1.call-update) | async-done | bytes 9830416 | tf_op jit(solution)/shard_map/all_gather | solution.py:888
  210.4 26.5 %feed_forward.1 = (bf16[576,768]{1,0:T(8,128)(2,1)}, f32[576,768]{1,0:T(8,128)}, f32[1,768]{1,0:T(1,128)}, bf16[768,6400]{1,0:T(8,128)(2,1)}) custom-call(f32[576,768]{1,0:T(8,128)} %convolution_add_fusion.second_ref, f32[1,768]{1,0:T(1,128)} %get-tuple-element.213.gain_ref, f32[576,1]{1,0:T(8,128)} %reshape.415.live_ref, bf16[576,768]{1,0:T(8,128)(2,1)} %bitcast.131, ...), custom_call_target="tpu_custom_call" | custom-call | flops 2038431744 | bytes 3342336 | tf_op jit(solution)/shard_map/feed_forward/pallas_call | solution.py:473
  240.9 19.5 %cross_backward.2 = (bf16[2,288,768]{2,1,0:T(8,128)(2,1)}, bf16[8,2,128,768]{3,2,1,0:T(8,128)(2,1)}, bf16[1024,1536]{1,0:T(8,128)(2,1)}) custom-call(s32[2]{0:T(128)} %len_ref.7, bf16[2,288,768]{2,1,0:T(8,128)(2,1)} %bitcast.96, bf16[2,1024,768]{2,1,0:T(8,128)(2,1)} %get-tuple-element.111.k_ref, bf16[2,1024,768]{2,1,0:T(8,128)(2,1)} %get-tuple-element.112.v_ref, ...), custom_call_target="tpu_custom_call" | custom-call | flops 887095296 | bytes 1062912 | tf_op jit(solution)/shard_map/cross_backward/pallas_call | solution.py:313
  260.3 24.8 %cross_backward.3 = (bf16[2,288,768]{2,1,0:T(8,128)(2,1)}, bf16[8,2,128,768]{3,2,1,0:T(8,128)(2,1)}, bf16[768,768]{1,0:T(8,128)(2,1)}, bf16[768,768]{1,0:T(8,128)(2,1)}) custom-call(s32[2]{0:T(128)} %len_ref.7, bf16[2,288,768]{2,1,0:T(8,128)(2,1)} %bitcast.97, ...), custom_call_target="tpu_custom_call", output_to_operand_aliasing={{0}: (10, {}), {1}: (11, {})} | custom-call | flops 887095296 | bytes 1062912 | tf_op jit(solution)/shard_map/cross_backward/pallas_call | solution.py:313
  296.1 4.9 %message.6 = bf16[2,192,3840]{2,1,0:T(8,128)(2,1)} custom-call(s32[3]{0:T(128)} %pad_add_fusion.sides_ref, bf16[2,2,192,768]{3,2,1,0:T(8,128)(2,1)} %bitcast.111, bf16[2,2,192,768]{3,2,1,0:T(8,128)(2,1)} %bitcast.99, bf16[2,2,192,768]{3,2,1,0:T(8,128)(2,1)} %bitcast.102, bf16[2,2,192,768]{3,2,1,0:T(8,128)(2,1)} %bitcast.105, bf16[2,2,192,768]{3,2,1,0:T(8,128)(2,1)} %bitcast.108), custom_call_target="tpu_custom_call" | custom-call | flops 184320 | bytes 737280 | tf_op jit(solution)/shard_map/message/pallas_call | solution.py:707
  301.2 4.4 all-to-all-start.1
  305.6 3.7 convolution_convert_fusion.4
  313.9 17.7 %self_backward.1 = (bf16[2,288,2304]{2,1,0:T(8,128)(2,1)}, f32[6,2,8,384]{3,2,1,0:T(8,128)}) custom-call(bf16[2,288,2304]{2,1,0:T(8,128)(2,1)} %bitcast.72, bf16[2,288,2304]{2,1,0:T(8,128)(2,1)} %bitcast.73, bf16[2,288,2304]{2,1,0:T(8,128)(2,1)} %bitcast.74, bf16[12,288,288]{2,1,0:T(8,128)(2,1)} %fusion.6.bias_ref, ...), custom_call_target="tpu_custom_call" | custom-call | flops 159252480 | bytes 995328 | tf_op jit(solution)/shard_map/self_backward/pallas_call | solution.py:160
  331.7 6.9 %bitcast_convert_fusion = bf16[768,2304]{1,0:T(8,128)(2,1)} fusion(bf16[2,288,2304]{2,1,0:T(8,128)(2,1)} %get-tuple-element.121, f32[768]{0:T(1024)S(1)} %get-tuple-element.201, f32[2,288]{1,0:T(2,128)S(1)} %get-tuple-element.214, bf16[2,288,768]{2,1,0:T(8,128)(2,1)} %param.21), kind=kOutput, calls=%fused_computation.2 | convolution fusion | flops 2041970688 | bytes 7083264 | tf_op jit(solution)/shard_map/dot_general | solution.py:38
  338.5 4.5 message.8
  343.0 11.5 %collective-permute-done.10.refs_6_ = bf16[1,192,3840]{2,1,0:T(8,128)(2,1)} collective-permute-done((bf16[1,192,3840]{2,1,0:T(8,128)(2,1)}, bf16[1,192,3840]{2,1,0:T(8,128)(2,1)}, u32[]{:S(2)}, u32[]{:S(2)}) %collective-permute-start.10) | collective-permute-done | bytes 1474592 | tf_op jit(solution)/shard_map/ppermute | solution.py:528
  354.6 4.4 message.9
  365.3 5.9 %multiply_reduce_fusion.1 = (f32[768]{0:T(1024)S(1)}, f32[576]{0:T(1024)S(1)}, f32[576,768]{1,0:T(8,128)S(1)}) fusion(f32[576]{0:T(1024)S(1)} %rsqrt.25, bf16[2,288,768]{2,1,0:T(8,128)(2,1)} %param.21, f32[768]{0:T(1024)S(1)} %get-tuple-element.201, bf16[576,2304]{1,0:T(8,128)(2,1)} %bitcast.140, bf16[768,3200]{1,0:T(8,128)(2,1)} %all-gather.3.cloned.1.call-done, ...), kind=kOutput, calls=%fused_computation.16 | convolution fusion | flops 2041969408 | bytes 9742848 | tf_op jit(solution)/shard_map/dot_general | solution.py:38
  375.9 15.9 %collective-permute-done.15 = f32[24,128]{1,0:T(8,128)S(1)} collective-permute-done((f32[24,128]{1,0:T(8,128)S(1)}, f32[24,128]{1,0:T(8,128)S(1)}, u32[]{:S(2)}, u32[]{:S(2)}) %collective-permute-start.15) | collective-permute-done | bytes 12320 | tf_op jit(solution)/shard_map/ppermute | solution.py:528
  403.5 9.2 %collective-permute-done.16.refs_1_ = bf16[4,24,2304]{2,1,0:T(8,128)(2,1)} collective-permute-done((bf16[4,24,2304]{2,1,0:T(8,128)(2,1)}, bf16[4,24,2304]{2,1,0:T(8,128)(2,1)}, u32[]{:S(2)}, u32[]{:S(2)}) %collective-permute-start.16) | collective-permute-done | bytes 442400 | tf_op jit(solution)/shard_map/ppermute | solution.py:528
  418.8 5.9 %collective-permute-start.20 = (bf16[1,24,3840]{2,1,0:T(8,128)(2,1)}, bf16[1,24,3840]{2,1,0:T(8,128)(2,1)S(1)}, u32[]{:S(2)}, u32[]{:S(2)}) collective-permute-start(bf16[1,24,3840]{2,1,0:T(8,128)(2,1)} %get-tuple-element.152), channel_id=1, source_target_pairs={{0,4},{1,5},{2,6},{3,7},{4,0},{5,1},{6,2},{7,3},{8,12},{9,13},{10,... | collective-permute-start | bytes 552968 | tf_op jit(solution)/shard_map/ppermute | solution.py:528
  424.6 3.7 collective-permute-done.21
  (154 shorter events, 114.8 us)
Async XLA Ops:
  7.2 105.3 %all-gather.3.cloned.1.call-start = ((), (), s32[]{:S(2)}) async-start(), calls=%async_computation.3 | async-start | bytes 5068800 | tf_op jit(solution)/shard_map/all_gather | solution.py:887
  10.7 199.7 %all-gather.5.cloned.1.call-start = ((), (), s32[]{:S(2)}) async-start(), calls=%async_computation.4 | async-start | bytes 10137600 | tf_op jit(solution)/shard_map/all_gather | solution.py:888
  11.5 10.2 %collective-permute-start.2 = (bf16[24,3072]{1,0:T(8,128)(2,1)}, bf16[24,3072]{1,0:T(8,128)(2,1)}, u32[]{:S(2)}, u32[]{:S(2)}) collective-permute-start(bf16[24,3072]{1,0:T(8,128)(2,1)} %get-tuple-element.90.refs_0_), channel_id=1, source_target_pairs={{0,6},{1,7},{2,4},{3,5},{4,2},{5,3},{6,0},{7,1},{8,14},{9,15},{10,... | collective-permute-start | bytes 442376 | tf_op jit(solution)/shard_map/ppermute | solution.py:528
  16.6 14.4 %collective-permute-start.1 = (bf16[24,3072]{1,0:T(8,128)(2,1)}, bf16[24,3072]{1,0:T(8,128)(2,1)}, u32[]{:S(2)}, u32[]{:S(2)}) collective-permute-start(bf16[24,3072]{1,0:T(8,128)(2,1)} %get-tuple-element.90.refs_0_), channel_id=1, source_target_pairs={{0,4},{1,5},{2,6},{3,7},{4,0},{5,1},{6,2},{7,3},{8,12},{9,13},{10,... | collective-permute-start | bytes 442376 | tf_op jit(solution)/shard_map/ppermute | solution.py:528
  16.6 14.4 %collective-permute-start = (bf16[24,3072]{1,0:T(8,128)(2,1)}, bf16[24,3072]{1,0:T(8,128)(2,1)}, u32[]{:S(2)}, u32[]{:S(2)}) collective-permute-start(bf16[24,3072]{1,0:T(8,128)(2,1)} %get-tuple-element.90.refs_0_), channel_id=1, source_target_pairs={{0,2},{1,3},{2,0},{3,1},{4,6},{5,7},{6,4},{7,5},{8,10},{9,11},{10,... | collective-permute-start | bytes 442376 | tf_op jit(solution)/shard_map/ppermute | solution.py:528
  33.0 7.9 %collective-permute-start.4 = (bf16[1,96,1536]{2,1,0:T(8,128)(2,1)}, bf16[1,96,1536]{2,1,0:T(8,128)(2,1)}, u32[]{:S(2)}, u32[]{:S(2)}) collective-permute-start(bf16[1,96,1536]{2,1,0:T(8,128)(2,1)} %bitcast.134), channel_id=1, source_target_pairs={{0,16},{1,17},{2,18},{3,19},{4,20},{5,21},{6,22},{7,23},{8,24},{9,... | collective-permute-start | bytes 884744 | tf_op jit(solution)/shard_map/ppermute | solution.py:528
  34.6 8.6 %collective-permute-start.3 = (bf16[4,24,1536]{2,1,0:T(8,128)(2,1)}, bf16[4,24,1536]{2,1,0:T(8,128)(2,1)}, u32[]{:S(2)}, u32[]{:S(2)}) collective-permute-start(bf16[4,24,1536]{2,1,0:T(8,128)(2,1)} %get-tuple-element.91.mine_ref), channel_id=1, source_target_pairs={{0,1},{1,0},{2,3},{3,2},{4,5},{5,4},{6,7},{7,6},{8,9},{9,8},{10,11... | collective-permute-start | bytes 884744 | tf_op jit(solution)/shard_map/ppermute | solution.py:528
  46.4 12.8 %collective-permute-start.5 = (bf16[1,192,1536]{2,1,0:T(8,128)(2,1)}, bf16[1,192,1536]{2,1,0:T(8,128)(2,1)S(1)}, u32[]{:S(2)}, u32[]{:S(2)}) collective-permute-start(bf16[1,192,1536]{2,1,0:T(8,128)(2,1)} %bitcast.127), channel_id=1, source_target_pairs={{0,16},{1,17},{2,18},{3,19},{4,20},{5,21},{6,22},{7,23},{8,24},{9,... | collective-permute-start | bytes 1769480 | tf_op jit(solution)/shard_map/ppermute | solution.py:528
  62.2 90.0 %all-to-all-start = ((bf16[16,128,768]{2,1,0:T(8,128)(2,1)}), bf16[16,128,768]{2,1,0:T(8,128)(2,1)S(1)}, u32[]{:S(2)}, u32[]{:S(2)}) async-start(bf16[16,128,768]{2,1,0:T(8,128)(2,1)} %param.22), calls=%async_computation | async-start | bytes 6291456 | tf_op jit(solution)/shard_map/all_to_all | solution.py:884
  67.7 378.5 %reduce-scatter.2.cloned.1.call-start = ((), (), s32[]{:S(2)}) async-start(), calls=%async_computation.5 | async-start | bytes 10137600 | tf_op jit(solution)/shard_map/reduce_scatter | solution.py:960
  70.2 37.0 %collective-permute-start.6 = (bf16[8,24,1536]{2,1,0:T(8,128)(2,1)}, bf16[8,24,1536]{2,1,0:T(8,128)(2,1)}, u32[]{:S(2)}, u32[]{:S(2)}) collective-permute-start(bf16[8,24,1536]{2,1,0:T(8,128)(2,1)} %bitcast.125), channel_id=1, source_target_pairs={{0,1},{1,0},{2,3},{3,2},{4,5},{5,4},{6,7},{7,6},{8,9},{9,8},{10,11... | collective-permute-start | bytes 1769480 | tf_op jit(solution)/shard_map/ppermute | solution.py:528
  112.5 28.2 %collective-permute-start.7 = (bf16[2,192,1536]{2,1,0:T(8,128)(2,1)}, bf16[2,192,1536]{2,1,0:T(8,128)(2,1)}, u32[]{:S(2)}, u32[]{:S(2)}) collective-permute-start(bf16[2,192,1536]{2,1,0:T(8,128)(2,1)} %bitcast.114), channel_id=1, source_target_pairs={{0,8},{1,9},{2,10},{3,11},{4,12},{5,13},{6,14},{7,15},{8,0},{9,1},... | collective-permute-start | bytes 3538952 | tf_op jit(solution)/shard_map/ppermute | solution.py:528
  112.5 32.1 %collective-permute-start.8 = (bf16[2,192,1536]{2,1,0:T(8,128)(2,1)}, bf16[2,192,1536]{2,1,0:T(8,128)(2,1)}, u32[]{:S(2)}, u32[]{:S(2)}) collective-permute-start(bf16[2,192,1536]{2,1,0:T(8,128)(2,1)} %bitcast.116), channel_id=1, source_target_pairs={{0,8},{1,9},{2,10},{3,11},{4,12},{5,13},{6,14},{7,15},{8,0},{9,1},... | collective-permute-start | bytes 3538952 | tf_op jit(solution)/shard_map/ppermute | solution.py:528
  170.6 16.9 %copy-start.3 = (bf16[2,2,192,1536]{3,2,1,0:T(8,128)(2,1)S(1)}, bf16[2,2,192,1536]{3,2,1,0:T(8,128)(2,1)}, u32[]{:S(2)}) copy-start(bf16[2,2,192,1536]{3,2,1,0:T(8,128)(2,1)} %merge_two.11) | copy-start | bytes 7077892
  260.3 24.8 %copy-start.4 = (bf16[2,2,192,1536]{3,2,1,0:T(8,128)(2,1)S(1)}, bf16[2,2,192,1536]{3,2,1,0:T(8,128)(2,1)}, u32[]{:S(2)}) copy-start(bf16[2,2,192,1536]{3,2,1,0:T(8,128)(2,1)} %merge_two.10) | copy-start | bytes 7077892
  301.0 8.3 %collective-permute-start.9 = (bf16[2,192,3840]{2,1,0:T(8,128)(2,1)}, bf16[2,192,3840]{2,1,0:T(8,128)(2,1)}, u32[]{:S(2)}, u32[]{:S(2)}) collective-permute-start(bf16[2,192,3840]{2,1,0:T(8,128)(2,1)} %message.6), channel_id=1, source_target_pairs={{0,8},{1,9},{2,10},{3,11},{4,12},{5,13},{6,14},{7,15},{8,0},{9,1},... | collective-permute-start | bytes 8847368 | tf_op jit(solution)/shard_map/ppermute | solution.py:528
  301.2 94.0 %all-to-all-start.1 = ((bf16[16,128,768]{2,1,0:T(8,128)(2,1)}), bf16[16,128,768]{2,1,0:T(8,128)(2,1)S(1)}, u32[]{:S(2)}, u32[]{:S(2)}) async-start(bf16[16,128,768]{2,1,0:T(8,128)(2,1)} %bitcast.98), calls=%async_computation.1 | async-start | bytes 6291456 | tf_op jit(solution)/shard_map/all_to_all | solution.py:884
  312.9 41.6 %collective-permute-start.10 = (bf16[1,192,3840]{2,1,0:T(8,128)(2,1)}, bf16[1,192,3840]{2,1,0:T(8,128)(2,1)}, u32[]{:S(2)}, u32[]{:S(2)}) collective-permute-start(bf16[1,192,3840]{2,1,0:T(8,128)(2,1)} %message.7), channel_id=1, source_target_pairs={{0,16},{1,17},{2,18},{3,19},{4,20},{5,21},{6,22},{7,23},{8,24},{9,... | collective-permute-start | bytes 4423688 | tf_op jit(solution)/shard_map/ppermute | solution.py:528
  354.5 7.6 %collective-permute-start.11 = (bf16[2,192,2304]{2,1,0:T(8,128)(2,1)}, bf16[2,192,2304]{2,1,0:T(8,128)(2,1)}, u32[]{:S(2)}, u32[]{:S(2)}) collective-permute-start(bf16[2,192,2304]{2,1,0:T(8,128)(2,1)} %message.8), channel_id=1, source_target_pairs={{0,8},{1,9},{2,10},{3,11},{4,12},{5,13},{6,14},{7,15},{8,0},{9,1},... | collective-permute-start | bytes 5308424 | tf_op jit(solution)/shard_map/ppermute | solution.py:528
  359.6 35.6 %collective-permute-start.13 = (bf16[4,24,3840]{2,1,0:T(8,128)(2,1)}, bf16[4,24,3840]{2,1,0:T(8,128)(2,1)}, u32[]{:S(2)}, u32[]{:S(2)}) collective-permute-start(bf16[4,24,3840]{2,1,0:T(8,128)(2,1)} %get-tuple-element.130), channel_id=1, source_target_pairs={{0,1},{1,0},{2,3},{3,2},{4,5},{5,4},{6,7},{7,6},{8,9},{9,8},{10,11... | collective-permute-start | bytes 2211848 | tf_op jit(solution)/shard_map/ppermute | solution.py:528
  365.1 30.1 %collective-permute-start.12 = (bf16[1,192,2304]{2,1,0:T(8,128)(2,1)}, bf16[1,192,2304]{2,1,0:T(8,128)(2,1)}, u32[]{:S(2)}, u32[]{:S(2)}) collective-permute-start(bf16[1,192,2304]{2,1,0:T(8,128)(2,1)} %message.10), channel_id=1, source_target_pairs={{0,16},{1,17},{2,18},{3,19},{4,20},{5,21},{6,22},{7,23},{8,24},{9,... | collective-permute-start | bytes 2654216 | tf_op jit(solution)/shard_map/ppermute | solution.py:528
  371.2 1.2 collective-permute-start.14
  372.4 19.3 %collective-permute-start.15 = (f32[24,128]{1,0:T(8,128)S(1)}, f32[24,128]{1,0:T(8,128)S(1)}, u32[]{:S(2)}, u32[]{:S(2)}) collective-permute-start(f32[24,128]{1,0:T(8,128)S(1)} %pad_add_fusion.1), channel_id=1, source_target_pairs={{0,16},{1,17},{2,18},{3,19},{4,20},{5,21},{6,22},{7,23},{8,24},{9,... | collective-permute-start | bytes 36872 | tf_op jit(solution)/shard_map/ppermute | solution.py:528
  398.6 14.1 %collective-permute-start.16 = (bf16[4,24,2304]{2,1,0:T(8,128)(2,1)}, bf16[4,24,2304]{2,1,0:T(8,128)(2,1)}, u32[]{:S(2)}, u32[]{:S(2)}) collective-permute-start(bf16[4,24,2304]{2,1,0:T(8,128)(2,1)} %get-tuple-element.140), channel_id=1, source_target_pairs={{0,1},{1,0},{2,3},{3,2},{4,5},{5,4},{6,7},{7,6},{8,9},{9,8},{10,11... | collective-permute-start | bytes 1327112 | tf_op jit(solution)/shard_map/ppermute | solution.py:528
  403.5 12.6 %collective-permute-start.19 = (bf16[2,24,3840]{2,1,0:T(8,128)(2,1)}, bf16[2,24,3840]{2,1,0:T(8,128)(2,1)S(1)}, u32[]{:S(2)}, u32[]{:S(2)}) collective-permute-start(bf16[2,24,3840]{2,1,0:T(8,128)(2,1)} %get-tuple-element.150), channel_id=1, source_target_pairs={{0,2},{1,3},{2,0},{3,1},{4,6},{5,7},{6,4},{7,5},{8,10},{9,11},{10,... | collective-permute-start | bytes 1105928 | tf_op jit(solution)/shard_map/ppermute | solution.py:528
  414.8 23.9 %collective-permute-start.17 = (bf16[2,24,2304]{2,1,0:T(8,128)(2,1)}, bf16[2,24,2304]{2,1,0:T(8,128)(2,1)}, u32[]{:S(2)}, u32[]{:S(2)}) collective-permute-start(bf16[2,24,2304]{2,1,0:T(8,128)(2,1)} %get-tuple-element.142), channel_id=1, source_target_pairs={{0,2},{1,3},{2,0},{3,1},{4,6},{5,7},{6,4},{7,5},{8,10},{9,11},{10,... | collective-permute-start | bytes 663560 | tf_op jit(solution)/shard_map/ppermute | solution.py:528
  418.8 23.9 %collective-permute-start.20 = (bf16[1,24,3840]{2,1,0:T(8,128)(2,1)}, bf16[1,24,3840]{2,1,0:T(8,128)(2,1)S(1)}, u32[]{:S(2)}, u32[]{:S(2)}) collective-permute-start(bf16[1,24,3840]{2,1,0:T(8,128)(2,1)} %get-tuple-element.152), channel_id=1, source_target_pairs={{0,4},{1,5},{2,6},{3,7},{4,0},{5,1},{6,2},{7,3},{8,12},{9,13},{10,... | collective-permute-start | bytes 552968 | tf_op jit(solution)/shard_map/ppermute | solution.py:528
  424.6 3.7 collective-permute-start.21
  428.3 4.8 %collective-permute-start.22 = (f32[24,128]{1,0:T(8,128)S(1)}, f32[24,128]{1,0:T(8,128)S(1)}, u32[]{:S(2)}, u32[]{:S(2)}) collective-permute-start(f32[24,128]{1,0:T(8,128)S(1)} %add.316), channel_id=1, source_target_pairs={{0,2},{1,3},{2,0},{3,1},{4,6},{5,7},{6,4},{7,5},{8,10},{9,11},{10,... | collective-permute-start | bytes 36872 | tf_op jit(solution)/shard_map/ppermute | solution.py:528
  433.1 4.6 collective-permute-start.23
  433.1 19.7 %copy-start.1 = (bf16[32,12]{0,1:T(8,128)(2,1)S(1)}, bf16[32,12]{0,1:T(8,128)(2,1)}, u32[]{:S(2)}) copy-start(bf16[32,12]{0,1:T(8,128)(2,1)} %param.40) | copy-start | bytes 2308
  440.4 5.9 %collective-permute-start.18 = (bf16[1,24,2304]{2,1,0:T(8,128)(2,1)}, bf16[1,24,2304]{2,1,0:T(8,128)(2,1)S(1)}, u32[]{:S(2)}, u32[]{:S(2)}) collective-permute-start(bf16[1,24,2304]{2,1,0:T(8,128)(2,1)} %get-tuple-element.144), channel_id=1, source_target_pairs={{0,4},{1,5},{2,6},{3,7},{4,0},{5,1},{6,2},{7,3},{8,12},{9,13},{10,... | collective-permute-start | bytes 331784 | tf_op jit(solution)/shard_map/ppermute | solution.py:528
  (18 other events, 79.8 us)
Sparse Core Ops, SparseCore 0:
  11.5 85.7 all-gather.2
  100.1 110.2 all-gather.4
  237.1 189.9 reduce-scatter.1

commit v6 on v5

--- a/solution.py
+++ b/solution.py
@@ -1048,8 +1048,8 @@
         last_come = cube.swap(last_send, 2)
         middle_grads = middle_sum.finish(middle_keep, middle_come)
         last_keep, last_send = last_sum.step(2, last_keep, last_come)
+        last_send, ff_grads = tie(last_send, ff_grads)
         last_come = cube.swap(last_send, 4)
-        last_come, ff_grads = tie(last_come, ff_grads)
         (d_qkv,) = last_sum.finish(last_keep, last_come)
     else:
         scatter = lambda value: lax.psum_scatter(

time: 466 us -> 469 us (level)
  no operation moved by 1% of the time
where the time goes in v6:
time: 469 us; the launch traced here: 463 us
  Pallas kernels  191 us (41%)
  waiting for transfers between devices  131 us (28%)
  matrix products  50.1 us (11%)
  starting transfers between devices  42 us (9%)
  local copies, waits for them, and re-layouts  20.8 us (4%)
  between operations  14.5 us (3%)
  other arithmetic  14.1 us (3%)
    ppermute x24, waiting for transfers between devices, swap(): return lax.ppermute(value, BOTH, pairs)  111 us
    dot_general x12, matrix products, dot(): return lax.dot_general(left, right, dims, preferred_element_type=f32)  47 us
    pallas_call x2, Pallas kernels, cross_backward(): pl.pallas_call(functools.partial(cross_backward_kernel, pair, last), out_...  44.2 us
    pallas_call x2, Pallas kernels, cross_forward(): pl.pallas_call(functools.partial(cross_forward_kernel, pair), out_shape=(...  33.6 us
    ppermute x24, starting transfers between devices, swap(): return lax.ppermute(value, BOTH, pairs)  31.5 us
    pallas_call x1, Pallas kernels, feed_forward(): pl.pallas_call(functools.partial(feed_forward_kernel, own), out_shape=(ja...  26.5 us
    pallas_call x6, Pallas kernels, message(): pl.pallas_call(kernel, out_shape=out_shape, grid_spec=pltpu.PrefetchScala...  23.7 us
    pallas_call x6, Pallas kernels, merge_two(): pl.pallas_call(kernel, out_shape=jax.ShapeDtypeStruct((a, 2, rows, n), bf...  20.5 us
  transfers between devices with their start and end apart: 29, of which 17 were waited for; matrix products, arithmetic and copies ran while one was open for 16% of the time, Pallas kernels for 35%

profile of v6, /device:TPU:0, one launch (start us, length us, event | category | flops | bytes accessed | tf_op | source)
XLA Modules:
  0.0 462.7 jit_solution(16464254522920875576)
XLA Ops:
  11.5 5.1 %collective-permute-start.2 = (bf16[24,3072]{1,0:T(8,128)(2,1)}, bf16[24,3072]{1,0:T(8,128)(2,1)}, u32[]{:S(2)}, u32[]{:S(2)}) collective-permute-start(bf16[24,3072]{1,0:T(8,128)(2,1)} %get-tuple-element.90.refs_0_), channel_id=1, source_target_pairs={{0,6},{1,7},{2,4},{3,5},{4,2},{5,3},{6,0},{7,1},{8,14},{9,15},{10,... | collective-permute-start | bytes 442376 | tf_op jit(solution)/shard_map/ppermute | solution.py:528
  21.7 9.3 %collective-permute-done.1.refs_2_ = bf16[24,3072]{1,0:T(8,128)(2,1)} collective-permute-done((bf16[24,3072]{1,0:T(8,128)(2,1)}, bf16[24,3072]{1,0:T(8,128)(2,1)}, u32[]{:S(2)}, u32[]{:S(2)}) %collective-permute-start.1) | collective-permute-done | bytes 147488 | tf_op jit(solution)/shard_map/ppermute | solution.py:528
  46.4 12.8 %collective-permute-done.5.come_ref = bf16[1,192,1536]{2,1,0:T(8,128)(2,1)S(1)} collective-permute-done((bf16[1,192,1536]{2,1,0:T(8,128)(2,1)}, bf16[1,192,1536]{2,1,0:T(8,128)(2,1)S(1)}, u32[]{:S(2)}, u32[]{:S(2)}) %collective-permute-start.5) | collective-permute-done | bytes 589856 | tf_op jit(solution)/shard_map/ppermute | solution.py:528
  62.2 5.5 %all-to-all-start = ((bf16[16,128,768]{2,1,0:T(8,128)(2,1)}), bf16[16,128,768]{2,1,0:T(8,128)(2,1)S(1)}, u32[]{:S(2)}, u32[]{:S(2)}) async-start(bf16[16,128,768]{2,1,0:T(8,128)(2,1)} %param.22), calls=%async_computation | async-start | bytes 6291456 | tf_op jit(solution)/shard_map/all_to_all | solution.py:884
  74.7 32.5 %collective-permute-done.6.come_ref = bf16[8,24,1536]{2,1,0:T(8,128)(2,1)} collective-permute-done((bf16[8,24,1536]{2,1,0:T(8,128)(2,1)}, bf16[8,24,1536]{2,1,0:T(8,128)(2,1)}, u32[]{:S(2)}, u32[]{:S(2)}) %collective-permute-start.6) | collective-permute-done | bytes 589856 | tf_op jit(solution)/shard_map/ppermute | solution.py:528
  107.2 5.3 %merge_two.9 = bf16[8,2,24,1536]{3,2,1,0:T(8,128)(2,1)} custom-call(s32[1]{0:T(128)} %bitcast.5.side_ref, bf16[8,24,1536]{2,1,0:T(8,128)(2,1)} %bitcast.126, bf16[8,24,1536]{2,1,0:T(8,128)(2,1)} %collective-permute-done.6.come_ref), custom_call_target="tpu_custom_call" | custom-call | bytes 294912 | tf_op jit(solution)/shard_map/merge_two/pallas_call | solution.py:574
  113.0 7.4 %copy.60 = bf16[768,3200]{0,1:T(8,128)(2,1)} copy(bf16[768,3200]{1,0:T(8,128)(2,1)} %all-gather.3.cloned.1.call-done) | data formatting | bytes 9830400 | tf_op jit(solution)/shard_map/optimization_barrier | solution.py:796
  121.7 6.2 %convolution_convert_fusion = bf16[576,2304]{1,0:T(8,128)(2,1)} fusion(bf16[768,3200]{1,0:T(8,128)(2,1)} %all-gather.3.cloned.1.call-done, f32[768]{0:T(1024)S(1)} %get-tuple-element.201, f32[576]{0:T(1024)S(1)} %rsqrt.25, bf16[576,768]{1,0:T(8,128)(2,1)} %bitcast.118), kind=kOutput, calls=%fused_computation.6 | convolution fusion | flops 2041528320 | bytes 7083264 | tf_op jit(solution)/shard_map/dot_general | solution.py:38
  127.9 8.8 %self_forward.1 = (bf16[2,288,768]{2,1,0:T(8,128)(2,1)}, f32[2,288,768]{2,1,0:T(8,128)}) custom-call(bf16[2,288,2304]{2,1,0:T(8,128)(2,1)} %bitcast.69, bf16[2,288,2304]{2,1,0:T(8,128)(2,1)} %bitcast.70, bf16[2,288,2304]{2,1,0:T(8,128)(2,1)} %bitcast.71, bf16[12,288,288]{2,1,0:T(8,128)(2,1)} %fusion.6.bias_ref), custom_call_target="tpu_custom_call" | custom-call | flops 63700992 | bytes 663552 | tf_op jit(solution)/shard_map/self_forward/pallas_call | solution.py:97
  136.8 3.9 multiply_reduce_fusion.4
  140.7 3.9 merge_two.10
  144.6 3.9 merge_two.11
  153.9 16.7 %cross_forward.2 = (bf16[2,288,768]{2,1,0:T(8,128)(2,1)}, f32[2,288,768]{2,1,0:T(8,128)}, bf16[2,1024,768]{2,1,0:T(8,128)(2,1)}, bf16[2,1024,768]{2,1,0:T(8,128)(2,1)}) custom-call(s32[2]{0:T(128)} %len_ref.7, bf16[2,288,768]{2,1,0:T(8,128)(2,1)} %bitcast.94, bf16[8,2,128,768]{3,2,1,0:T(8,128)(2,1)} %bitcast.75, bf16[768,1536]{1,0:T(8,128)(2,1)} %bitcast.86, ...), custom_call_target="tpu_custom_call" | custom-call | flops 415236096 | bytes 811008 | tf_op jit(solution)/shard_map/cross_forward/pallas_call | solution.py:213
  170.6 16.8 %cross_forward.3 = (bf16[2,288,768]{2,1,0:T(8,128)(2,1)}, f32[2,288,768]{2,1,0:T(8,128)}, bf16[2,1024,768]{2,1,0:T(8,128)(2,1)}, bf16[2,1024,768]{2,1,0:T(8,128)(2,1)}) custom-call(s32[2]{0:T(128)} %len_ref.7, bf16[2,288,768]{2,1,0:T(8,128)(2,1)} %bitcast.95, ...), custom_call_target="tpu_custom_call", output_to_operand_aliasing={{0}: (5, {}), {1}: (6, {}), {2}: (7, {}), {3}: (8, {})} | custom-call | flops 415236096 | bytes 811008 | tf_op jit(solution)/shard_map/cross_forward/pallas_call | solution.py:213
  187.5 3.9 convolution_add_fusion.second_ref
  191.3 19.1 %all-gather.5.cloned.1.call-done.down_ref.gate_low_ref.gate_high_ref.up_low_ref.up_high_ref = bf16[768,6400]{1,0:T(8,128)(2,1)} async-done(((bf16[24,6400]{1,0:T(8,128)(2,1)}), bf16[768,6400]{1,0:T(8,128)(2,1)}) %all-gather.5.cloned.1.call-update) | async-done | bytes 9830416 | tf_op jit(solution)/shard_map/all_gather | solution.py:888
  210.4 26.5 %feed_forward.1 = (bf16[576,768]{1,0:T(8,128)(2,1)}, f32[576,768]{1,0:T(8,128)}, f32[1,768]{1,0:T(1,128)}, bf16[768,6400]{1,0:T(8,128)(2,1)}) custom-call(f32[576,768]{1,0:T(8,128)} %convolution_add_fusion.second_ref, f32[1,768]{1,0:T(1,128)} %get-tuple-element.213.gain_ref, f32[576,1]{1,0:T(8,128)} %reshape.415.live_ref, bf16[576,768]{1,0:T(8,128)(2,1)} %bitcast.131, ...), custom_call_target="tpu_custom_call" | custom-call | flops 2038431744 | bytes 3342336 | tf_op jit(solution)/shard_map/feed_forward/pallas_call | solution.py:473
  240.9 19.5 %cross_backward.2 = (bf16[2,288,768]{2,1,0:T(8,128)(2,1)}, bf16[8,2,128,768]{3,2,1,0:T(8,128)(2,1)}, bf16[1024,1536]{1,0:T(8,128)(2,1)}) custom-call(s32[2]{0:T(128)} %len_ref.7, bf16[2,288,768]{2,1,0:T(8,128)(2,1)} %bitcast.96, bf16[2,1024,768]{2,1,0:T(8,128)(2,1)} %get-tuple-element.111.k_ref, bf16[2,1024,768]{2,1,0:T(8,128)(2,1)} %get-tuple-element.112.v_ref, ...), custom_call_target="tpu_custom_call" | custom-call | flops 887095296 | bytes 1062912 | tf_op jit(solution)/shard_map/cross_backward/pallas_call | solution.py:313
  260.3 24.8 %cross_backward.3 = (bf16[2,288,768]{2,1,0:T(8,128)(2,1)}, bf16[8,2,128,768]{3,2,1,0:T(8,128)(2,1)}, bf16[768,768]{1,0:T(8,128)(2,1)}, bf16[768,768]{1,0:T(8,128)(2,1)}) custom-call(s32[2]{0:T(128)} %len_ref.7, bf16[2,288,768]{2,1,0:T(8,128)(2,1)} %bitcast.97, ...), custom_call_target="tpu_custom_call", output_to_operand_aliasing={{0}: (10, {}), {1}: (11, {})} | custom-call | flops 887095296 | bytes 1062912 | tf_op jit(solution)/shard_map/cross_backward/pallas_call | solution.py:313
  296.1 4.9 %message.6 = bf16[2,192,3840]{2,1,0:T(8,128)(2,1)} custom-call(s32[3]{0:T(128)} %pad_add_fusion.sides_ref, bf16[2,2,192,768]{3,2,1,0:T(8,128)(2,1)} %bitcast.111, bf16[2,2,192,768]{3,2,1,0:T(8,128)(2,1)} %bitcast.99, bf16[2,2,192,768]{3,2,1,0:T(8,128)(2,1)} %bitcast.102, bf16[2,2,192,768]{3,2,1,0:T(8,128)(2,1)} %bitcast.105, bf16[2,2,192,768]{3,2,1,0:T(8,128)(2,1)} %bitcast.108), custom_call_target="tpu_custom_call" | custom-call | flops 184320 | bytes 737280 | tf_op jit(solution)/shard_map/message/pallas_call | solution.py:707
  301.2 4.4 all-to-all-start.1
  305.6 3.7 convolution_convert_fusion.4
  313.9 17.7 %self_backward.1 = (bf16[2,288,2304]{2,1,0:T(8,128)(2,1)}, f32[6,2,8,384]{3,2,1,0:T(8,128)}) custom-call(bf16[2,288,2304]{2,1,0:T(8,128)(2,1)} %bitcast.72, bf16[2,288,2304]{2,1,0:T(8,128)(2,1)} %bitcast.73, bf16[2,288,2304]{2,1,0:T(8,128)(2,1)} %bitcast.74, bf16[12,288,288]{2,1,0:T(8,128)(2,1)} %fusion.6.bias_ref, ...), custom_call_target="tpu_custom_call" | custom-call | flops 159252480 | bytes 995328 | tf_op jit(solution)/shard_map/self_backward/pallas_call | solution.py:160
  331.7 6.9 %bitcast_convert_fusion = bf16[768,2304]{1,0:T(8,128)(2,1)} fusion(bf16[2,288,2304]{2,1,0:T(8,128)(2,1)} %get-tuple-element.121, f32[768]{0:T(1024)S(1)} %get-tuple-element.201, f32[2,288]{1,0:T(2,128)S(1)} %get-tuple-element.214, bf16[2,288,768]{2,1,0:T(8,128)(2,1)} %param.21), kind=kOutput, calls=%fused_computation.2 | convolution fusion | flops 2041970688 | bytes 7083264 | tf_op jit(solution)/shard_map/dot_general | solution.py:38
  338.5 4.5 message.8
  343.0 11.5 %collective-permute-done.10.refs_6_ = bf16[1,192,3840]{2,1,0:T(8,128)(2,1)} collective-permute-done((bf16[1,192,3840]{2,1,0:T(8,128)(2,1)}, bf16[1,192,3840]{2,1,0:T(8,128)(2,1)}, u32[]{:S(2)}, u32[]{:S(2)}) %collective-permute-start.10) | collective-permute-done | bytes 1474592 | tf_op jit(solution)/shard_map/ppermute | solution.py:528
  354.6 4.4 message.9
  365.3 5.9 %multiply_reduce_fusion.1 = (f32[768]{0:T(1024)S(1)}, f32[576]{0:T(1024)S(1)}, f32[576,768]{1,0:T(8,128)S(1)}) fusion(f32[576]{0:T(1024)S(1)} %rsqrt.25, bf16[2,288,768]{2,1,0:T(8,128)(2,1)} %param.21, f32[768]{0:T(1024)S(1)} %get-tuple-element.201, bf16[576,2304]{1,0:T(8,128)(2,1)} %bitcast.140, bf16[768,3200]{1,0:T(8,128)(2,1)} %all-gather.3.cloned.1.call-done, ...), kind=kOutput, calls=%fused_computation.16 | convolution fusion | flops 2041969408 | bytes 9742848 | tf_op jit(solution)/shard_map/dot_general | solution.py:38
  375.9 15.9 %collective-permute-done.15 = f32[24,128]{1,0:T(8,128)S(1)} collective-permute-done((f32[24,128]{1,0:T(8,128)S(1)}, f32[24,128]{1,0:T(8,128)S(1)}, u32[]{:S(2)}, u32[]{:S(2)}) %collective-permute-start.15) | collective-permute-done | bytes 12320 | tf_op jit(solution)/shard_map/ppermute | solution.py:528
  403.5 9.2 %collective-permute-done.16.refs_1_ = bf16[4,24,2304]{2,1,0:T(8,128)(2,1)} collective-permute-done((bf16[4,24,2304]{2,1,0:T(8,128)(2,1)}, bf16[4,24,2304]{2,1,0:T(8,128)(2,1)}, u32[]{:S(2)}, u32[]{:S(2)}) %collective-permute-start.16) | collective-permute-done | bytes 442400 | tf_op jit(solution)/shard_map/ppermute | solution.py:528
  418.8 5.9 %collective-permute-start.20 = (bf16[1,24,3840]{2,1,0:T(8,128)(2,1)}, bf16[1,24,3840]{2,1,0:T(8,128)(2,1)S(1)}, u32[]{:S(2)}, u32[]{:S(2)}) collective-permute-start(bf16[1,24,3840]{2,1,0:T(8,128)(2,1)} %get-tuple-element.152), channel_id=1, source_target_pairs={{0,4},{1,5},{2,6},{3,7},{4,0},{5,1},{6,2},{7,3},{8,12},{9,13},{10,... | collective-permute-start | bytes 552968 | tf_op jit(solution)/shard_map/ppermute | solution.py:528
  424.6 3.7 collective-permute-done.21
  (154 shorter events, 117.7 us)
Async XLA Ops:
  7.2 105.3 %all-gather.3.cloned.1.call-start = ((), (), s32[]{:S(2)}) async-start(), calls=%async_computation.3 | async-start | bytes 5068800 | tf_op jit(solution)/shard_map/all_gather | solution.py:887
  10.7 199.7 %all-gather.5.cloned.1.call-start = ((), (), s32[]{:S(2)}) async-start(), calls=%async_computation.4 | async-start | bytes 10137600 | tf_op jit(solution)/shard_map/all_gather | solution.py:888
  11.5 10.2 %collective-permute-start.2 = (bf16[24,3072]{1,0:T(8,128)(2,1)}, bf16[24,3072]{1,0:T(8,128)(2,1)}, u32[]{:S(2)}, u32[]{:S(2)}) collective-permute-start(bf16[24,3072]{1,0:T(8,128)(2,1)} %get-tuple-element.90.refs_0_), channel_id=1, source_target_pairs={{0,6},{1,7},{2,4},{3,5},{4,2},{5,3},{6,0},{7,1},{8,14},{9,15},{10,... | collective-permute-start | bytes 442376 | tf_op jit(solution)/shard_map/ppermute | solution.py:528
  16.6 14.4 %collective-permute-start.1 = (bf16[24,3072]{1,0:T(8,128)(2,1)}, bf16[24,3072]{1,0:T(8,128)(2,1)}, u32[]{:S(2)}, u32[]{:S(2)}) collective-permute-start(bf16[24,3072]{1,0:T(8,128)(2,1)} %get-tuple-element.90.refs_0_), channel_id=1, source_target_pairs={{0,4},{1,5},{2,6},{3,7},{4,0},{5,1},{6,2},{7,3},{8,12},{9,13},{10,... | collective-permute-start | bytes 442376 | tf_op jit(solution)/shard_map/ppermute | solution.py:528
  16.6 14.4 %collective-permute-start = (bf16[24,3072]{1,0:T(8,128)(2,1)}, bf16[24,3072]{1,0:T(8,128)(2,1)}, u32[]{:S(2)}, u32[]{:S(2)}) collective-permute-start(bf16[24,3072]{1,0:T(8,128)(2,1)} %get-tuple-element.90.refs_0_), channel_id=1, source_target_pairs={{0,2},{1,3},{2,0},{3,1},{4,6},{5,7},{6,4},{7,5},{8,10},{9,11},{10,... | collective-permute-start | bytes 442376 | tf_op jit(solution)/shard_map/ppermute | solution.py:528
  33.0 7.9 %collective-permute-start.4 = (bf16[1,96,1536]{2,1,0:T(8,128)(2,1)}, bf16[1,96,1536]{2,1,0:T(8,128)(2,1)}, u32[]{:S(2)}, u32[]{:S(2)}) collective-permute-start(bf16[1,96,1536]{2,1,0:T(8,128)(2,1)} %bitcast.134), channel_id=1, source_target_pairs={{0,16},{1,17},{2,18},{3,19},{4,20},{5,21},{6,22},{7,23},{8,24},{9,... | collective-permute-start | bytes 884744 | tf_op jit(solution)/shard_map/ppermute | solution.py:528
  34.6 8.6 %collective-permute-start.3 = (bf16[4,24,1536]{2,1,0:T(8,128)(2,1)}, bf16[4,24,1536]{2,1,0:T(8,128)(2,1)}, u32[]{:S(2)}, u32[]{:S(2)}) collective-permute-start(bf16[4,24,1536]{2,1,0:T(8,128)(2,1)} %get-tuple-element.91.mine_ref), channel_id=1, source_target_pairs={{0,1},{1,0},{2,3},{3,2},{4,5},{5,4},{6,7},{7,6},{8,9},{9,8},{10,11... | collective-permute-start | bytes 884744 | tf_op jit(solution)/shard_map/ppermute | solution.py:528
  46.4 12.8 %collective-permute-start.5 = (bf16[1,192,1536]{2,1,0:T(8,128)(2,1)}, bf16[1,192,1536]{2,1,0:T(8,128)(2,1)S(1)}, u32[]{:S(2)}, u32[]{:S(2)}) collective-permute-start(bf16[1,192,1536]{2,1,0:T(8,128)(2,1)} %bitcast.127), channel_id=1, source_target_pairs={{0,16},{1,17},{2,18},{3,19},{4,20},{5,21},{6,22},{7,23},{8,24},{9,... | collective-permute-start | bytes 1769480 | tf_op jit(solution)/shard_map/ppermute | solution.py:528
  62.2 90.0 %all-to-all-start = ((bf16[16,128,768]{2,1,0:T(8,128)(2,1)}), bf16[16,128,768]{2,1,0:T(8,128)(2,1)S(1)}, u32[]{:S(2)}, u32[]{:S(2)}) async-start(bf16[16,128,768]{2,1,0:T(8,128)(2,1)} %param.22), calls=%async_computation | async-start | bytes 6291456 | tf_op jit(solution)/shard_map/all_to_all | solution.py:884
  67.7 375.6 %reduce-scatter.2.cloned.1.call-start = ((), (), s32[]{:S(2)}) async-start(), calls=%async_computation.5 | async-start | bytes 10137600 | tf_op jit(solution)/shard_map/reduce_scatter | solution.py:960
  70.2 37.0 %collective-permute-start.6 = (bf16[8,24,1536]{2,1,0:T(8,128)(2,1)}, bf16[8,24,1536]{2,1,0:T(8,128)(2,1)}, u32[]{:S(2)}, u32[]{:S(2)}) collective-permute-start(bf16[8,24,1536]{2,1,0:T(8,128)(2,1)} %bitcast.125), channel_id=1, source_target_pairs={{0,1},{1,0},{2,3},{3,2},{4,5},{5,4},{6,7},{7,6},{8,9},{9,8},{10,11... | collective-permute-start | bytes 1769480 | tf_op jit(solution)/shard_map/ppermute | solution.py:528
  112.5 28.2 %collective-permute-start.7 = (bf16[2,192,1536]{2,1,0:T(8,128)(2,1)}, bf16[2,192,1536]{2,1,0:T(8,128)(2,1)}, u32[]{:S(2)}, u32[]{:S(2)}) collective-permute-start(bf16[2,192,1536]{2,1,0:T(8,128)(2,1)} %bitcast.114), channel_id=1, source_target_pairs={{0,8},{1,9},{2,10},{3,11},{4,12},{5,13},{6,14},{7,15},{8,0},{9,1},... | collective-permute-start | bytes 3538952 | tf_op jit(solution)/shard_map/ppermute | solution.py:528
  112.5 32.1 %collective-permute-start.8 = (bf16[2,192,1536]{2,1,0:T(8,128)(2,1)}, bf16[2,192,1536]{2,1,0:T(8,128)(2,1)}, u32[]{:S(2)}, u32[]{:S(2)}) collective-permute-start(bf16[2,192,1536]{2,1,0:T(8,128)(2,1)} %bitcast.116), channel_id=1, source_target_pairs={{0,8},{1,9},{2,10},{3,11},{4,12},{5,13},{6,14},{7,15},{8,0},{9,1},... | collective-permute-start | bytes 3538952 | tf_op jit(solution)/shard_map/ppermute | solution.py:528
  170.6 16.9 %copy-start.3 = (bf16[2,2,192,1536]{3,2,1,0:T(8,128)(2,1)S(1)}, bf16[2,2,192,1536]{3,2,1,0:T(8,128)(2,1)}, u32[]{:S(2)}) copy-start(bf16[2,2,192,1536]{3,2,1,0:T(8,128)(2,1)} %merge_two.11) | copy-start | bytes 7077892
  260.3 24.8 %copy-start.4 = (bf16[2,2,192,1536]{3,2,1,0:T(8,128)(2,1)S(1)}, bf16[2,2,192,1536]{3,2,1,0:T(8,128)(2,1)}, u32[]{:S(2)}) copy-start(bf16[2,2,192,1536]{3,2,1,0:T(8,128)(2,1)} %merge_two.10) | copy-start | bytes 7077892
  301.0 8.3 %collective-permute-start.9 = (bf16[2,192,3840]{2,1,0:T(8,128)(2,1)}, bf16[2,192,3840]{2,1,0:T(8,128)(2,1)}, u32[]{:S(2)}, u32[]{:S(2)}) collective-permute-start(bf16[2,192,3840]{2,1,0:T(8,128)(2,1)} %message.6), channel_id=1, source_target_pairs={{0,8},{1,9},{2,10},{3,11},{4,12},{5,13},{6,14},{7,15},{8,0},{9,1},... | collective-permute-start | bytes 8847368 | tf_op jit(solution)/shard_map/ppermute | solution.py:528
  301.2 94.0 %all-to-all-start.1 = ((bf16[16,128,768]{2,1,0:T(8,128)(2,1)}), bf16[16,128,768]{2,1,0:T(8,128)(2,1)S(1)}, u32[]{:S(2)}, u32[]{:S(2)}) async-start(bf16[16,128,768]{2,1,0:T(8,128)(2,1)} %bitcast.98), calls=%async_computation.1 | async-start | bytes 6291456 | tf_op jit(solution)/shard_map/all_to_all | solution.py:884
  312.9 41.6 %collective-permute-start.10 = (bf16[1,192,3840]{2,1,0:T(8,128)(2,1)}, bf16[1,192,3840]{2,1,0:T(8,128)(2,1)}, u32[]{:S(2)}, u32[]{:S(2)}) collective-permute-start(bf16[1,192,3840]{2,1,0:T(8,128)(2,1)} %message.7), channel_id=1, source_target_pairs={{0,16},{1,17},{2,18},{3,19},{4,20},{5,21},{6,22},{7,23},{8,24},{9,... | collective-permute-start | bytes 4423688 | tf_op jit(solution)/shard_map/ppermute | solution.py:528
  354.5 7.6 %collective-permute-start.11 = (bf16[2,192,2304]{2,1,0:T(8,128)(2,1)}, bf16[2,192,2304]{2,1,0:T(8,128)(2,1)}, u32[]{:S(2)}, u32[]{:S(2)}) collective-permute-start(bf16[2,192,2304]{2,1,0:T(8,128)(2,1)} %message.8), channel_id=1, source_target_pairs={{0,8},{1,9},{2,10},{3,11},{4,12},{5,13},{6,14},{7,15},{8,0},{9,1},... | collective-permute-start | bytes 5308424 | tf_op jit(solution)/shard_map/ppermute | solution.py:528
  359.6 35.6 %collective-permute-start.13 = (bf16[4,24,3840]{2,1,0:T(8,128)(2,1)}, bf16[4,24,3840]{2,1,0:T(8,128)(2,1)}, u32[]{:S(2)}, u32[]{:S(2)}) collective-permute-start(bf16[4,24,3840]{2,1,0:T(8,128)(2,1)} %get-tuple-element.130), channel_id=1, source_target_pairs={{0,1},{1,0},{2,3},{3,2},{4,5},{5,4},{6,7},{7,6},{8,9},{9,8},{10,11... | collective-permute-start | bytes 2211848 | tf_op jit(solution)/shard_map/ppermute | solution.py:528
  365.1 30.1 %collective-permute-start.12 = (bf16[1,192,2304]{2,1,0:T(8,128)(2,1)}, bf16[1,192,2304]{2,1,0:T(8,128)(2,1)}, u32[]{:S(2)}, u32[]{:S(2)}) collective-permute-start(bf16[1,192,2304]{2,1,0:T(8,128)(2,1)} %message.10), channel_id=1, source_target_pairs={{0,16},{1,17},{2,18},{3,19},{4,20},{5,21},{6,22},{7,23},{8,24},{9,... | collective-permute-start | bytes 2654216 | tf_op jit(solution)/shard_map/ppermute | solution.py:528
  371.2 1.2 collective-permute-start.14
  372.4 19.3 %collective-permute-start.15 = (f32[24,128]{1,0:T(8,128)S(1)}, f32[24,128]{1,0:T(8,128)S(1)}, u32[]{:S(2)}, u32[]{:S(2)}) collective-permute-start(f32[24,128]{1,0:T(8,128)S(1)} %pad_add_fusion.1), channel_id=1, source_target_pairs={{0,16},{1,17},{2,18},{3,19},{4,20},{5,21},{6,22},{7,23},{8,24},{9,... | collective-permute-start | bytes 36872 | tf_op jit(solution)/shard_map/ppermute | solution.py:528
  398.6 14.1 %collective-permute-start.16 = (bf16[4,24,2304]{2,1,0:T(8,128)(2,1)}, bf16[4,24,2304]{2,1,0:T(8,128)(2,1)}, u32[]{:S(2)}, u32[]{:S(2)}) collective-permute-start(bf16[4,24,2304]{2,1,0:T(8,128)(2,1)} %get-tuple-element.140), channel_id=1, source_target_pairs={{0,1},{1,0},{2,3},{3,2},{4,5},{5,4},{6,7},{7,6},{8,9},{9,8},{10,11... | collective-permute-start | bytes 1327112 | tf_op jit(solution)/shard_map/ppermute | solution.py:528
  403.5 12.6 %collective-permute-start.19 = (bf16[2,24,3840]{2,1,0:T(8,128)(2,1)}, bf16[2,24,3840]{2,1,0:T(8,128)(2,1)S(1)}, u32[]{:S(2)}, u32[]{:S(2)}) collective-permute-start(bf16[2,24,3840]{2,1,0:T(8,128)(2,1)} %get-tuple-element.150), channel_id=1, source_target_pairs={{0,2},{1,3},{2,0},{3,1},{4,6},{5,7},{6,4},{7,5},{8,10},{9,11},{10,... | collective-permute-start | bytes 1105928 | tf_op jit(solution)/shard_map/ppermute | solution.py:528
  414.8 26.8 %collective-permute-start.17 = (bf16[2,24,2304]{2,1,0:T(8,128)(2,1)}, bf16[2,24,2304]{2,1,0:T(8,128)(2,1)}, u32[]{:S(2)}, u32[]{:S(2)}) collective-permute-start(bf16[2,24,2304]{2,1,0:T(8,128)(2,1)} %get-tuple-element.142), channel_id=1, source_target_pairs={{0,2},{1,3},{2,0},{3,1},{4,6},{5,7},{6,4},{7,5},{8,10},{9,11},{10,... | collective-permute-start | bytes 663560 | tf_op jit(solution)/shard_map/ppermute | solution.py:528
  418.8 20.4 %collective-permute-start.20 = (bf16[1,24,3840]{2,1,0:T(8,128)(2,1)}, bf16[1,24,3840]{2,1,0:T(8,128)(2,1)S(1)}, u32[]{:S(2)}, u32[]{:S(2)}) collective-permute-start(bf16[1,24,3840]{2,1,0:T(8,128)(2,1)} %get-tuple-element.152), channel_id=1, source_target_pairs={{0,4},{1,5},{2,6},{3,7},{4,0},{5,1},{6,2},{7,3},{8,12},{9,13},{10,... | collective-permute-start | bytes 552968 | tf_op jit(solution)/shard_map/ppermute | solution.py:528
  424.6 3.7 collective-permute-start.21
  428.3 4.8 %collective-permute-start.22 = (f32[24,128]{1,0:T(8,128)S(1)}, f32[24,128]{1,0:T(8,128)S(1)}, u32[]{:S(2)}, u32[]{:S(2)}) collective-permute-start(f32[24,128]{1,0:T(8,128)S(1)} %add.316), channel_id=1, source_target_pairs={{0,2},{1,3},{2,0},{3,1},{4,6},{5,7},{6,4},{7,5},{8,10},{9,11},{10,... | collective-permute-start | bytes 36872 | tf_op jit(solution)/shard_map/ppermute | solution.py:528
  433.1 4.6 collective-permute-start.23
  433.1 22.6 %copy-start.1 = (bf16[32,12]{0,1:T(8,128)(2,1)S(1)}, bf16[32,12]{0,1:T(8,128)(2,1)}, u32[]{:S(2)}) copy-start(bf16[32,12]{0,1:T(8,128)(2,1)} %param.40) | copy-start | bytes 2308
  445.9 5.9 %collective-permute-start.18 = (bf16[1,24,2304]{2,1,0:T(8,128)(2,1)}, bf16[1,24,2304]{2,1,0:T(8,128)(2,1)S(1)}, u32[]{:S(2)}, u32[]{:S(2)}) collective-permute-start(bf16[1,24,2304]{2,1,0:T(8,128)(2,1)} %get-tuple-element.146), channel_id=1, source_target_pairs={{0,4},{1,5},{2,6},{3,7},{4,0},{5,1},{6,2},{7,3},{8,12},{9,13},{10,... | collective-permute-start | bytes 331784 | tf_op jit(solution)/shard_map/ppermute | solution.py:528
  (18 other events, 77.9 us)
Sparse Core Ops, SparseCore 0:
  11.5 85.7 all-gather.2
  100.1 110.2 all-gather.4
  237.1 189.9 reduce-scatter.1
